TPU v7x, 256 devices: a whole 4x4x8 slice. The times are simulated.
256 devices in a mesh: wide: 128 (over z, x, y), narrow: 2 (over core).
Axes of the slice: x: 4, y: 4, z: 8, core: 2. Of those that a mesh axis runs over, the one named last changes fastest.
Arguments:
- point_feats: bfloat16 [65536, 512], P(('wide', 'narrow')), may hold values from -24 to 24
- region_ids: int32 [16384], P(('wide', 'narrow')), may hold values from 0 to 63, as said below
- w_qkv: bfloat16 [512, 1536], replicated, may hold values from -0.25 to 0.25
- w_out: bfloat16 [512, 512], replicated, may hold values from -0.25 to 0.25
- w_expert_in: bfloat16 [512, 131072], P(None, 'wide'), may hold values from -0.25 to 0.25
- b_expert_in: float32 [131072], P('wide'), may hold values from -4 to 4
- w_expert_out: bfloat16 [131072, 512], P('wide'), may hold values from -0.125 to 0.125
- out_cotangent: bfloat16 [65536, 512], P(('wide', 'narrow')), may hold values from -18 to 18
Outputs:
- layer_out: bfloat16 [65536, 512], P(('wide', 'narrow'))
- grad_feats: bfloat16 [65536, 512], P(('wide', 'narrow'))
- grad_attention: float32 [512, 2048], P(('wide', 'narrow'))
- grad_expert_in: float32 [512, 131072], P('narrow', 'wide')
- grad_expert_out: float32 [131072, 512], P('wide', 'narrow')
- grad_expert_bias: float32 [131072], P(('wide', 'narrow'))
Inputs may be any that keep to these rules, and one draw needn't show every extreme that they name: `region_ids`: the 64 blocks of one device name any one region at most 2 times, and one region is named exactly 2 times by the blocks of every device.
All inputs are finite; a program needn't handle non-finite values.
Results may differ from a plain program's by a relative error of at most 0.0095.
Values may be sent and summed in bfloat16 or wider, within the bound.
No kernel may reach another device: no remote copies, remote signals or barrier semaphores. Data moves between devices by JAX's collectives and lax.ppermute only.
A program may use at most 128 MiB of HBM per device.

v0:
```python
import jax
import jax.numpy as jnp
from jax import lax
from jax.experimental import pallas as pl
from jax.experimental.pallas import tpu as pltpu
from jax.sharding import PartitionSpec as P

F32 = jnp.float32
BF = jnp.bfloat16
EPS = 1e-05
GS = 0.7978845608
GC = 0.044715
W = 512
PTS = 256
NB = 64
CHIPS = 128
TOTAL = 65536.0
SHARE = 64.0 / 65536.0
HALF = 1024
VM = pl.BlockSpec(memory_space=pltpu.VMEM)
SM = pl.BlockSpec(memory_space=pltpu.SMEM)


def mm(a, b):
    return jnp.dot(a, b, preferred_element_type=F32)


def mm_t(a, b):
    return lax.dot_general(a, b, (((1,), (1,)), ((), ())), preferred_element_type=F32)


def t_mm(a, b):
    return lax.dot_general(a, b, (((0,), (0,)), ((), ())), preferred_element_type=F32)


def head_ones():
    r = lax.broadcasted_iota(jnp.int32, (W, W), 0) // 64
    c = lax.broadcasted_iota(jnp.int32, (W, W), 1) // 64
    return jnp.where(r == c, 1.0 / 64.0, 0.0).astype(BF)


def head_mean(v, ones):
    hi = v.astype(BF)
    lo = (v - hi.astype(F32)).astype(BF)
    return mm(hi, ones) + mm(lo, ones)


def normalize(raw, ones):
    cen = raw.astype(F32) - mm(raw, ones)
    scale = jnp.sqrt(head_mean(cen * cen, ones) + EPS)
    return cen / scale, scale


def low_rows(shape):
    return lax.broadcasted_iota(jnp.int32, shape, 0) < 4


def call(body, outs, scratch=(), smem_in=(), n_in=0, smem_out=(), cost=None, specs=None):
    return pl.pallas_call(
        body,
        out_shape=outs,
        grid=(1,) if specs else (),
        in_specs=[(specs or {}).get(i, SM if i in smem_in else VM) for i in range(n_in)],
        out_specs=[SM if i in smem_out else VM for i in range(len(outs))],
        scratch_shapes=list(scratch),
        cost_estimate=cost,
        compiler_params=pltpu.CompilerParams(vmem_limit_bytes=56 * 1024 * 1024),
    )


def cost(us):
    return pl.CostEstimate(flops=int(us * 1e9), bytes_accessed=int(us * 1e6), transcendentals=0)


def sds(shape, dtype):
    return jax.ShapeDtypeStruct(shape, dtype)


def front_kernel(ids, x_ref, c_ref, wq_ref, wo_ref, send, slots, qkv_ref, g_ref, cnt, ss):
    @pl.loop(0, NB)
    def _(i):
        cnt[i] = 0

    @pl.loop(0, NB)
    def _(b):
        r = ids[b]
        k = cnt[r]
        cnt[r] = k + 1
        slots[b] = 2 * r + k

    send[:, :, 0:W] = jnp.zeros((CHIPS, 8, W), BF)
    low = low_rows((8, W))

    @pl.loop(0, 16)
    def _(i):
        x = x_ref[pl.ds(pl.multiple_of(i * 16, 16), 16), :].astype(F32)
        c = c_ref[pl.ds(pl.multiple_of(i * 16, 16), 16), :].astype(F32)
        for h in range(2):
            xa, ca = x[8 * h : 8 * h + 8], c[8 * h : 8 * h + 8]
            xr, cr = pltpu.roll(xa, 4, 0), pltpu.roll(ca, 4, 0)
            send[slots[4 * i + 2 * h], :, 0:W] = jnp.where(low, xa, cr).astype(BF)
            send[slots[4 * i + 2 * h + 1], :, 0:W] = jnp.where(low, xr, ca).astype(BF)

    ones = head_ones()
    qkv = mm(x_ref[...], wq_ref[...]).astype(BF)
    qkv_ref[...] = qkv
    g = mm_t(c_ref[...], wo_ref[...]).astype(BF)
    g_ref[...] = g
    kn = normalize(qkv[:, W : 2 * W], ones)[0].astype(BF)
    vn = normalize(qkv[:, 2 * W :], ones)[0].astype(BF)
    left = lax.broadcasted_iota(jnp.int32, (64, 128), 1) < 64
    for j in range(4):
        s = slice(128 * j, 128 * j + 128)
        a = t_mm(kn[:, s], vn[:, s])
        ss[64 * j : 64 * j + 64, :] = jnp.where(left, a[:64], a[64:])
        a = t_mm(qkv[:, s], g[:, s])
        ss[256 + 64 * j : 320 + 64 * j, :] = jnp.where(left, a[:64], a[64:])
    low2 = low_rows((8, 128))

    @pl.loop(0, 64)
    def _(i):
        v = ss[pl.ds(pl.multiple_of(i * 8, 8), 8), :]
        hi = v.astype(BF).astype(F32)
        lo = v - hi
        send[2 * i, :, W:] = jnp.where(low2, hi, pltpu.roll(lo, 4, 0)).astype(BF)
        send[2 * i + 1, :, W:] = jnp.where(low2, pltpu.roll(hi, 4, 0), lo).astype(BF)


def query_kernel(pos, x_ref, g_ref, keep, send):
    x, g = x_ref[...], g_ref[...]
    for core, dst in ((pos[3], keep), (1 - pos[3], send)):
        xk = mm(x, pick(core)).astype(BF)
        dst[...] = (t_mm(xk, g) * (1.0 / TOTAL)).astype(dst.dtype)


def pick(core):
    r = lax.broadcasted_iota(jnp.int32, (W, PTS), 0)
    k = lax.broadcasted_iota(jnp.int32, (W, PTS), 1)
    return jnp.where(r == 4 * (k % CHIPS) + 2 * core + k // CHIPS, 1.0, 0.0).astype(BF)


def chunk_kernel(recv, out):
    v = jnp.sum(recv[...].astype(F32), axis=0)
    out[...] = v + pltpu.roll(v, 4, 0)


def spread_kernel(a_ref, b_ref, keep, near, out, rows):
    v = ((a_ref[...] + b_ref[...]) * (1.0 / TOTAL)).astype(BF)
    out[:, :, 0:128] = jnp.broadcast_to(v[None], (CHIPS, 8, 128))
    tot = keep[...] + near[...].astype(F32)
    for j in range(2):
        for q in range(4):
            rows[pl.ds(4 * j + q, CHIPS, stride=8), :] = tot[CHIPS * j : CHIPS * j + CHIPS, 128 * q : 128 * q + 128]
    out[:, :, 128:256] = rows[...].reshape(CHIPS, 8, 128).astype(BF)


def expert_kernel(
    pos, recv, wi, wiy, win, wo, woy, won, b_ref, bp_ref, send, x_s, c_s, hid, gpre, o_s, k_s
):
    n = pos[3]
    mine = pl.ds(pl.multiple_of(n * 256, 256), 256)
    other = pl.ds(pl.multiple_of(256 - n * 256, 256), 256)
    low = low_rows((8, W))

    @pl.loop(0, 32)
    def _(i):
        xs, cs = [], []
        for h in range(2):
            a = recv[4 * i + 2 * h].astype(F32)
            b = recv[4 * i + 2 * h + 1].astype(F32)
            xs.append(jnp.where(low, a, pltpu.roll(b, 4, 0)))
            cs.append(jnp.where(low, pltpu.roll(a, 4, 0), b))
        rows = pl.ds(pl.multiple_of(i * 16, 16), 16)
        x_s[rows, :] = jnp.concatenate(xs, axis=0).astype(BF)
        c_s[rows, :] = jnp.concatenate(cs, axis=0).astype(BF)

    def act(pre, gh, cols):
        sq = pre * pre
        t = jnp.tanh(GS * (pre + GC * pre * sq))
        up = 0.5 * (1.0 + t)
        hid[:, cols] = (pre * up).astype(BF)
        slope = up + 0.5 * pre * (1.0 - t * t) * GS * (1.0 + 3.0 * GC * sq)
        gpre[:, cols] = (gh * slope).astype(BF)

    @pl.loop(0, 4)
    def _(i):
        cols = pl.ds(pl.multiple_of(i * 256, 256), 256)
        pre = mm(x_s[...], wi[:, cols]) + b_ref[:, cols]
        gh = mm_t(c_s[...], wo[cols, :])
        act(pre, gh, cols)

    @pl.loop(0, 4)
    def _(i):
        cols = pl.ds(pl.multiple_of(i * 256, 256), 256)
        pre = mm(x_s[:, mine], wiy[:, cols]) + mm(x_s[:, other], win[:, cols]) + bp_ref[:, cols]
        gh = mm_t(c_s[:, mine], woy[cols, :]) + mm_t(c_s[:, other], won[cols, :])
        act(pre, gh, pl.ds(pl.multiple_of(HALF + i * 256, 256), 256))

    for yr, kr, part in ((woy, wiy, mine), (won, win, other)):
        o_s[:, part] = mm(hid[:, :HALF], wo[:, part]) + mm(hid[:, HALF:], yr[...])
        k_s[:, part] = mm_t(gpre[:, :HALF], wi[part, :]) + mm_t(gpre[:, HALF:], kr[...])

    @pl.loop(0, 64)
    def _(i):
        rows = pl.ds(pl.multiple_of(i * 8, 8), 8)
        o, k = o_s[rows, :], k_s[rows, :]
        send[2 * i, :, :] = jnp.where(low, o, pltpu.roll(k, 4, 0)).astype(BF)
        send[2 * i + 1, :, :] = jnp.where(low, pltpu.roll(o, 4, 0), k).astype(BF)


def weight_in_kernel(pos, x_s, gpre, keep, send):
    n = pos[3]
    mine = pl.ds(pl.multiple_of(n * 256, 256), 256)
    other = pl.ds(pl.multiple_of(256 - n * 256, 256), 256)

    @pl.loop(0, 4)
    def _(i):
        cols = pl.ds(pl.multiple_of(i * 512, 512), 512)
        g = gpre[:, cols]
        keep[0:256, cols] = t_mm(x_s[:, mine], g) * SHARE
        send[0:256, cols] = (t_mm(x_s[:, other], g) * SHARE).astype(BF)
        bias = jnp.sum(g.astype(F32), axis=0, keepdims=True) * SHARE
        keep[256:272, cols] = jnp.broadcast_to(bias, (16, 512))
        send[256:272, cols] = jnp.broadcast_to(bias, (16, 512)).astype(BF)


def weight_out_kernel(pos, c_s, hid, keep, send):
    n = pos[3]
    mine = pl.ds(pl.multiple_of(n * 256, 256), 256)
    other = pl.ds(pl.multiple_of(256 - n * 256, 256), 256)

    @pl.loop(0, 4)
    def _(i):
        cols = pl.ds(pl.multiple_of(i * 512, 512), 512)
        h = hid[:, cols]
        keep[cols, :] = t_mm(h, c_s[:, mine]) * SHARE
        send[cols, :] = (t_mm(h, c_s[:, other]) * SHARE).astype(BF)


def merge_in_kernel(keep, recv, here, away):
    here[...] = keep[:, :HALF] + recv[:, :HALF].astype(F32)
    away[...] = (keep[:, HALF:] + recv[:, HALF:].astype(F32)).astype(BF)


def merge_out_kernel(keep, recv, here, away):
    here[...] = keep[:HALF, :] + recv[:HALF, :].astype(F32)
    away[...] = (keep[HALF:, :] + recv[HALF:, :].astype(F32)).astype(BF)


def end_in_kernel(pos, here, recv, out, bias, row):
    out[...] = here[:256, :] + recv[:256, :].astype(F32)
    row[...] = (here[256:272, :] + recv[256:272, :].astype(F32))[0:8, :]
    bias[...] = row[0:1, pl.ds(pl.multiple_of(pos[3] * 512, 512), 512)]


def end_out_kernel(here, recv, out):
    out[...] = here[...] + recv[...].astype(F32)


def attn_kernel(pos, rs, qkv_ref, g_ref, x_ref, c_ref, mix_ref, gq, keep, send, query, ss):
    low = low_rows((8, 128))

    @pl.loop(0, 32)
    def _(i):
        t = [
            jnp.where(low, rs[4 * i + 2 * h, :, 0:128].astype(F32), rs[4 * i + 2 * h + 1, :, 0:128].astype(F32))
            for h in range(2)
        ]
        ss[pl.ds(pl.multiple_of(i * 16, 16), 16), :] = jnp.concatenate(t, axis=0).astype(BF)

    ones = head_ones()
    qkv, g = qkv_ref[...], g_ref[...]
    ku, ks = normalize(qkv[:, W : 2 * W], ones)
    vu, vs = normalize(qkv[:, 2 * W :], ones)
    kn, vn = ku.astype(BF), vu.astype(BF)
    left = lax.broadcasted_iota(jnp.int32, (64, 128), 1) < 64
    total = jnp.sum(rs[:, :, 128:256].astype(F32), axis=0)
    total_hi = total.astype(BF)
    total_lo = (total - total_hi.astype(F32)).astype(BF)
    block = lax.broadcasted_iota(jnp.int32, (8, 128), 0) % 4

    def diag(p):
        z = jnp.zeros_like(p)
        return jnp.concatenate([jnp.where(left, p, z), jnp.where(left, z, p)], axis=0)

    gk, gv = [], []
    rows = jnp.zeros((8, 128), F32)
    for j in range(4):
        s = slice(128 * j, 128 * j + 128)
        sm = diag(ss[64 * j : 64 * j + 64, :].astype(F32)).astype(BF)
        gs = diag(ss[256 + 64 * j : 320 + 64 * j, :].astype(F32)).astype(BF)
        mix_ref[:, s] = mm(qkv[:, s], sm).astype(BF)
        gq[:, s] = mm_t(g[:, s], sm).astype(BF)
        rows = jnp.where(block == j, mm_t(total_hi, sm) + mm_t(total_lo, sm), rows)
        gk.append(mm_t(vn[:, s], gs))
        gv.append(mm(kn[:, s], gs))
    query[...] = rows

    def back(gr, u, sc):
        return ((gr - head_mean(gr, ones) - u * head_mean(gr * u, ones)) / sc).astype(BF)

    gq[:, W : 2 * W] = back(jnp.concatenate(gk, axis=1), ku, ks)
    gq[:, 2 * W :] = back(jnp.concatenate(gv, axis=1), vu, vs)
    x, c, mixed = x_ref[...], c_ref[...], mix_ref[...]
    for core, dst in ((pos[3], keep), (1 - pos[3], send)):
        sel = pick(core)
        xk, mk = mm(x, sel).astype(BF), mm(mixed, sel).astype(BF)
        for q in range(2):
            dst[:, W * q : W * q + W] = (t_mm(xk, gq[:, W * q + W : W * q + 2 * W]) * (1.0 / TOTAL)).astype(dst.dtype)
        dst[:, 2 * W :] = (t_mm(mk, c) * (1.0 / TOTAL)).astype(dst.dtype)


def base_kernel(x, c, mixed, gq, wq, wo, base_o, base_k):
    base_o[...] = x[...].astype(F32) + mm(mixed[...], wo[...])
    base_k[...] = c[...].astype(F32) + mm_t(gq[...], wq[...])


def join_kernel(ret, keep, near, out, rows):
    out[:, :, 0:W] = ret[...]
    size = 8 * CHIPS
    for t in range(3):
        for j in range(2):
            part = slice(CHIPS * j, CHIPS * j + CHIPS)
            for q in range(4):
                cols = slice(384 * q + 128 * t, 384 * q + 128 * t + 128)
                v = keep[part, cols] + near[part, cols].astype(F32)
                rows[pl.ds(size * t + 4 * j + q, CHIPS, stride=8), :] = v
        v = rows[size * t : size * t + size, :].reshape(CHIPS, 8, 128)
        out[:, :, W + 128 * t : W + 128 * t + 128] = v.astype(BF)


def final_kernel(slots, ret, base_o, base_k, query, lo, gf, att):
    low = low_rows((8, W))

    @pl.loop(0, 16)
    def _(i):
        os, ks = [], []
        for h in range(2):
            a = ret[slots[4 * i + 2 * h], :, 0:W].astype(F32)
            b = ret[slots[4 * i + 2 * h + 1], :, 0:W].astype(F32)
            os.append(jnp.where(low, a, pltpu.roll(b, 4, 0)))
            ks.append(jnp.where(low, pltpu.roll(a, 4, 0), b))
        rows = pl.ds(pl.multiple_of(i * 16, 16), 16)
        lo[rows, :] = (base_o[rows, :] + jnp.concatenate(os, axis=0)).astype(BF)
        gf[rows, :] = (base_k[rows, :] + jnp.concatenate(ks, axis=0)).astype(BF)

    v = jnp.sum(ret[:, :, W:].astype(F32), axis=0)
    q = query[...]
    for j in range(2):
        for b in range(4):
            r = slice(4 * j + b, 4 * j + b + 1)
            att[j : j + 1, 128 * b : 128 * b + 128] = q[r]
            att[j : j + 1, W + 384 * b : W + 384 * b + 384] = v[r]


def layer(x, ids, wq, wo_att, wi, bi, wo, c):
    n = lax.axis_index("narrow")
    w = lax.axis_index("wide")
    pos = jnp.stack([w // 16, w // 4 % 4, w % 4, n]).astype(jnp.int32)
    pair = [(i, i ^ 1) for i in range(CHIPS)]
    swap = [(0, 1), (1, 0)]

    def across(v):
        return lax.ppermute(v, "wide", pair)

    def beside(v):
        return lax.ppermute(v, "narrow", swap)

    def deal(v):
        return lax.all_to_all(v, "wide", split_axis=0, concat_axis=0, tiled=True)

    def run(body, us, outs, args, scratch=(), smem_in=(), smem_out=(), specs=None):
        return call(
            body, outs, scratch, smem_in=smem_in, n_in=len(args), smem_out=smem_out, cost=cost(us),
            specs=specs,
        )(*args)

    wiy = across(lax.dynamic_slice_in_dim(wi, n * 256, 256, 0))
    woy = across(lax.dynamic_slice_in_dim(wo, n * 256, 256, 1))
    bp = across(bi)
    win, won = beside(wiy), beside(woy)

    send, slots, qkv, g = run(
        front_kernel, 5,
        [sds((CHIPS, 8, 640), BF), sds((NB,), jnp.int32), sds((PTS, 3 * W), BF), sds((PTS, W), BF)],
        (ids, x, c, wq, wo_att), [pltpu.SMEM((NB,), jnp.int32), pltpu.VMEM((W, 128), F32)], (0,), (1,),
    )
    recv = deal(send)
    keep_q, away_q = run(query_kernel, 2, [sds((PTS, W), F32), sds((PTS, W), BF)], (pos, x, g), (), (0,))
    near_q = beside(away_q)
    (chunk,) = run(
        chunk_kernel, 1, [sds((8, 128), F32)], (recv,),
        specs={0: pl.BlockSpec((CHIPS, 8, 128), lambda i: (0, 0, 4))},
    )
    (spread,) = run(
        spread_kernel, 1, [sds((CHIPS, 8, 256), BF)], (chunk, beside(chunk), keep_q, near_q),
        [pltpu.VMEM((8 * CHIPS, 128), F32)],
    )
    rs = deal(spread)
    ret, x_s, c_s, hid, gpre = run(
        expert_kernel, 12,
        [sds((CHIPS, 8, W), BF), sds((W, W), BF), sds((W, W), BF), sds((W, 2 * HALF), BF), sds((W, 2 * HALF), BF)],
        (pos, recv, wi, wiy, win, wo, woy, won, bi.reshape(1, HALF), bp.reshape(1, HALF)),
        [pltpu.VMEM((W, W), F32), pltpu.VMEM((W, W), F32)], (0,),
        specs={1: pl.BlockSpec((CHIPS, 8, W), lambda i: (0, 0, 0))},
    )
    mixed, gq, keep, away, query = run(
        attn_kernel, 7,
        [sds((PTS, W), BF), sds((PTS, 3 * W), BF), sds((PTS, 3 * W), F32), sds((PTS, 3 * W), BF), sds((8, 128), F32)],
        (pos, rs, qkv, g, x, c), [pltpu.VMEM((W, 128), BF)], (0,),
    )
    near = beside(away)
    base_o, base_k = run(base_kernel, 2, [sds((PTS, W), F32), sds((PTS, W), F32)], (x, c, mixed, gq, wq, wo_att))
    (joined,) = run(join_kernel, 2, [sds((CHIPS, 8, 896), BF)], (ret, keep, near), [pltpu.VMEM((24 * CHIPS, 128), F32)])
    back = deal(joined)
    keep_i, send_i = run(
        weight_in_kernel, 4, [sds((272, 2 * HALF), F32), sds((272, 2 * HALF), BF)], (pos, x_s, gpre), (), (0,)
    )
    got_i = beside(send_i)
    keep_o, send_o = run(
        weight_out_kernel, 4, [sds((2 * HALF, 256), F32), sds((2 * HALF, 256), BF)], (pos, c_s, hid), (), (0,)
    )
    got_o = beside(send_o)
    here_i, away_i = run(merge_in_kernel, 1, [sds((272, HALF), F32), sds((272, HALF), BF)], (keep_i, got_i))
    far_i = across(away_i)
    here_o, away_o = run(merge_out_kernel, 1, [sds((HALF, 256), F32), sds((HALF, 256), BF)], (keep_o, got_o))
    far_o = across(away_o)
    grad_in, grad_b = run(
        end_in_kernel, 1, [sds((256, HALF), F32), sds((1, 512), F32)],
        (pos, here_i, far_i), [pltpu.VMEM((8, HALF), F32)], (0,),
    )
    (grad_out,) = run(end_out_kernel, 1, [sds((HALF, 256), F32)], (here_o, far_o))
    layer_out, grad_feats, att = run(
        final_kernel, 3, [sds((PTS, W), BF), sds((PTS, W), BF), sds((2, 4 * W), F32)],
        (slots, back, base_o, base_k, query), (), (0,),
    )
    return (layer_out, grad_feats, att, grad_in, grad_out, grad_b.reshape(512))


def solution(mesh):
    placed = (
        P(("wide", "narrow"), None),
        P(("wide", "narrow")),
        P(),
        P(),
        P(None, "wide"),
        P("wide"),
        P("wide", None),
        P(("wide", "narrow"), None),
    )
    return jax.shard_map(
        layer,
        mesh=mesh,
        in_specs=placed,
        out_specs=(
            P(("wide", "narrow"), None),
            P(("wide", "narrow"), None),
            P(("wide", "narrow"), None),
            P("narrow", "wide"),
            P("wide", "narrow"),
            P(("wide", "narrow")),
        ),
        check_vma=False,
    )
```

profile of v0, /device:TPU:1, one launch (start us, length us, event | category | flops | bytes accessed | tf_op | source)
XLA Modules:
  0.0 204.6 jit_solution(6566005754464836456)
XLA Ops:
  0.6 7.3 %shard_map.127 = (bf16[128,8,640]{2,1,0:T(8,128)(2,1)}, s32[64]{0:T(128)}, bf16[256,1536]{1,0:T(8,128)(2,1)}, bf16[256,512]{1,0:T(8,128)(2,1)}) custom-call(s32[64]{0:T(128)} %ids.1, bf16[256,512]{1,0:T(8,128)(2,1)} %x.1, bf16[256,512]{1,0:T(8,128)(2,1)} %c.1, bf16[512,1536]{1,0:T(8,128)(2,1)} %wq.1, bf16[512,512]{1,0:T(8,128)(2,1)} %wo.3), custom_call_target="tpu_custom_call" | custom-call | flops 5000000000 | bytes 5000000 | tf_op jit(solution)/shard_map/pallas_call | solution.py:373
  8.0 16.3 %all-to-all-start = ((bf16[128,8,640]{2,1,0:T(8,128)(2,1)}), bf16[128,8,640]{2,1,0:T(8,128)(2,1)S(1)}, u32[]{:S(2)}, u32[]{:S(2)}) async-start(bf16[128,8,640]{2,1,0:T(8,128)(2,1)} %get-tuple-element.38), calls=%async_computation | async-start | bytes 2621440 | tf_op jit(solution)/shard_map/all_to_all | solution.py:370
  25.0 2.5 %shard_map.130 = (f32[256,512]{1,0:T(8,128)}, bf16[256,512]{1,0:T(8,128)(2,1)}) custom-call(s32[4]{0:T(128)} %pad_add_fusion.pos, bf16[256,512]{1,0:T(8,128)(2,1)} %x.1, bf16[256,512]{1,0:T(8,128)(2,1)} %get-tuple-element.40.g_ref), custom_call_target="tpu_custom_call" | custom-call | flops 2000000000 | bytes 2000000 | tf_op jit(solution)/shard_map/pallas_call | solution.py:373
  28.5 30.0 %all-to-all-done.recv = bf16[128,8,640]{2,1,0:T(8,128)(2,1)S(1)} async-done(((bf16[128,8,640]{2,1,0:T(8,128)(2,1)}), bf16[128,8,640]{2,1,0:T(8,128)(2,1)S(1)}, u32[]{:S(2)}, u32[]{:S(2)}) %all-to-all-start) | async-done | bytes 1310752 | tf_op jit(solution)/shard_map/all_to_all | solution.py:370
  61.2 3.4 %collective-permute-start.5 = (f32[8,128]{1,0:T(8,128)}, f32[8,128]{1,0:T(8,128)S(1)}, u32[]{:S(2)}, u32[]{:S(2)}) collective-permute-start(f32[8,128]{1,0:T(8,128)} %shard_map.129.a_ref), channel_id=1, source_target_pairs={{0,1},{1,0},{2,3},{3,2},{4,5},{5,4},{6,7},{7,6},{8,9},{9,8},{10,11... | collective-permute-start | bytes 12296 | tf_op jit(solution)/shard_map/ppermute | solution.py:367
  66.2 2.2 %shard_map.131 = bf16[128,8,256]{2,1,0:T(8,128)(2,1)} custom-call(f32[8,128]{1,0:T(8,128)} %shard_map.129.a_ref, f32[8,128]{1,0:T(8,128)} %copy-done.17, f32[256,512]{1,0:T(8,128)} %get-tuple-element.41.keep, bf16[256,512]{1,0:T(8,128)(2,1)} %copy-done.14), custom_call_target="tpu_custom_call" | custom-call | flops 1000000000 | bytes 1000000 | tf_op jit(solution)/shard_map/pallas_call | solution.py:373
  68.4 6.3 %all-to-all-start.1 = ((bf16[128,8,256]{2,1,0:T(8,128)(2,1)}), bf16[128,8,256]{2,1,0:T(8,128)(2,1)S(1)}, u32[]{:S(2)}, u32[]{:S(2)}) async-start(bf16[128,8,256]{2,1,0:T(8,128)(2,1)} %shard_map.131), calls=%async_computation.1 | async-start | bytes 1048576 | tf_op jit(solution)/shard_map/all_to_all | solution.py:370
  77.0 16.4 %collective-permute-done.wiy = bf16[256,1024]{1,0:T(8,128)(2,1)S(1)} collective-permute-done((bf16[256,1024]{1,0:T(8,128)(2,1)S(1)}, bf16[256,1024]{1,0:T(8,128)(2,1)S(1)}, u32[]{:S(2)}, u32[]{:S(2)}) %collective-permute-start) | collective-permute-done | bytes 524320 | tf_op jit(solution)/shard_map/ppermute | solution.py:364
  93.4 1.9 collective-permute-start.1
  95.3 9.4 %collective-permute-done.2.woy = bf16[1024,256]{1,0:T(8,128)(2,1)S(1)} collective-permute-done((bf16[1024,256]{1,0:T(8,128)(2,1)S(1)}, bf16[1024,256]{1,0:T(8,128)(2,1)S(1)}, u32[]{:S(2)}, u32[]{:S(2)}) %collective-permute-start.2) | collective-permute-done | bytes 524320 | tf_op jit(solution)/shard_map/ppermute | solution.py:364
  106.7 6.7 %shard_map.132 = (bf16[256,512]{1,0:T(8,128)(2,1)}, bf16[256,1536]{1,0:T(8,128)(2,1)}, f32[256,1536]{1,0:T(8,128)}, bf16[256,1536]{1,0:T(8,128)(2,1)}, f32[8,128]{1,0:T(8,128)}) custom-call(s32[4]{0:T(128)} %pad_add_fusion.pos, bf16[128,8,256]{2,1,0:T(8,128)(2,1)} %copy-done.2, bf16[256,1536]{1,0:T(8,128)(2,1)} %get-tuple-element.43.qkv_ref, ...), custom_call_target="tpu_custom_call" | custom-call | flops 7000000000 | bytes 7000000 | tf_op jit(solution)/shard_map/pallas_call | solution.py:373
  114.5 13.9 %shard_map.128 = (bf16[128,8,512]{2,1,0:T(8,128)(2,1)}, bf16[512,512]{1,0:T(8,128)(2,1)}, bf16[512,512]{1,0:T(8,128)(2,1)}, bf16[512,2048]{1,0:T(8,128)(2,1)}, bf16[512,2048]{1,0:T(8,128)(2,1)}) custom-call(s32[4]{0:T(128)} %pad_add_fusion.pos, bf16[128,8,640]{2,1,0:T(8,128)(2,1)} %copy-done.1, bf16[512,1024]{1,0:T(8,128)(2,1)} %wi.1, ...), custom_call_target="tpu_custom_call" | custom-call | flops 12000000000 | bytes 12000000 | tf_op jit(solution)/shard_map/pallas_call | solution.py:373
  129.3 3.7 %shard_map.133 = bf16[128,8,896]{2,1,0:T(8,128)(2,1)} custom-call(bf16[128,8,512]{2,1,0:T(8,128)(2,1)} %get-tuple-element.39.ret, f32[256,1536]{1,0:T(8,128)} %get-tuple-element.44.keep, bf16[256,1536]{1,0:T(8,128)(2,1)} %copy-done.7), custom_call_target="tpu_custom_call" | custom-call | flops 2000000000 | bytes 2000000 | tf_op jit(solution)/shard_map/pallas_call | solution.py:373
  133.0 12.3 %all-to-all-start.2 = ((bf16[128,8,896]{2,1,0:T(8,128)(2,1)}), bf16[128,8,896]{2,1,0:T(8,128)(2,1)S(1)}, u32[]{:S(2)}, u32[]{:S(2)}) async-start(bf16[128,8,896]{2,1,0:T(8,128)(2,1)} %shard_map.133), calls=%async_computation.2 | async-start | bytes 3670016 | tf_op jit(solution)/shard_map/all_to_all | solution.py:370
  145.3 5.4 %shard_map.139 = (f32[2048,256]{1,0:T(8,128)}, bf16[2048,256]{1,0:T(8,128)(2,1)}) custom-call(s32[4]{0:T(128)} %pad_add_fusion.pos, bf16[512,512]{1,0:T(8,128)(2,1)} %get-tuple-element.61.c_s, bf16[512,2048]{1,0:T(8,128)(2,1)} %get-tuple-element.62.hid), custom_call_target="tpu_custom_call" | custom-call | flops 4000000000 | bytes 4000000 | tf_op jit(solution)/shard_map/pallas_call | solution.py:373
  151.4 5.4 %shard_map.136 = (f32[272,2048]{1,0:T(8,128)}, bf16[272,2048]{1,0:T(8,128)(2,1)}) custom-call(s32[4]{0:T(128)} %pad_add_fusion.pos, bf16[512,512]{1,0:T(8,128)(2,1)} %get-tuple-element.54.x_s, bf16[512,2048]{1,0:T(8,128)(2,1)} %get-tuple-element.55.gpre), custom_call_target="tpu_custom_call" | custom-call | flops 4000000000 | bytes 4000000 | tf_op jit(solution)/shard_map/pallas_call | solution.py:373
  157.8 3.1 %shard_map.140 = (f32[1024,256]{1,0:T(8,128)}, bf16[1024,256]{1,0:T(8,128)(2,1)}) custom-call(f32[2048,256]{1,0:T(8,128)} %get-tuple-element.63.keep, bf16[2048,256]{1,0:T(8,128)(2,1)} %copy-done.6), custom_call_target="tpu_custom_call" | custom-call | flops 1000000000 | bytes 1000000 | tf_op jit(solution)/shard_map/pallas_call | solution.py:373
  162.7 3.2 %shard_map.137 = (f32[272,1024]{1,0:T(8,128)}, bf16[272,1024]{1,0:T(8,128)(2,1)}) custom-call(f32[272,2048]{1,0:T(8,128)} %get-tuple-element.56.keep, bf16[272,2048]{1,0:T(8,128)(2,1)} %copy-done.5), custom_call_target="tpu_custom_call" | custom-call | flops 1000000000 | bytes 1000000 | tf_op jit(solution)/shard_map/pallas_call | solution.py:373
  166.5 3.5 %shard_map.134 = (f32[256,512]{1,0:T(8,128)}, f32[256,512]{1,0:T(8,128)}) custom-call(bf16[256,512]{1,0:T(8,128)(2,1)} %x.1, bf16[256,512]{1,0:T(8,128)(2,1)} %c.1, bf16[256,512]{1,0:T(8,128)(2,1)} %get-tuple-element.46.mixed, bf16[256,1536]{1,0:T(8,128)(2,1)} %get-tuple-element.47.gq, bf16[512,1536]{1,0:T(8,128)(2,1)} %wq.1, bf16[512,512]{1,0:T(8,128)(2,1)} %wo.3), custom_call_target="tpu_custom_call" | custom-call | flops 2000000000 | bytes 2000000 | tf_op jit(solution)/shard_map/pallas_call | solution.py:373
  170.0 12.1 %collective-permute-done.11.recv = bf16[1024,256]{1,0:T(8,128)(2,1)S(1)} collective-permute-done((bf16[1024,256]{1,0:T(8,128)(2,1)}, bf16[1024,256]{1,0:T(8,128)(2,1)S(1)}, u32[]{:S(2)}, u32[]{:S(2)}) %collective-permute-start.11) | collective-permute-done | bytes 524320 | tf_op jit(solution)/shard_map/ppermute | solution.py:364
  182.9 2.4 %shard_map.141 = f32[1024,256]{1,0:T(8,128)} custom-call(f32[1024,256]{1,0:T(8,128)} %get-tuple-element.65.here, bf16[1024,256]{1,0:T(8,128)(2,1)} %copy-done.13), custom_call_target="tpu_custom_call" | custom-call | flops 1000000000 | bytes 1000000 | tf_op jit(solution)/shard_map/pallas_call | solution.py:373
  185.3 11.8 %collective-permute-done.9.recv = bf16[272,1024]{1,0:T(8,128)(2,1)S(1)} collective-permute-done((bf16[272,1024]{1,0:T(8,128)(2,1)}, bf16[272,1024]{1,0:T(8,128)(2,1)S(1)}, u32[]{:S(2)}, u32[]{:S(2)}) %collective-permute-start.9) | collective-permute-done | bytes 557088 | tf_op jit(solution)/shard_map/ppermute | solution.py:364
  198.0 2.5 %shard_map.138 = (f32[256,1024]{1,0:T(8,128)}, f32[1,512]{1,0:T(1,128)}) custom-call(s32[4]{0:T(128)} %pad_add_fusion.pos, f32[272,1024]{1,0:T(8,128)} %get-tuple-element.58.here, bf16[272,1024]{1,0:T(8,128)(2,1)} %copy-done.8), custom_call_target="tpu_custom_call" | custom-call | flops 1000000000 | bytes 1000000 | tf_op jit(solution)/shard_map/pallas_call | solution.py:373
  201.7 2.8 %shard_map.135 = (bf16[256,512]{1,0:T(8,128)(2,1)}, bf16[256,512]{1,0:T(8,128)(2,1)}, f32[2,2048]{1,0:T(2,128)}) custom-call(s32[64]{0:T(128)} %get-tuple-element.37.slots, bf16[128,8,896]{2,1,0:T(8,128)(2,1)} %copy-done, f32[256,512]{1,0:T(8,128)} %get-tuple-element.48.base_o, f32[256,512]{1,0:T(8,128)} %get-tuple-element.49.base_k, ...), custom_call_target="tpu_custom_call" | custom-call | flops 3000000000 | bytes 3000000 | tf_op jit(solution)/shard_map/pallas_call | solution.py:373
  (60 shorter events, 19.4 us)
Async XLA Ops:
  8.0 50.4 %all-to-all-start = ((bf16[128,8,640]{2,1,0:T(8,128)(2,1)}), bf16[128,8,640]{2,1,0:T(8,128)(2,1)S(1)}, u32[]{:S(2)}, u32[]{:S(2)}) async-start(bf16[128,8,640]{2,1,0:T(8,128)(2,1)} %get-tuple-element.38), calls=%async_computation | async-start | bytes 2621440 | tf_op jit(solution)/shard_map/all_to_all | solution.py:370
  27.5 37.1 %collective-permute-start.6 = (bf16[256,512]{1,0:T(8,128)(2,1)}, bf16[256,512]{1,0:T(8,128)(2,1)S(1)}, u32[]{:S(2)}, u32[]{:S(2)}) collective-permute-start(bf16[256,512]{1,0:T(8,128)(2,1)} %get-tuple-element.42), channel_id=1, source_target_pairs={{0,1},{1,0},{2,3},{3,2},{4,5},{5,4},{6,7},{7,6},{8,9},{9,8},{10,11... | collective-permute-start | bytes 786440 | tf_op jit(solution)/shard_map/ppermute | solution.py:367
  58.4 1.1 copy-start.1
  61.2 4.5 %collective-permute-start.5 = (f32[8,128]{1,0:T(8,128)}, f32[8,128]{1,0:T(8,128)S(1)}, u32[]{:S(2)}, u32[]{:S(2)}) collective-permute-start(f32[8,128]{1,0:T(8,128)} %shard_map.129.a_ref), channel_id=1, source_target_pairs={{0,1},{1,0},{2,3},{3,2},{4,5},{5,4},{6,7},{7,6},{8,9},{9,8},{10,11... | collective-permute-start | bytes 12296 | tf_op jit(solution)/shard_map/ppermute | solution.py:367
  64.6 1.0 copy-start.14
  66.2 8.5 %copy-start.3 = (bf16[512,1024]{1,0:T(8,128)(2,1)S(1)}, bf16[512,1024]{1,0:T(8,128)(2,1)}, u32[]{:S(2)}) copy-start(bf16[512,1024]{1,0:T(8,128)(2,1)} %wi.1) | copy-start | bytes 3145732
  68.4 7.0 %copy-start.4 = (bf16[1024,512]{1,0:T(8,128)(2,1)S(1)}, bf16[1024,512]{1,0:T(8,128)(2,1)}, u32[]{:S(2)}) copy-start(bf16[1024,512]{1,0:T(8,128)(2,1)} %wo.2) | copy-start | bytes 3145732
  68.4 8.1 %copy-start.15 = (f32[1024]{0:T(1024)S(1)}, f32[1024]{0:T(1024)}, u32[]{:S(2)}) copy-start(f32[1024]{0:T(1024)} %param.13) | copy-start | bytes 12292
  68.4 37.5 %all-to-all-start.1 = ((bf16[128,8,256]{2,1,0:T(8,128)(2,1)}), bf16[128,8,256]{2,1,0:T(8,128)(2,1)S(1)}, u32[]{:S(2)}, u32[]{:S(2)}) async-start(bf16[128,8,256]{2,1,0:T(8,128)(2,1)} %shard_map.131), calls=%async_computation.1 | async-start | bytes 1048576 | tf_op jit(solution)/shard_map/all_to_all | solution.py:370
  74.8 18.7 %collective-permute-start = (bf16[256,1024]{1,0:T(8,128)(2,1)S(1)}, bf16[256,1024]{1,0:T(8,128)(2,1)S(1)}, u32[]{:S(2)}, u32[]{:S(2)}) collective-permute-start(bf16[256,1024]{1,0:T(8,128)(2,1)S(1)} %constant_dynamic-slice_fusion.1), channel_id=1, source_target_pairs={{0,2},{2,0},{4,6},{6,4},{8,10},{10,8},{12,14},{14,12},{16,18},{18,... | collective-permute-start | bytes 1572872 | tf_op jit(solution)/shard_map/ppermute | solution.py:364
  75.5 29.3 %collective-permute-start.2 = (bf16[1024,256]{1,0:T(8,128)(2,1)S(1)}, bf16[1024,256]{1,0:T(8,128)(2,1)S(1)}, u32[]{:S(2)}, u32[]{:S(2)}) collective-permute-start(bf16[1024,256]{1,0:T(8,128)(2,1)S(1)} %constant_dynamic-slice_fusion), channel_id=1, source_target_pairs={{0,2},{2,0},{4,6},{6,4},{8,10},{10,8},{12,14},{14,12},{16,18},{18,... | collective-permute-start | bytes 1572872 | tf_op jit(solution)/shard_map/ppermute | solution.py:364
  76.5 37.1 %collective-permute-start.4 = (f32[1024]{0:T(1024)S(1)}, f32[1024]{0:T(1024)S(1)}, u32[]{:S(2)}, u32[]{:S(2)}) collective-permute-start(f32[1024]{0:T(1024)S(1)} %copy-done.15), channel_id=1, source_target_pairs={{0,2},{2,0},{4,6},{6,4},{8,10},{10,8},{12,14},{14,12},{16,18},{18,... | collective-permute-start | bytes 12296 | tf_op jit(solution)/shard_map/ppermute | solution.py:364
  93.4 20.0 %copy-start.9 = (bf16[256,1024]{1,0:T(8,128)(2,1)}, bf16[256,1024]{1,0:T(8,128)(2,1)S(1)}, u32[]{:S(2)}) copy-start(bf16[256,1024]{1,0:T(8,128)(2,1)S(1)} %collective-permute-done.wiy) | copy-start | bytes 1572868
  93.4 20.1 %collective-permute-start.1 = (bf16[256,1024]{1,0:T(8,128)(2,1)S(1)}, bf16[256,1024]{1,0:T(8,128)(2,1)S(1)}, u32[]{:S(2)}, u32[]{:S(2)}) collective-permute-start(bf16[256,1024]{1,0:T(8,128)(2,1)S(1)} %collective-permute-done.wiy), channel_id=1, source_target_pairs={{0,1},{1,0},{2,3},{3,2},{4,5},{5,4},{6,7},{7,6},{8,9},{9,8},{10,11... | collective-permute-start | bytes 1572872 | tf_op jit(solution)/shard_map/ppermute | solution.py:367
  104.7 8.7 %copy-start.10 = (bf16[1024,256]{1,0:T(8,128)(2,1)}, bf16[1024,256]{1,0:T(8,128)(2,1)S(1)}, u32[]{:S(2)}) copy-start(bf16[1024,256]{1,0:T(8,128)(2,1)S(1)} %collective-permute-done.2.woy) | copy-start | bytes 1572868
  104.7 8.8 %collective-permute-start.3 = (bf16[1024,256]{1,0:T(8,128)(2,1)S(1)}, bf16[1024,256]{1,0:T(8,128)(2,1)S(1)}, u32[]{:S(2)}, u32[]{:S(2)}) collective-permute-start(bf16[1024,256]{1,0:T(8,128)(2,1)S(1)} %collective-permute-done.2.woy), channel_id=1, source_target_pairs={{0,1},{1,0},{2,3},{3,2},{4,5},{5,4},{6,7},{7,6},{8,9},{9,8},{10,11... | collective-permute-start | bytes 1572872 | tf_op jit(solution)/shard_map/ppermute | solution.py:367
  113.4 15.0 %collective-permute-start.7 = (bf16[256,1536]{1,0:T(8,128)(2,1)}, bf16[256,1536]{1,0:T(8,128)(2,1)S(1)}, u32[]{:S(2)}, u32[]{:S(2)}) collective-permute-start(bf16[256,1536]{1,0:T(8,128)(2,1)} %get-tuple-element.45), channel_id=1, source_target_pairs={{0,1},{1,0},{2,3},{3,2},{4,5},{5,4},{6,7},{7,6},{8,9},{9,8},{10,11... | collective-permute-start | bytes 2359304 | tf_op jit(solution)/shard_map/ppermute | solution.py:367
  133.0 67.5 %all-to-all-start.2 = ((bf16[128,8,896]{2,1,0:T(8,128)(2,1)}), bf16[128,8,896]{2,1,0:T(8,128)(2,1)S(1)}, u32[]{:S(2)}, u32[]{:S(2)}) async-start(bf16[128,8,896]{2,1,0:T(8,128)(2,1)} %shard_map.133), calls=%async_computation.2 | async-start | bytes 3670016 | tf_op jit(solution)/shard_map/all_to_all | solution.py:370
  150.6 6.2 %collective-permute-start.10 = (bf16[2048,256]{1,0:T(8,128)(2,1)}, bf16[2048,256]{1,0:T(8,128)(2,1)S(1)}, u32[]{:S(2)}, u32[]{:S(2)}) collective-permute-start(bf16[2048,256]{1,0:T(8,128)(2,1)} %get-tuple-element.64), channel_id=1, source_target_pairs={{0,1},{1,0},{2,3},{3,2},{4,5},{5,4},{6,7},{7,6},{8,9},{9,8},{10,11... | collective-permute-start | bytes 3145736 | tf_op jit(solution)/shard_map/ppermute | solution.py:367
  156.8 5.0 %collective-permute-start.8 = (bf16[272,2048]{1,0:T(8,128)(2,1)}, bf16[272,2048]{1,0:T(8,128)(2,1)S(1)}, u32[]{:S(2)}, u32[]{:S(2)}) collective-permute-start(bf16[272,2048]{1,0:T(8,128)(2,1)} %get-tuple-element.57), channel_id=1, source_target_pairs={{0,1},{1,0},{2,3},{3,2},{4,5},{5,4},{6,7},{7,6},{8,9},{9,8},{10,11... | collective-permute-start | bytes 3342344 | tf_op jit(solution)/shard_map/ppermute | solution.py:367
  160.9 21.2 %collective-permute-start.11 = (bf16[1024,256]{1,0:T(8,128)(2,1)}, bf16[1024,256]{1,0:T(8,128)(2,1)S(1)}, u32[]{:S(2)}, u32[]{:S(2)}) collective-permute-start(bf16[1024,256]{1,0:T(8,128)(2,1)} %get-tuple-element.66), channel_id=1, source_target_pairs={{0,2},{2,0},{4,6},{6,4},{8,10},{10,8},{12,14},{14,12},{16,18},{18,... | collective-permute-start | bytes 1572872 | tf_op jit(solution)/shard_map/ppermute | solution.py:364
  161.8 1.0 copy-start.5
  165.9 31.2 %collective-permute-start.9 = (bf16[272,1024]{1,0:T(8,128)(2,1)}, bf16[272,1024]{1,0:T(8,128)(2,1)S(1)}, u32[]{:S(2)}, u32[]{:S(2)}) collective-permute-start(bf16[272,1024]{1,0:T(8,128)(2,1)} %get-tuple-element.59), channel_id=1, source_target_pairs={{0,2},{2,0},{4,6},{6,4},{8,10},{10,8},{12,14},{14,12},{16,18},{18,... | collective-permute-start | bytes 1671176 | tf_op jit(solution)/shard_map/ppermute | solution.py:364
  200.5 1.3 copy-start
  (9 other events, 7.2 us)
where the time goes:
time: 205 us
  waiting for transfers between devices  80.7 us (39%)
  Pallas kernels  66.2 us (32%)
  starting transfers between devices  46.9 us (23%)
  local copies, waits for them, and re-layouts  9.26 us (5%)
    pallas_call x15, Pallas kernels, run(): call(body, outs, scratch, smem_in=smem_in, n_in=len(args), smem_out=smem_...  66.2 us
    ppermute x5, waiting for transfers between devices, across(): return lax.ppermute(v, 'wide', pair)  49.7 us
    all_to_all x3, starting transfers between devices, deal(): return lax.all_to_all(v, 'wide', split_axis=0, concat_axis=0, tiled=True)  34.9 us
    all_to_all x3, waiting for transfers between devices, deal(): return lax.all_to_all(v, 'wide', split_axis=0, concat_axis=0, tiled=True)  30 us
    unnamed x36, local copies, waits for them, and re-layouts  9.18 us
    ppermute x7, starting transfers between devices, beside(): return lax.ppermute(v, 'narrow', swap)  8.36 us
  transfers between devices with their start and end apart: 15, of which 6 were waited for; matrix products, arithmetic and copies ran while one was open for 0% of the time, Pallas kernels for 25%

commit v1 on v0

--- a/solution.py
+++ b/solution.py
@@ -55,7 +55,7 @@
     return lax.broadcasted_iota(jnp.int32, shape, 0) < 4
 
 
-def call(body, outs, scratch=(), smem_in=(), n_in=0, smem_out=(), cost=None, specs=None):
+def call(body, outs, scratch=(), smem_in=(), n_in=0, smem_out=(), cost=None, specs=None, mib=24):
     return pl.pallas_call(
         body,
         out_shape=outs,
@@ -64,7 +64,7 @@
         out_specs=[SM if i in smem_out else VM for i in range(len(outs))],
         scratch_shapes=list(scratch),
         cost_estimate=cost,
-        compiler_params=pltpu.CompilerParams(vmem_limit_bytes=56 * 1024 * 1024),
+        compiler_params=pltpu.CompilerParams(vmem_limit_bytes=mib * 1024 * 1024),
     )
 
 
@@ -139,19 +139,21 @@
     return jnp.where(r == 4 * (k % CHIPS) + 2 * core + k // CHIPS, 1.0, 0.0).astype(BF)
 
 
-def chunk_kernel(recv, out):
-    v = jnp.sum(recv[...].astype(F32), axis=0)
-    out[...] = v + pltpu.roll(v, 4, 0)
-
-
-def spread_kernel(a_ref, b_ref, keep, near, out, rows):
-    v = ((a_ref[...] + b_ref[...]) * (1.0 / TOTAL)).astype(BF)
-    out[:, :, 0:128] = jnp.broadcast_to(v[None], (CHIPS, 8, 128))
+def deal_query_kernel(keep, near, out, rows):
     tot = keep[...] + near[...].astype(F32)
     for j in range(2):
         for q in range(4):
             rows[pl.ds(4 * j + q, CHIPS, stride=8), :] = tot[CHIPS * j : CHIPS * j + CHIPS, 128 * q : 128 * q + 128]
-    out[:, :, 128:256] = rows[...].reshape(CHIPS, 8, 128).astype(BF)
+    out[...] = rows[...].reshape(CHIPS, 8, 128).astype(BF)
+
+
+def spread_kernel(recv, query, out):
+    v = jnp.sum(recv[...].astype(F32), axis=0)
+    v = (v + pltpu.roll(v, 4, 0)) * (1.0 / TOTAL)
+    hi = v.astype(BF).astype(F32)
+    v = jnp.where(low_rows((8, 128)), hi, v - hi).astype(BF)
+    out[:, :, 0:128] = jnp.broadcast_to(v[None], (CHIPS, 8, 128))
+    out[:, :, 128:256] = query[...]
 
 
 def expert_kernel(
@@ -208,65 +210,54 @@
         send[2 * i + 1, :, :] = jnp.where(low, pltpu.roll(o, 4, 0), k).astype(BF)
 
 
-def weight_in_kernel(pos, x_s, gpre, keep, send):
+def weight_kernel(pos, x_s, c_s, hid, gpre, keep_i, send_i, keep_o, send_o):
     n = pos[3]
     mine = pl.ds(pl.multiple_of(n * 256, 256), 256)
     other = pl.ds(pl.multiple_of(256 - n * 256, 256), 256)
 
-    @pl.loop(0, 4)
+    @pl.loop(0, 2)
     def _(i):
         cols = pl.ds(pl.multiple_of(i * 512, 512), 512)
         g = gpre[:, cols]
-        keep[0:256, cols] = t_mm(x_s[:, mine], g) * SHARE
-        send[0:256, cols] = (t_mm(x_s[:, other], g) * SHARE).astype(BF)
+        keep_i[0:256, cols] = t_mm(x_s[:, mine], g) * SHARE
+        send_i[0:256, cols] = (t_mm(x_s[:, other], g) * SHARE).astype(BF)
         bias = jnp.sum(g.astype(F32), axis=0, keepdims=True) * SHARE
-        keep[256:272, cols] = jnp.broadcast_to(bias, (16, 512))
-        send[256:272, cols] = jnp.broadcast_to(bias, (16, 512)).astype(BF)
-
-
-def weight_out_kernel(pos, c_s, hid, keep, send):
-    n = pos[3]
-    mine = pl.ds(pl.multiple_of(n * 256, 256), 256)
-    other = pl.ds(pl.multiple_of(256 - n * 256, 256), 256)
-
-    @pl.loop(0, 4)
-    def _(i):
-        cols = pl.ds(pl.multiple_of(i * 512, 512), 512)
+        keep_i[256:272, cols] = jnp.broadcast_to(bias, (16, 512))
+        send_i[256:272, cols] = jnp.broadcast_to(bias, (16, 512)).astype(BF)
         h = hid[:, cols]
-        keep[cols, :] = t_mm(h, c_s[:, mine]) * SHARE
-        send[cols, :] = (t_mm(h, c_s[:, other]) * SHARE).astype(BF)
-
-
-def merge_in_kernel(keep, recv, here, away):
-    here[...] = keep[:, :HALF] + recv[:, :HALF].astype(F32)
-    away[...] = (keep[:, HALF:] + recv[:, HALF:].astype(F32)).astype(BF)
-
-
-def merge_out_kernel(keep, recv, here, away):
-    here[...] = keep[:HALF, :] + recv[:HALF, :].astype(F32)
-    away[...] = (keep[HALF:, :] + recv[HALF:, :].astype(F32)).astype(BF)
-
-
-def end_in_kernel(pos, here, recv, out, bias, row):
-    out[...] = here[:256, :] + recv[:256, :].astype(F32)
-    row[...] = (here[256:272, :] + recv[256:272, :].astype(F32))[0:8, :]
+        keep_o[cols, :] = t_mm(h, c_s[:, mine]) * SHARE
+        send_o[cols, :] = (t_mm(h, c_s[:, other]) * SHARE).astype(BF)
+
+
+def merge_kernel(keep_i, got_i, keep_o, got_o, away_i, away_o):
+    away_i[...] = (keep_i[...] + got_i[...].astype(F32)).astype(BF)
+    away_o[...] = (keep_o[...] + got_o[...].astype(F32)).astype(BF)
+
+
+def end_kernel(pos, keep_i, got_i, far_i, keep_o, got_o, far_o, grad_i, bias, grad_o, row):
+    def total(a, b, c, rows):
+        return a[rows, :] + b[rows, :].astype(F32) + c[rows, :].astype(F32)
+
+    grad_i[...] = total(keep_i, got_i, far_i, slice(0, 256))
+    row[...] = total(keep_i, got_i, far_i, slice(256, 272))[0:8, :]
     bias[...] = row[0:1, pl.ds(pl.multiple_of(pos[3] * 512, 512), 512)]
-
-
-def end_out_kernel(here, recv, out):
-    out[...] = here[...] + recv[...].astype(F32)
-
-
-def attn_kernel(pos, rs, qkv_ref, g_ref, x_ref, c_ref, mix_ref, gq, keep, send, query, ss):
+    grad_o[...] = total(keep_o, got_o, far_o, slice(0, HALF))
+
+
+def attn_kernel(pos, rs, rs2, qkv_ref, g_ref, x_ref, c_ref, mix_ref, gq, keep, send, query, ss):
     low = low_rows((8, 128))
 
     @pl.loop(0, 32)
     def _(i):
-        t = [
-            jnp.where(low, rs[4 * i + 2 * h, :, 0:128].astype(F32), rs[4 * i + 2 * h + 1, :, 0:128].astype(F32))
-            for h in range(2)
-        ]
-        ss[pl.ds(pl.multiple_of(i * 16, 16), 16), :] = jnp.concatenate(t, axis=0).astype(BF)
+        tiles = []
+        for h in range(2):
+            pair = []
+            for k in range(2):
+                d = 4 * i + 2 * h + k
+                v = rs[d, :, 0:128].astype(F32) + rs2[d].astype(F32)
+                pair.append(v + pltpu.roll(v, 4, 0))
+            tiles.append(jnp.where(low, pair[0], pair[1]))
+        ss[pl.ds(pl.multiple_of(i * 16, 16), 16), :] = jnp.concatenate(tiles, axis=0).astype(BF)
 
     ones = head_ones()
     qkv, g = qkv_ref[...], g_ref[...]
@@ -369,10 +360,10 @@
     def deal(v):
         return lax.all_to_all(v, "wide", split_axis=0, concat_axis=0, tiled=True)
 
-    def run(body, us, outs, args, scratch=(), smem_in=(), smem_out=(), specs=None):
+    def run(body, us, outs, args, scratch=(), smem_in=(), smem_out=(), specs=None, mib=24):
         return call(
             body, outs, scratch, smem_in=smem_in, n_in=len(args), smem_out=smem_out, cost=cost(us),
-            specs=specs,
+            specs=specs, mib=mib,
         )(*args)
 
     wiy = across(lax.dynamic_slice_in_dim(wi, n * 256, 256, 0))
@@ -387,14 +378,13 @@
     )
     recv = deal(send)
     keep_q, away_q = run(query_kernel, 2, [sds((PTS, W), F32), sds((PTS, W), BF)], (pos, x, g), (), (0,))
-    near_q = beside(away_q)
-    (chunk,) = run(
-        chunk_kernel, 1, [sds((8, 128), F32)], (recv,),
+    (dealt_q,) = run(
+        deal_query_kernel, 1, [sds((CHIPS, 8, 128), BF)], (keep_q, beside(away_q)),
+        [pltpu.VMEM((8 * CHIPS, 128), F32)],
+    )
+    (spread,) = run(
+        spread_kernel, 1, [sds((CHIPS, 8, 256), BF)], (recv, dealt_q),
         specs={0: pl.BlockSpec((CHIPS, 8, 128), lambda i: (0, 0, 4))},
-    )
-    (spread,) = run(
-        spread_kernel, 1, [sds((CHIPS, 8, 256), BF)], (chunk, beside(chunk), keep_q, near_q),
-        [pltpu.VMEM((8 * CHIPS, 128), F32)],
     )
     rs = deal(spread)
     ret, x_s, c_s, hid, gpre = run(
@@ -402,34 +392,38 @@
         [sds((CHIPS, 8, W), BF), sds((W, W), BF), sds((W, W), BF), sds((W, 2 * HALF), BF), sds((W, 2 * HALF), BF)],
         (pos, recv, wi, wiy, win, wo, woy, won, bi.reshape(1, HALF), bp.reshape(1, HALF)),
         [pltpu.VMEM((W, W), F32), pltpu.VMEM((W, W), F32)], (0,),
-        specs={1: pl.BlockSpec((CHIPS, 8, W), lambda i: (0, 0, 0))},
-    )
+        specs={1: pl.BlockSpec((CHIPS, 8, W), lambda i: (0, 0, 0))}, mib=32,
+    )
+    rs2 = beside(rs)
+
+    def weights(half):
+        part = pl.BlockSpec((W, HALF), lambda i: (0, half))
+        return run(
+            weight_kernel, 5,
+            [sds((272, HALF), F32), sds((272, HALF), BF), sds((HALF, 256), F32), sds((HALF, 256), BF)],
+            (pos, x_s, c_s, hid, gpre), (), (0,), specs={3: part, 4: part},
+        )
+
+    keep_i, send_i, keep_o, send_o = weights(1)
+    got_i, got_o = beside(send_i), beside(send_o)
     mixed, gq, keep, away, query = run(
         attn_kernel, 7,
         [sds((PTS, W), BF), sds((PTS, 3 * W), BF), sds((PTS, 3 * W), F32), sds((PTS, 3 * W), BF), sds((8, 128), F32)],
-        (pos, rs, qkv, g, x, c), [pltpu.VMEM((W, 128), BF)], (0,),
+        (pos, rs, rs2, qkv, g, x, c), [pltpu.VMEM((W, 128), BF)], (0,),
+        specs={2: pl.BlockSpec((CHIPS, 8, 128), lambda i: (0, 0, 0))},
     )
     near = beside(away)
-    base_o, base_k = run(base_kernel, 2, [sds((PTS, W), F32), sds((PTS, W), F32)], (x, c, mixed, gq, wq, wo_att))
+    away_i, away_o = run(merge_kernel, 2, [sds((272, HALF), BF), sds((HALF, 256), BF)], (keep_i, got_i, keep_o, got_o))
+    far_i, far_o = across(away_i), across(away_o)
     (joined,) = run(join_kernel, 2, [sds((CHIPS, 8, 896), BF)], (ret, keep, near), [pltpu.VMEM((24 * CHIPS, 128), F32)])
     back = deal(joined)
-    keep_i, send_i = run(
-        weight_in_kernel, 4, [sds((272, 2 * HALF), F32), sds((272, 2 * HALF), BF)], (pos, x_s, gpre), (), (0,)
-    )
-    got_i = beside(send_i)
-    keep_o, send_o = run(
-        weight_out_kernel, 4, [sds((2 * HALF, 256), F32), sds((2 * HALF, 256), BF)], (pos, c_s, hid), (), (0,)
-    )
-    got_o = beside(send_o)
-    here_i, away_i = run(merge_in_kernel, 1, [sds((272, HALF), F32), sds((272, HALF), BF)], (keep_i, got_i))
-    far_i = across(away_i)
-    here_o, away_o = run(merge_out_kernel, 1, [sds((HALF, 256), F32), sds((HALF, 256), BF)], (keep_o, got_o))
-    far_o = across(away_o)
-    grad_in, grad_b = run(
-        end_in_kernel, 1, [sds((256, HALF), F32), sds((1, 512), F32)],
-        (pos, here_i, far_i), [pltpu.VMEM((8, HALF), F32)], (0,),
-    )
-    (grad_out,) = run(end_out_kernel, 1, [sds((HALF, 256), F32)], (here_o, far_o))
+    base_o, base_k = run(base_kernel, 2, [sds((PTS, W), F32), sds((PTS, W), F32)], (x, c, mixed, gq, wq, wo_att))
+    keep_i, send_i, keep_o, send_o = weights(0)
+    got_i, got_o = beside(send_i), beside(send_o)
+    grad_in, grad_b, grad_out = run(
+        end_kernel, 3, [sds((256, HALF), F32), sds((1, 512), F32), sds((HALF, 256), F32)],
+        (pos, keep_i, got_i, far_i, keep_o, got_o, far_o), [pltpu.VMEM((8, HALF), F32)], (0,),
+    )
     layer_out, grad_feats, att = run(
         final_kernel, 3, [sds((PTS, W), BF), sds((PTS, W), BF), sds((2, 4 * W), F32)],
         (slots, back, base_o, base_k, query), (), (0,),

time: 205 us -> 195 us (0.951)
  Pallas kernels: 66.2 us -> 32.3 us
  local copies, waits for them, and re-layouts: 9.26 us -> 21.1 us
  waiting for transfers between devices: 80.7 us -> 90 us
  starting transfers between devices: 46.9 us -> 49.4 us
    pallas_call x15 -> x13, Pallas kernels: 66.2 us -> 32.3 us  [run(): call(body, outs, scratch, smem_in=smem_in, n_in=len(args), smem_out=smem_...]
    all_to_all x3, waiting for transfers between devices: 30 us -> 44 us  [deal(): return lax.all_to_all(v, 'wide', split_axis=0, concat_axis=0, tiled=True)]
    unnamed x36 -> x64, local copies, waits for them, and re-layouts: 9.18 us -> 18.4 us
    ppermute x5, waiting for transfers between devices: 49.7 us -> 43.9 us  [across(): return lax.ppermute(v, 'wide', pair)]
    all_to_all x3, starting transfers between devices: 34.9 us -> 37.1 us  [deal(): return lax.all_to_all(v, 'wide', split_axis=0, concat_axis=0, tiled=True)]
    ppermute x7 -> x9, starting transfers between devices: 8.36 us -> 9.03 us  [beside(): return lax.ppermute(v, 'narrow', swap)]
  transfers between devices with their start and end apart: 15 -> 17, of which waited for: 6 -> 6; matrix products, arithmetic and copies ran while one was open for 0% -> 1% of each run, Pallas kernels for 25% -> 12%
where the time goes in v1:
time: 195 us; the launch traced here: 194 us
  waiting for transfers between devices  90 us (46%)
  starting transfers between devices  49.4 us (25%)
  Pallas kernels  32.3 us (17%)
  local copies, waits for them, and re-layouts  21.1 us (11%)
    all_to_all x3, waiting for transfers between devices, deal(): return lax.all_to_all(v, 'wide', split_axis=0, concat_axis=0, tiled=True)  44 us
    ppermute x5, waiting for transfers between devices, across(): return lax.ppermute(v, 'wide', pair)  43.9 us
    all_to_all x3, starting transfers between devices, deal(): return lax.all_to_all(v, 'wide', split_axis=0, concat_axis=0, tiled=True)  37.1 us
    pallas_call x13, Pallas kernels, run(): call(body, outs, scratch, smem_in=smem_in, n_in=len(args), smem_out=smem_...  32.3 us
    unnamed x64, local copies, waits for them, and re-layouts  18.4 us
    ppermute x9, starting transfers between devices, beside(): return lax.ppermute(v, 'narrow', swap)  9.03 us
  transfers between devices with their start and end apart: 17, of which 6 were waited for; matrix products, arithmetic and copies ran while one was open for 1% of the time, Pallas kernels for 12%

profile of v1, /device:TPU:1, one launch (start us, length us, event | category | flops | bytes accessed | tf_op | source)
XLA Modules:
  0.0 193.8 jit_solution(5326375982177229568)
XLA Ops:
  0.6 1.4 copy-done.3
  5.6 5.7 %shard_map.127 = (bf16[128,8,640]{2,1,0:T(8,128)(2,1)}, s32[64]{0:T(128)S(1)}, bf16[256,1536]{1,0:T(8,128)(2,1)S(1)}, bf16[256,512]{1,0:T(8,128)(2,1)S(1)}) custom-call(s32[64]{0:T(128)S(1)} %copy-done.13, bf16[256,512]{1,0:T(8,128)(2,1)S(1)} %copy-done.7, bf16[256,512]{1,0:T(8,128)(2,1)S(1)} %copy-done.9, bf16[512,1536]{1,0:T(8,128)(2,1)S(1)} %copy-done.3, ...), custom_call_target="tpu_custom_call" | custom-call | flops 5000000000 | bytes 5000000 | tf_op jit(solution)/shard_map/pallas_call | solution.py:364
  12.3 16.5 %all-to-all-start = ((bf16[128,8,640]{2,1,0:T(8,128)(2,1)}), bf16[128,8,640]{2,1,0:T(8,128)(2,1)S(1)}, u32[]{:S(2)}, u32[]{:S(2)}) async-start(bf16[128,8,640]{2,1,0:T(8,128)(2,1)} %get-tuple-element.41), calls=%async_computation | async-start | bytes 2621440 | tf_op jit(solution)/shard_map/all_to_all | solution.py:361
  28.9 1.3 shard_map.129
  32.5 30.4 %all-to-all-done.recv = bf16[128,8,640]{2,1,0:T(8,128)(2,1)S(1)} async-done(((bf16[128,8,640]{2,1,0:T(8,128)(2,1)}), bf16[128,8,640]{2,1,0:T(8,128)(2,1)S(1)}, u32[]{:S(2)}, u32[]{:S(2)}) %all-to-all-start) | async-done | bytes 1310752 | tf_op jit(solution)/shard_map/all_to_all | solution.py:361
  63.9 8.3 %all-to-all-start.1 = ((bf16[128,8,256]{2,1,0:T(8,128)(2,1)}), bf16[128,8,256]{2,1,0:T(8,128)(2,1)S(1)}, u32[]{:S(2)}, u32[]{:S(2)}) async-start(bf16[128,8,256]{2,1,0:T(8,128)(2,1)} %shard_map.131), calls=%async_computation.1 | async-start | bytes 1048576 | tf_op jit(solution)/shard_map/all_to_all | solution.py:361
  73.6 1.9 constant_dynamic-slice_fusion
  76.4 13.6 %all-to-all-done.1.rs = bf16[128,8,256]{2,1,0:T(8,128)(2,1)S(1)} async-done(((bf16[128,8,256]{2,1,0:T(8,128)(2,1)}), bf16[128,8,256]{2,1,0:T(8,128)(2,1)S(1)}, u32[]{:S(2)}, u32[]{:S(2)}) %all-to-all-start.1) | async-done | bytes 524320 | tf_op jit(solution)/shard_map/all_to_all | solution.py:361
  90.0 3.8 %collective-permute-start.6 = (bf16[128,8,256]{2,1,0:T(8,128)(2,1)S(1)}, bf16[128,8,256]{2,1,0:T(8,128)(2,1)S(1)}, u32[]{:S(2)}, u32[]{:S(2)}) collective-permute-start(bf16[128,8,256]{2,1,0:T(8,128)(2,1)S(1)} %all-to-all-done.1.rs), channel_id=1, source_target_pairs={{0,1},{1,0},{2,3},{3,2},{4,5},{5,4},{6,7},{7,6},{8,9},{9,8},{10,11... | collective-permute-start | bytes 1572872 | tf_op jit(solution)/shard_map/ppermute | solution.py:358
  94.4 8.0 %collective-permute-done.2.woy = bf16[1024,256]{1,0:T(8,128)(2,1)} collective-permute-done((bf16[1024,256]{1,0:T(8,128)(2,1)}, bf16[1024,256]{1,0:T(8,128)(2,1)}, u32[]{:S(2)}, u32[]{:S(2)}) %collective-permute-start.2) | collective-permute-done | bytes 524320 | tf_op jit(solution)/shard_map/ppermute | solution.py:355
  102.5 1.8 collective-permute-start.3
  106.4 4.9 %shard_map.132 = (bf16[256,512]{1,0:T(8,128)(2,1)S(1)}, bf16[256,1536]{1,0:T(8,128)(2,1)S(1)}, f32[256,1536]{1,0:T(8,128)S(1)}, bf16[256,1536]{1,0:T(8,128)(2,1)S(1)}, f32[8,128]{1,0:T(8,128)S(1)}) custom-call(s32[4]{0:T(128)S(1)} %pad_add_fusion.pos, bf16[128,8,256]{2,1,0:T(8,128)(2,1)S(1)} %all-to-all-done.1.rs, ...), custom_call_target="tpu_custom_call" | custom-call | flops 7000000000 | bytes 7000000 | tf_op jit(solution)/shard_map/pallas_call | solution.py:364
  112.9 9.9 %shard_map.128 = (bf16[128,8,512]{2,1,0:T(8,128)(2,1)S(1)}, bf16[512,512]{1,0:T(8,128)(2,1)S(1)}, bf16[512,512]{1,0:T(8,128)(2,1)S(1)}, bf16[512,2048]{1,0:T(8,128)(2,1)S(1)}, bf16[512,2048]{1,0:T(8,128)(2,1)S(1)}) custom-call(s32[4]{0:T(128)S(1)} %pad_add_fusion.pos, bf16[128,8,640]{2,1,0:T(8,128)(2,1)S(1)} %all-to-all-done.recv, ...), custom_call_target="tpu_custom_call" | custom-call | flops 12000000000 | bytes 12000000 | tf_op jit(solution)/shard_map/pallas_call | solution.py:364
  122.8 1.4 copy-done.18
  124.1 1.4 copy-done.20
  127.7 1.3 copy-done
  129.0 12.3 %all-to-all-start.2 = ((bf16[128,8,896]{2,1,0:T(8,128)(2,1)}), bf16[128,8,896]{2,1,0:T(8,128)(2,1)S(1)}, u32[]{:S(2)}, u32[]{:S(2)}) async-start(bf16[128,8,896]{2,1,0:T(8,128)(2,1)} %copy-done), calls=%async_computation.2 | async-start | bytes 3670016 | tf_op jit(solution)/shard_map/all_to_all | solution.py:361
  141.3 1.6 copy-done.19
  142.9 1.6 copy-done.21
  144.5 2.1 %shard_map.137 = (f32[272,1024]{1,0:T(8,128)S(1)}, bf16[272,1024]{1,0:T(8,128)(2,1)S(1)}, f32[1024,256]{1,0:T(8,128)S(1)}, bf16[1024,256]{1,0:T(8,128)(2,1)S(1)}) custom-call(s32[4]{0:T(128)S(1)} %pad_add_fusion.pos, bf16[512,512]{1,0:T(8,128)(2,1)S(1)} %copy-done.27, bf16[512,512]{1,0:T(8,128)(2,1)S(1)} %copy-done.30, bf16[512,2048]{1,0:T(8,128)(2,1)S(1)} %copy-done.19, ...), custom_call_target="tpu_custom_call" | custom-call | flops 5000000000 | bytes 5000000 | tf_op jit(solution)/shard_map/pallas_call | solution.py:364
  147.7 2.1 %shard_map.136 = (f32[272,1024]{1,0:T(8,128)S(1)}, bf16[272,1024]{1,0:T(8,128)(2,1)S(1)}, f32[1024,256]{1,0:T(8,128)S(1)}, bf16[1024,256]{1,0:T(8,128)(2,1)S(1)}) custom-call(s32[4]{0:T(128)S(1)} %pad_add_fusion.pos, bf16[512,512]{1,0:T(8,128)(2,1)S(1)} %copy-done.28, bf16[512,512]{1,0:T(8,128)(2,1)S(1)} %copy-done.31, bf16[512,2048]{1,0:T(8,128)(2,1)S(1)} %copy-done.19, ...), custom_call_target="tpu_custom_call" | custom-call | flops 5000000000 | bytes 5000000 | tf_op jit(solution)/shard_map/pallas_call | solution.py:364
  153.3 35.9 %collective-permute-done.13.far_o = bf16[1024,256]{1,0:T(8,128)(2,1)S(1)} collective-permute-done((bf16[1024,256]{1,0:T(8,128)(2,1)S(1)}, bf16[1024,256]{1,0:T(8,128)(2,1)S(1)}, u32[]{:S(2)}, u32[]{:S(2)}) %collective-permute-start.13) | collective-permute-done | bytes 524320 | tf_op jit(solution)/shard_map/ppermute | solution.py:355
  189.2 2.1 %shard_map.139 = (f32[256,1024]{1,0:T(8,128)}, f32[1,512]{1,0:T(1,128)}, f32[1024,256]{1,0:T(8,128)}) custom-call(s32[4]{0:T(128)S(1)} %pad_add_fusion.pos, f32[272,1024]{1,0:T(8,128)S(1)} %get-tuple-element.61.keep_i, bf16[272,1024]{1,0:T(8,128)(2,1)S(1)} %collective-permute-done.8.got_i, bf16[272,1024]{1,0:T(8,128)(2,1)S(1)} %collective-permute-done.11.far_i, ...), custom_call_target="tpu_custom_call" | custom-call | flops 3000000000 | bytes 3000000 | tf_op jit(solution)/shard_map/pallas_call | solution.py:364
  192.2 1.6 shard_map.135
  (90 shorter events, 22.2 us)
Async XLA Ops:
  12.3 17.9 %copy-start.22 = (bf16[256,512]{1,0:T(8,128)(2,1)}, bf16[256,512]{1,0:T(8,128)(2,1)S(1)}, u32[]{:S(2)}) copy-start(bf16[256,512]{1,0:T(8,128)(2,1)S(1)} %get-tuple-element.43.g_ref) | copy-start | bytes 786436
  12.3 16.6 %copy-start.8 = (bf16[256,512]{1,0:T(8,128)(2,1)S(1)}, bf16[256,512]{1,0:T(8,128)(2,1)}, u32[]{:S(2)}) copy-start(bf16[256,512]{1,0:T(8,128)(2,1)} %x.1) | copy-start | bytes 786436
  12.3 50.6 %all-to-all-start = ((bf16[128,8,640]{2,1,0:T(8,128)(2,1)}), bf16[128,8,640]{2,1,0:T(8,128)(2,1)S(1)}, u32[]{:S(2)}, u32[]{:S(2)}) async-start(bf16[128,8,640]{2,1,0:T(8,128)(2,1)} %get-tuple-element.41), calls=%async_computation | async-start | bytes 2621440 | tf_op jit(solution)/shard_map/all_to_all | solution.py:361
  30.1 2.2 %collective-permute-start.5 = (bf16[256,512]{1,0:T(8,128)(2,1)S(1)}, bf16[256,512]{1,0:T(8,128)(2,1)S(1)}, u32[]{:S(2)}, u32[]{:S(2)}) collective-permute-start(bf16[256,512]{1,0:T(8,128)(2,1)S(1)} %get-tuple-element.45), channel_id=1, source_target_pairs={{0,1},{1,0},{2,3},{3,2},{4,5},{5,4},{6,7},{7,6},{8,9},{9,8},{10,11... | collective-permute-start | bytes 786440 | tf_op jit(solution)/shard_map/ppermute | solution.py:358
  32.5 39.7 %copy-start.1 = (bf16[512,1024]{1,0:T(8,128)(2,1)S(1)}, bf16[512,1024]{1,0:T(8,128)(2,1)}, u32[]{:S(2)}) copy-start(bf16[512,1024]{1,0:T(8,128)(2,1)} %wi.1) | copy-start | bytes 3145732
  63.9 30.0 %copy-start.12 = (f32[1024]{0:T(1024)S(1)}, f32[1024]{0:T(1024)}, u32[]{:S(2)}) copy-start(f32[1024]{0:T(1024)} %param.13) | copy-start | bytes 12292
  63.9 40.4 %copy-start.10 = (bf16[256,512]{1,0:T(8,128)(2,1)S(1)}, bf16[256,512]{1,0:T(8,128)(2,1)}, u32[]{:S(2)}) copy-start(bf16[256,512]{1,0:T(8,128)(2,1)} %c.1) | copy-start | bytes 786436
  63.9 26.2 %all-to-all-start.1 = ((bf16[128,8,256]{2,1,0:T(8,128)(2,1)}), bf16[128,8,256]{2,1,0:T(8,128)(2,1)S(1)}, u32[]{:S(2)}, u32[]{:S(2)}) async-start(bf16[128,8,256]{2,1,0:T(8,128)(2,1)} %shard_map.131), calls=%async_computation.1 | async-start | bytes 1048576 | tf_op jit(solution)/shard_map/all_to_all | solution.py:361
  73.1 21.1 %collective-permute-start = (bf16[256,1024]{1,0:T(8,128)(2,1)}, bf16[256,1024]{1,0:T(8,128)(2,1)}, u32[]{:S(2)}, u32[]{:S(2)}) collective-permute-start(bf16[256,1024]{1,0:T(8,128)(2,1)} %constant_dynamic-slice_fusion.1), channel_id=1, source_target_pairs={{0,2},{2,0},{4,6},{6,4},{8,10},{10,8},{12,14},{14,12},{16,18},{18,... | collective-permute-start | bytes 1572872 | tf_op jit(solution)/shard_map/ppermute | solution.py:355
  75.5 26.9 %collective-permute-start.2 = (bf16[1024,256]{1,0:T(8,128)(2,1)}, bf16[1024,256]{1,0:T(8,128)(2,1)}, u32[]{:S(2)}, u32[]{:S(2)}) collective-permute-start(bf16[1024,256]{1,0:T(8,128)(2,1)} %constant_dynamic-slice_fusion), channel_id=1, source_target_pairs={{0,2},{2,0},{4,6},{6,4},{8,10},{10,8},{12,14},{14,12},{16,18},{18,... | collective-permute-start | bytes 1572872 | tf_op jit(solution)/shard_map/ppermute | solution.py:355
  90.0 14.3 %collective-permute-start.6 = (bf16[128,8,256]{2,1,0:T(8,128)(2,1)S(1)}, bf16[128,8,256]{2,1,0:T(8,128)(2,1)S(1)}, u32[]{:S(2)}, u32[]{:S(2)}) collective-permute-start(bf16[128,8,256]{2,1,0:T(8,128)(2,1)S(1)} %all-to-all-done.1.rs), channel_id=1, source_target_pairs={{0,1},{1,0},{2,3},{3,2},{4,5},{5,4},{6,7},{7,6},{8,9},{9,8},{10,11... | collective-permute-start | bytes 1572872 | tf_op jit(solution)/shard_map/ppermute | solution.py:358
  93.9 19.0 %collective-permute-start.4 = (f32[1024]{0:T(1024)S(1)}, f32[1024]{0:T(1024)S(1)}, u32[]{:S(2)}, u32[]{:S(2)}) collective-permute-start(f32[1024]{0:T(1024)S(1)} %copy-done.12), channel_id=1, source_target_pairs={{0,2},{2,0},{4,6},{6,4},{8,10},{10,8},{12,14},{14,12},{16,18},{18,... | collective-permute-start | bytes 12296 | tf_op jit(solution)/shard_map/ppermute | solution.py:355
  94.2 18.7 %collective-permute-start.1 = (bf16[256,1024]{1,0:T(8,128)(2,1)}, bf16[256,1024]{1,0:T(8,128)(2,1)S(1)}, u32[]{:S(2)}, u32[]{:S(2)}) collective-permute-start(bf16[256,1024]{1,0:T(8,128)(2,1)} %collective-permute-done.wiy), channel_id=1, source_target_pairs={{0,1},{1,0},{2,3},{3,2},{4,5},{5,4},{6,7},{7,6},{8,9},{9,8},{10,11... | collective-permute-start | bytes 1572872 | tf_op jit(solution)/shard_map/ppermute | solution.py:358
  102.5 10.4 %collective-permute-start.3 = (bf16[1024,256]{1,0:T(8,128)(2,1)}, bf16[1024,256]{1,0:T(8,128)(2,1)S(1)}, u32[]{:S(2)}, u32[]{:S(2)}) collective-permute-start(bf16[1024,256]{1,0:T(8,128)(2,1)} %collective-permute-done.2.woy), channel_id=1, source_target_pairs={{0,1},{1,0},{2,3},{3,2},{4,5},{5,4},{6,7},{7,6},{8,9},{9,8},{10,11... | collective-permute-start | bytes 1572872 | tf_op jit(solution)/shard_map/ppermute | solution.py:358
  112.8 14.2 %collective-permute-start.7 = (bf16[256,1536]{1,0:T(8,128)(2,1)S(1)}, bf16[256,1536]{1,0:T(8,128)(2,1)S(1)}, u32[]{:S(2)}, u32[]{:S(2)}) collective-permute-start(bf16[256,1536]{1,0:T(8,128)(2,1)S(1)} %get-tuple-element.48), channel_id=1, source_target_pairs={{0,1},{1,0},{2,3},{3,2},{4,5},{5,4},{6,7},{7,6},{8,9},{9,8},{10,11... | collective-permute-start | bytes 2359304 | tf_op jit(solution)/shard_map/ppermute | solution.py:358
  129.0 12.3 %copy-start.27 = (bf16[512,512]{1,0:T(8,128)(2,1)S(1)}, bf16[512,512]{1,0:T(8,128)(2,1)}, u32[]{:S(2)}) copy-start(bf16[512,512]{1,0:T(8,128)(2,1)} %copy-done.26) | copy-start | bytes 1572868
  129.0 12.3 %copy-start.30 = (bf16[512,512]{1,0:T(8,128)(2,1)S(1)}, bf16[512,512]{1,0:T(8,128)(2,1)}, u32[]{:S(2)}) copy-start(bf16[512,512]{1,0:T(8,128)(2,1)} %copy-done.29) | copy-start | bytes 1572868
  129.0 63.2 %all-to-all-start.2 = ((bf16[128,8,896]{2,1,0:T(8,128)(2,1)}), bf16[128,8,896]{2,1,0:T(8,128)(2,1)S(1)}, u32[]{:S(2)}, u32[]{:S(2)}) async-start(bf16[128,8,896]{2,1,0:T(8,128)(2,1)} %copy-done), calls=%async_computation.2 | async-start | bytes 3670016 | tf_op jit(solution)/shard_map/all_to_all | solution.py:361
  146.5 3.5 %collective-permute-start.9 = (bf16[272,1024]{1,0:T(8,128)(2,1)S(1)}, bf16[272,1024]{1,0:T(8,128)(2,1)S(1)}, u32[]{:S(2)}, u32[]{:S(2)}) collective-permute-start(bf16[272,1024]{1,0:T(8,128)(2,1)S(1)} %get-tuple-element.64), channel_id=1, source_target_pairs={{0,1},{1,0},{2,3},{3,2},{4,5},{5,4},{6,7},{7,6},{8,9},{9,8},{10,11... | collective-permute-start | bytes 1671176 | tf_op jit(solution)/shard_map/ppermute | solution.py:358
  147.4 2.7 %collective-permute-start.10 = (bf16[1024,256]{1,0:T(8,128)(2,1)S(1)}, bf16[1024,256]{1,0:T(8,128)(2,1)S(1)}, u32[]{:S(2)}, u32[]{:S(2)}) collective-permute-start(bf16[1024,256]{1,0:T(8,128)(2,1)S(1)} %get-tuple-element.66), channel_id=1, source_target_pairs={{0,1},{1,0},{2,3},{3,2},{4,5},{5,4},{6,7},{7,6},{8,9},{9,8},{10,11... | collective-permute-start | bytes 1572872 | tf_op jit(solution)/shard_map/ppermute | solution.py:358
  149.8 3.5 %collective-permute-start.8 = (bf16[272,1024]{1,0:T(8,128)(2,1)S(1)}, bf16[272,1024]{1,0:T(8,128)(2,1)S(1)}, u32[]{:S(2)}, u32[]{:S(2)}) collective-permute-start(bf16[272,1024]{1,0:T(8,128)(2,1)S(1)} %get-tuple-element.62), channel_id=1, source_target_pairs={{0,1},{1,0},{2,3},{3,2},{4,5},{5,4},{6,7},{7,6},{8,9},{9,8},{10,11... | collective-permute-start | bytes 1671176 | tf_op jit(solution)/shard_map/ppermute | solution.py:358
  150.2 38.9 %collective-permute-start.11 = (bf16[272,1024]{1,0:T(8,128)(2,1)S(1)}, bf16[272,1024]{1,0:T(8,128)(2,1)S(1)}, u32[]{:S(2)}, u32[]{:S(2)}) collective-permute-start(bf16[272,1024]{1,0:T(8,128)(2,1)S(1)} %get-tuple-element.67), channel_id=1, source_target_pairs={{0,2},{2,0},{4,6},{6,4},{8,10},{10,8},{12,14},{14,12},{16,18},{18,... | collective-permute-start | bytes 1671176 | tf_op jit(solution)/shard_map/ppermute | solution.py:355
  151.2 2.1 %collective-permute-start.12 = (bf16[1024,256]{1,0:T(8,128)(2,1)S(1)}, bf16[1024,256]{1,0:T(8,128)(2,1)S(1)}, u32[]{:S(2)}, u32[]{:S(2)}) collective-permute-start(bf16[1024,256]{1,0:T(8,128)(2,1)S(1)} %get-tuple-element.69), channel_id=1, source_target_pairs={{0,1},{1,0},{2,3},{3,2},{4,5},{5,4},{6,7},{7,6},{8,9},{9,8},{10,11... | collective-permute-start | bytes 1572872 | tf_op jit(solution)/shard_map/ppermute | solution.py:358
  151.8 37.4 %collective-permute-start.13 = (bf16[1024,256]{1,0:T(8,128)(2,1)S(1)}, bf16[1024,256]{1,0:T(8,128)(2,1)S(1)}, u32[]{:S(2)}, u32[]{:S(2)}) collective-permute-start(bf16[1024,256]{1,0:T(8,128)(2,1)S(1)} %get-tuple-element.70), channel_id=1, source_target_pairs={{0,2},{2,0},{4,6},{6,4},{8,10},{10,8},{12,14},{14,12},{16,18},{18,... | collective-permute-start | bytes 1572872 | tf_op jit(solution)/shard_map/ppermute | solution.py:355
  (25 other events, 42.3 us)

commit v2 on v1

--- a/solution.py
+++ b/solution.py
@@ -76,7 +76,22 @@
     return jax.ShapeDtypeStruct(shape, dtype)
 
 
-def front_kernel(ids, x_ref, c_ref, wq_ref, wo_ref, send, slots, qkv_ref, g_ref, cnt, ss):
+def far(shape, dtype):
+    return pltpu.HBM(shape, dtype)
+
+
+def in_hbm(v):
+    return pltpu.with_memory_space_constraint(v, pltpu.HBM)
+
+
+def front_kernel(ids, x_ref, c_ref, wq_hbm, wo_hbm, send, slots, qkv_ref, g_ref, cnt, ss, wq_ref, wo_ref, sems):
+    loads = [
+        pltpu.make_async_copy(wq_hbm, wq_ref, sems.at[0]),
+        pltpu.make_async_copy(wo_hbm, wo_ref, sems.at[1]),
+    ]
+    for load in loads:
+        load.start()
+
     @pl.loop(0, NB)
     def _(i):
         cnt[i] = 0
@@ -101,6 +116,8 @@
             send[slots[4 * i + 2 * h], :, 0:W] = jnp.where(low, xa, cr).astype(BF)
             send[slots[4 * i + 2 * h + 1], :, 0:W] = jnp.where(low, xr, ca).astype(BF)
 
+    for load in loads:
+        load.wait()
     ones = head_ones()
     qkv = mm(x_ref[...], wq_ref[...]).astype(BF)
     qkv_ref[...] = qkv
@@ -157,7 +174,8 @@
 
 
 def expert_kernel(
-    pos, recv, wi, wiy, win, wo, woy, won, b_ref, bp_ref, send, x_s, c_s, hid, gpre, o_s, k_s
+    pos, recv, wi, wiy, win, wo, woy, won, b_ref, bp_ref,
+    send, x_out, c_out, hid_out, gpre_out, keep_i, send_i, keep_o, send_o, x_s, c_s, hid, gpre, o_s, k_s
 ):
     n = pos[3]
     mine = pl.ds(pl.multiple_of(n * 256, 256), 256)
@@ -209,24 +227,34 @@
         send[2 * i, :, :] = jnp.where(low, o, pltpu.roll(k, 4, 0)).astype(BF)
         send[2 * i + 1, :, :] = jnp.where(low, pltpu.roll(o, 4, 0), k).astype(BF)
 
-
-def weight_kernel(pos, x_s, c_s, hid, gpre, keep_i, send_i, keep_o, send_o):
-    n = pos[3]
+    x_out[...] = x_s[...]
+    c_out[...] = c_s[...]
+    hid_out[...] = hid[:, :HALF]
+    gpre_out[...] = gpre[:, :HALF]
+    grad_part(n, HALF, x_s, c_s, hid, gpre, keep_i, send_i, keep_o, send_o)
+
+
+def grad_part(n, start, x_s, c_s, hid, gpre, keep_i, send_i, keep_o, send_o):
     mine = pl.ds(pl.multiple_of(n * 256, 256), 256)
     other = pl.ds(pl.multiple_of(256 - n * 256, 256), 256)
 
     @pl.loop(0, 2)
     def _(i):
         cols = pl.ds(pl.multiple_of(i * 512, 512), 512)
-        g = gpre[:, cols]
+        src = pl.ds(pl.multiple_of(start + i * 512, 512), 512)
+        g = gpre[:, src]
         keep_i[0:256, cols] = t_mm(x_s[:, mine], g) * SHARE
         send_i[0:256, cols] = (t_mm(x_s[:, other], g) * SHARE).astype(BF)
         bias = jnp.sum(g.astype(F32), axis=0, keepdims=True) * SHARE
         keep_i[256:272, cols] = jnp.broadcast_to(bias, (16, 512))
         send_i[256:272, cols] = jnp.broadcast_to(bias, (16, 512)).astype(BF)
-        h = hid[:, cols]
+        h = hid[:, src]
         keep_o[cols, :] = t_mm(h, c_s[:, mine]) * SHARE
         send_o[cols, :] = (t_mm(h, c_s[:, other]) * SHARE).astype(BF)
+
+
+def weight_kernel(pos, x_s, c_s, hid, gpre, keep_i, send_i, keep_o, send_o):
+    grad_part(pos[3], 0, x_s, c_s, hid, gpre, keep_i, send_i, keep_o, send_o)
 
 
 def merge_kernel(keep_i, got_i, keep_o, got_o, away_i, away_o):
@@ -371,10 +399,16 @@
     bp = across(bi)
     win, won = beside(wiy), beside(woy)
 
+    anywhere = pl.BlockSpec(memory_space=pltpu.HBM)
     send, slots, qkv, g = run(
         front_kernel, 5,
-        [sds((CHIPS, 8, 640), BF), sds((NB,), jnp.int32), sds((PTS, 3 * W), BF), sds((PTS, W), BF)],
-        (ids, x, c, wq, wo_att), [pltpu.SMEM((NB,), jnp.int32), pltpu.VMEM((W, 128), F32)], (0,), (1,),
+        [far((CHIPS, 8, 640), BF), sds((NB,), jnp.int32), far((PTS, 3 * W), BF), far((PTS, W), BF)],
+        (ids, in_hbm(x), in_hbm(c), in_hbm(wq), in_hbm(wo_att)),
+        [
+            pltpu.SMEM((NB,), jnp.int32), pltpu.VMEM((W, 128), F32), pltpu.VMEM((W, 3 * W), BF),
+            pltpu.VMEM((W, W), BF), pltpu.SemaphoreType.DMA((2,)),
+        ],
+        (0,), (1,), specs={3: anywhere, 4: anywhere}, mib=48,
     )
     recv = deal(send)
     keep_q, away_q = run(query_kernel, 2, [sds((PTS, W), F32), sds((PTS, W), BF)], (pos, x, g), (), (0,))
@@ -383,29 +417,21 @@
         [pltpu.VMEM((8 * CHIPS, 128), F32)],
     )
     (spread,) = run(
-        spread_kernel, 1, [sds((CHIPS, 8, 256), BF)], (recv, dealt_q),
+        spread_kernel, 1, [far((CHIPS, 8, 256), BF)], (recv, dealt_q),
         specs={0: pl.BlockSpec((CHIPS, 8, 128), lambda i: (0, 0, 4))},
     )
     rs = deal(spread)
-    ret, x_s, c_s, hid, gpre = run(
+    grads = [((272, HALF), F32), ((272, HALF), BF), ((HALF, 256), F32), ((HALF, 256), BF)]
+    ret, x_s, c_s, hid, gpre, keep_i, send_i, keep_o, send_o = run(
         expert_kernel, 12,
-        [sds((CHIPS, 8, W), BF), sds((W, W), BF), sds((W, W), BF), sds((W, 2 * HALF), BF), sds((W, 2 * HALF), BF)],
-        (pos, recv, wi, wiy, win, wo, woy, won, bi.reshape(1, HALF), bp.reshape(1, HALF)),
-        [pltpu.VMEM((W, W), F32), pltpu.VMEM((W, W), F32)], (0,),
-        specs={1: pl.BlockSpec((CHIPS, 8, W), lambda i: (0, 0, 0))}, mib=32,
-    )
+        [far((CHIPS, 8, W), BF), far((W, W), BF), far((W, W), BF), far((W, HALF), BF), far((W, HALF), BF)]
+        + [far(*v) for v in grads],
+        (pos, recv, *map(in_hbm, (wi, wiy, win, wo, woy, won)), bi.reshape(1, HALF), bp.reshape(1, HALF)),
+        [pltpu.VMEM((W, W), BF)] * 2 + [pltpu.VMEM((W, 2 * HALF), BF)] * 2 + [pltpu.VMEM((W, W), F32)] * 2, (0,),
+        specs={1: pl.BlockSpec((CHIPS, 8, W), lambda i: (0, 0, 0))}, mib=48,
+    )
+    got_i, got_o = beside(send_i), beside(send_o)
     rs2 = beside(rs)
-
-    def weights(half):
-        part = pl.BlockSpec((W, HALF), lambda i: (0, half))
-        return run(
-            weight_kernel, 5,
-            [sds((272, HALF), F32), sds((272, HALF), BF), sds((HALF, 256), F32), sds((HALF, 256), BF)],
-            (pos, x_s, c_s, hid, gpre), (), (0,), specs={3: part, 4: part},
-        )
-
-    keep_i, send_i, keep_o, send_o = weights(1)
-    got_i, got_o = beside(send_i), beside(send_o)
     mixed, gq, keep, away, query = run(
         attn_kernel, 7,
         [sds((PTS, W), BF), sds((PTS, 3 * W), BF), sds((PTS, 3 * W), F32), sds((PTS, 3 * W), BF), sds((8, 128), F32)],
@@ -413,12 +439,14 @@
         specs={2: pl.BlockSpec((CHIPS, 8, 128), lambda i: (0, 0, 0))},
     )
     near = beside(away)
-    away_i, away_o = run(merge_kernel, 2, [sds((272, HALF), BF), sds((HALF, 256), BF)], (keep_i, got_i, keep_o, got_o))
+    base_o, base_k = run(base_kernel, 1, [far((PTS, W), F32), far((PTS, W), F32)], (x, c, mixed, gq, wq, wo_att))
+    away_i, away_o = run(merge_kernel, 1, [sds((272, HALF), BF), sds((HALF, 256), BF)], (keep_i, got_i, keep_o, got_o))
     far_i, far_o = across(away_i), across(away_o)
-    (joined,) = run(join_kernel, 2, [sds((CHIPS, 8, 896), BF)], (ret, keep, near), [pltpu.VMEM((24 * CHIPS, 128), F32)])
+    (joined,) = run(join_kernel, 2, [far((CHIPS, 8, 896), BF)], (ret, keep, near), [pltpu.VMEM((24 * CHIPS, 128), F32)])
     back = deal(joined)
-    base_o, base_k = run(base_kernel, 2, [sds((PTS, W), F32), sds((PTS, W), F32)], (x, c, mixed, gq, wq, wo_att))
-    keep_i, send_i, keep_o, send_o = weights(0)
+    keep_i, send_i, keep_o, send_o = run(
+        weight_kernel, 5, [sds(*v) for v in grads], (pos, x_s, c_s, hid, gpre), (), (0,)
+    )
     got_i, got_o = beside(send_i), beside(send_o)
     grad_in, grad_b, grad_out = run(
         end_kernel, 3, [sds((256, HALF), F32), sds((1, 512), F32), sds((HALF, 256), F32)],
@@ -426,7 +454,7 @@
     )
     layer_out, grad_feats, att = run(
         final_kernel, 3, [sds((PTS, W), BF), sds((PTS, W), BF), sds((2, 4 * W), F32)],
-        (slots, back, base_o, base_k, query), (), (0,),
+        (slots, back, in_hbm(base_o), in_hbm(base_k), query), (), (0,),
     )
     return (layer_out, grad_feats, att, grad_in, grad_out, grad_b.reshape(512))
 

time: 195 us -> 193 us (0.990)
  local copies, waits for them, and re-layouts: 21.1 us -> 11.6 us
  Pallas kernels: 32.3 us -> 39.1 us
    unnamed x64 -> x36, local copies, waits for them, and re-layouts: 18.4 us -> 9.47 us
    pallas_call x13 -> x12, Pallas kernels: 32.3 us -> 39.1 us  [run(): call(body, outs, scratch, smem_in=smem_in, n_in=len(args), smem_out=smem_...]
  transfers between devices with their start and end apart: 17 -> 17, of which waited for: 6 -> 6; matrix products, arithmetic and copies ran while one was open for 1% -> 1% of each run, Pallas kernels for 12% -> 14%
where the time goes in v2:
time: 193 us; the launch traced here: 192 us
  waiting for transfers between devices  91 us (47%)
  starting transfers between devices  49.6 us (26%)
  Pallas kernels  39.1 us (20%)
  local copies, waits for them, and re-layouts  11.6 us (6%)
    ppermute x5, waiting for transfers between devices, across(): return lax.ppermute(v, 'wide', pair)  44.6 us
    all_to_all x3, waiting for transfers between devices, deal(): return lax.all_to_all(v, 'wide', split_axis=0, concat_axis=0, tiled=True)  44.4 us
    pallas_call x12, Pallas kernels, run(): call(body, outs, scratch, smem_in=smem_in, n_in=len(args), smem_out=smem_...  39.1 us
    all_to_all x3, starting transfers between devices, deal(): return lax.all_to_all(v, 'wide', split_axis=0, concat_axis=0, tiled=True)  36.9 us
    unnamed x36, local copies, waits for them, and re-layouts  9.47 us
    ppermute x9, starting transfers between devices, beside(): return lax.ppermute(v, 'narrow', swap)  9.16 us
  transfers between devices with their start and end apart: 17, of which 6 were waited for; matrix products, arithmetic and copies ran while one was open for 1% of the time, Pallas kernels for 14%

profile of v2, /device:TPU:1, one launch (start us, length us, event | category | flops | bytes accessed | tf_op | source)
XLA Modules:
  0.0 192.3 jit_solution(11873728825847704460)
XLA Ops:
  1.3 7.0 %shard_map.127 = (bf16[128,8,640]{2,1,0:T(8,128)(2,1)}, s32[64]{0:T(128)S(1)}, bf16[256,1536]{1,0:T(8,128)(2,1)}, bf16[256,512]{1,0:T(8,128)(2,1)}) custom-call(s32[64]{0:T(128)S(1)} %copy-done.5, bf16[256,512]{1,0:T(8,128)(2,1)} %x.1, bf16[256,512]{1,0:T(8,128)(2,1)} %c.1, bf16[512,1536]{1,0:T(8,128)(2,1)} %wq.1, bf16[512,512]{1,0:T(8,128)(2,1)} %wo.3), custom_call_target="tpu_custom_call" | custom-call | flops 5000000000 | bytes 5000000 | tf_op jit(solution)/shard_map/pallas_call | solution.py:392
  8.3 16.5 %all-to-all-start = ((bf16[128,8,640]{2,1,0:T(8,128)(2,1)}), bf16[128,8,640]{2,1,0:T(8,128)(2,1)S(1)}, u32[]{:S(2)}, u32[]{:S(2)}) async-start(bf16[128,8,640]{2,1,0:T(8,128)(2,1)} %get-tuple-element.41), calls=%async_computation | async-start | bytes 2621440 | tf_op jit(solution)/shard_map/all_to_all | solution.py:389
  24.9 1.3 shard_map.129
  27.2 1.2 collective-permute-done.5.near
  28.5 30.4 %all-to-all-done.recv = bf16[128,8,640]{2,1,0:T(8,128)(2,1)S(1)} async-done(((bf16[128,8,640]{2,1,0:T(8,128)(2,1)}), bf16[128,8,640]{2,1,0:T(8,128)(2,1)S(1)}, u32[]{:S(2)}, u32[]{:S(2)}) %all-to-all-start) | async-done | bytes 1310752 | tf_op jit(solution)/shard_map/all_to_all | solution.py:389
  59.9 8.3 %all-to-all-start.1 = ((bf16[128,8,256]{2,1,0:T(8,128)(2,1)}), bf16[128,8,256]{2,1,0:T(8,128)(2,1)S(1)}, u32[]{:S(2)}, u32[]{:S(2)}) async-start(bf16[128,8,256]{2,1,0:T(8,128)(2,1)} %shard_map.131), calls=%async_computation.1 | async-start | bytes 1048576 | tf_op jit(solution)/shard_map/all_to_all | solution.py:389
  68.3 1.1 constant_dynamic-slice_fusion.1
  72.1 14.0 %all-to-all-done.1.rs = bf16[128,8,256]{2,1,0:T(8,128)(2,1)S(1)} async-done(((bf16[128,8,256]{2,1,0:T(8,128)(2,1)}), bf16[128,8,256]{2,1,0:T(8,128)(2,1)S(1)}, u32[]{:S(2)}, u32[]{:S(2)}) %all-to-all-start.1) | async-done | bytes 524320 | tf_op jit(solution)/shard_map/all_to_all | solution.py:389
  86.1 3.8 %collective-permute-start.6 = (bf16[128,8,256]{2,1,0:T(8,128)(2,1)S(1)}, bf16[128,8,256]{2,1,0:T(8,128)(2,1)S(1)}, u32[]{:S(2)}, u32[]{:S(2)}) collective-permute-start(bf16[128,8,256]{2,1,0:T(8,128)(2,1)S(1)} %all-to-all-done.1.rs), channel_id=1, source_target_pairs={{0,1},{1,0},{2,3},{3,2},{4,5},{5,4},{6,7},{7,6},{8,9},{9,8},{10,11... | collective-permute-start | bytes 1572872 | tf_op jit(solution)/shard_map/ppermute | solution.py:386
  90.5 8.0 %collective-permute-done.2.woy = bf16[1024,256]{1,0:T(8,128)(2,1)} collective-permute-done((bf16[1024,256]{1,0:T(8,128)(2,1)S(1)}, bf16[1024,256]{1,0:T(8,128)(2,1)}, u32[]{:S(2)}, u32[]{:S(2)}) %collective-permute-start.2) | collective-permute-done | bytes 524320 | tf_op jit(solution)/shard_map/ppermute | solution.py:383
  98.5 1.8 collective-permute-start.3
  101.3 1.1 copy-done.13
  102.4 4.9 %shard_map.132 = (bf16[256,512]{1,0:T(8,128)(2,1)S(1)}, bf16[256,1536]{1,0:T(8,128)(2,1)S(1)}, f32[256,1536]{1,0:T(8,128)S(1)}, bf16[256,1536]{1,0:T(8,128)(2,1)S(1)}, f32[8,128]{1,0:T(8,128)S(1)}) custom-call(s32[4]{0:T(128)S(1)} %pad_add_fusion.pos, bf16[128,8,256]{2,1,0:T(8,128)(2,1)S(1)} %all-to-all-done.1.rs, ...), custom_call_target="tpu_custom_call" | custom-call | flops 7000000000 | bytes 7000000 | tf_op jit(solution)/shard_map/pallas_call | solution.py:392
  108.4 14.8 %shard_map.128 = (bf16[128,8,512]{2,1,0:T(8,128)(2,1)}, bf16[512,512]{1,0:T(8,128)(2,1)}, bf16[512,512]{1,0:T(8,128)(2,1)}, bf16[512,1024]{1,0:T(8,128)(2,1)}, b...) custom-call(s32[4]{0:T(128)S(1)} %pad_add_fusion.pos, ...), custom_call_target="tpu_custom_call" | custom-call | flops 12000000000 | bytes 12000000 | tf_op jit(solution)/shard_map/pallas_call | solution.py:392
  123.2 1.2 copy-done.8
  124.4 1.8 shard_map.133
  126.2 12.1 %all-to-all-start.2 = ((bf16[128,8,896]{2,1,0:T(8,128)(2,1)}), bf16[128,8,896]{2,1,0:T(8,128)(2,1)S(1)}, u32[]{:S(2)}, u32[]{:S(2)}) async-start(bf16[128,8,896]{2,1,0:T(8,128)(2,1)} %shard_map.133), calls=%async_computation.2 | async-start | bytes 3670016 | tf_op jit(solution)/shard_map/all_to_all | solution.py:389
  139.6 1.2 copy-done.11
  140.8 1.2 copy-done.12
  144.1 2.1 %shard_map.136 = (f32[272,1024]{1,0:T(8,128)S(1)}, bf16[272,1024]{1,0:T(8,128)(2,1)S(1)}, f32[1024,256]{1,0:T(8,128)S(1)}, bf16[1024,256]{1,0:T(8,128)(2,1)S(1)}) custom-call(s32[4]{0:T(128)S(1)} %pad_add_fusion.pos, bf16[512,512]{1,0:T(8,128)(2,1)S(1)} %copy-done.14, bf16[512,512]{1,0:T(8,128)(2,1)S(1)} %copy-done.15, bf16[512,1024]{1,0:T(8,128)(2,1)S(1)} %copy-done.11, ...), custom_call_target="tpu_custom_call" | custom-call | flops 5000000000 | bytes 5000000 | tf_op jit(solution)/shard_map/pallas_call | solution.py:392
  149.7 36.6 %collective-permute-done.13.far_o = bf16[1024,256]{1,0:T(8,128)(2,1)S(1)} collective-permute-done((bf16[1024,256]{1,0:T(8,128)(2,1)S(1)}, bf16[1024,256]{1,0:T(8,128)(2,1)S(1)}, u32[]{:S(2)}, u32[]{:S(2)}) %collective-permute-start.13) | collective-permute-done | bytes 524320 | tf_op jit(solution)/shard_map/ppermute | solution.py:383
  186.3 2.2 %shard_map.138 = (f32[256,1024]{1,0:T(8,128)}, f32[1,512]{1,0:T(1,128)}, f32[1024,256]{1,0:T(8,128)}) custom-call(s32[4]{0:T(128)S(1)} %pad_add_fusion.pos, f32[272,1024]{1,0:T(8,128)S(1)} %get-tuple-element.61.keep_i, bf16[272,1024]{1,0:T(8,128)(2,1)S(1)} %collective-permute-done.8.got_i, bf16[272,1024]{1,0:T(8,128)(2,1)S(1)} %collective-permute-done.11.far_i, ...), custom_call_target="tpu_custom_call" | custom-call | flops 3000000000 | bytes 3000000 | tf_op jit(solution)/shard_map/pallas_call | solution.py:392
  188.4 1.6 shard_map.134
  190.0 2.3 %shard_map.135 = (bf16[256,512]{1,0:T(8,128)(2,1)}, bf16[256,512]{1,0:T(8,128)(2,1)}, f32[2,2048]{1,0:T(2,128)}) custom-call(s32[64]{0:T(128)S(1)} %get-tuple-element.40.slots, bf16[128,8,896]{2,1,0:T(8,128)(2,1)S(1)} %all-to-all-done.2.ret, f32[256,512]{1,0:T(8,128)} %get-tuple-element.51.base_o, f32[256,512]{1,0:T(8,128)} %get-tuple-element.52.base_k, ...), custom_call_target="tpu_custom_call" | custom-call | flops 3000000000 | bytes 3000000 | tf_op jit(solution)/shard_map/pallas_call | solution.py:392
  (61 shorter events, 15.1 us)
Async XLA Ops:
  8.3 16.6 %copy-start.2 = (bf16[256,512]{1,0:T(8,128)(2,1)S(1)}, bf16[256,512]{1,0:T(8,128)(2,1)}, u32[]{:S(2)}) copy-start(bf16[256,512]{1,0:T(8,128)(2,1)} %x.1) | copy-start | bytes 786436
  8.3 16.6 %copy-start.9 = (bf16[256,512]{1,0:T(8,128)(2,1)S(1)}, bf16[256,512]{1,0:T(8,128)(2,1)}, u32[]{:S(2)}) copy-start(bf16[256,512]{1,0:T(8,128)(2,1)} %get-tuple-element.43.g_ref) | copy-start | bytes 786436
  8.3 50.6 %all-to-all-start = ((bf16[128,8,640]{2,1,0:T(8,128)(2,1)}), bf16[128,8,640]{2,1,0:T(8,128)(2,1)S(1)}, u32[]{:S(2)}, u32[]{:S(2)}) async-start(bf16[128,8,640]{2,1,0:T(8,128)(2,1)} %get-tuple-element.41), calls=%async_computation | async-start | bytes 2621440 | tf_op jit(solution)/shard_map/all_to_all | solution.py:389
  26.2 2.2 %collective-permute-start.5 = (bf16[256,512]{1,0:T(8,128)(2,1)S(1)}, bf16[256,512]{1,0:T(8,128)(2,1)S(1)}, u32[]{:S(2)}, u32[]{:S(2)}) collective-permute-start(bf16[256,512]{1,0:T(8,128)(2,1)S(1)} %get-tuple-element.45), channel_id=1, source_target_pairs={{0,1},{1,0},{2,3},{3,2},{4,5},{5,4},{6,7},{7,6},{8,9},{9,8},{10,11... | collective-permute-start | bytes 786440 | tf_op jit(solution)/shard_map/ppermute | solution.py:386
  59.9 30.0 %copy-start.4 = (f32[1024]{0:T(1024)S(1)}, f32[1024]{0:T(1024)}, u32[]{:S(2)}) copy-start(f32[1024]{0:T(1024)} %param.13) | copy-start | bytes 12292
  59.9 40.4 %copy-start.3 = (bf16[256,512]{1,0:T(8,128)(2,1)S(1)}, bf16[256,512]{1,0:T(8,128)(2,1)}, u32[]{:S(2)}) copy-start(bf16[256,512]{1,0:T(8,128)(2,1)} %c.1) | copy-start | bytes 786436
  59.9 26.1 %all-to-all-start.1 = ((bf16[128,8,256]{2,1,0:T(8,128)(2,1)}), bf16[128,8,256]{2,1,0:T(8,128)(2,1)S(1)}, u32[]{:S(2)}, u32[]{:S(2)}) async-start(bf16[128,8,256]{2,1,0:T(8,128)(2,1)} %shard_map.131), calls=%async_computation.1 | async-start | bytes 1048576 | tf_op jit(solution)/shard_map/all_to_all | solution.py:389
  69.4 20.8 %collective-permute-start = (bf16[256,1024]{1,0:T(8,128)(2,1)S(1)}, bf16[256,1024]{1,0:T(8,128)(2,1)}, u32[]{:S(2)}, u32[]{:S(2)}) collective-permute-start(bf16[256,1024]{1,0:T(8,128)(2,1)S(1)} %constant_dynamic-slice_fusion.1), channel_id=1, source_target_pairs={{0,2},{2,0},{4,6},{6,4},{8,10},{10,8},{12,14},{14,12},{16,18},{18,... | collective-permute-start | bytes 1572872 | tf_op jit(solution)/shard_map/ppermute | solution.py:383
  71.1 27.4 %collective-permute-start.2 = (bf16[1024,256]{1,0:T(8,128)(2,1)S(1)}, bf16[1024,256]{1,0:T(8,128)(2,1)}, u32[]{:S(2)}, u32[]{:S(2)}) collective-permute-start(bf16[1024,256]{1,0:T(8,128)(2,1)S(1)} %constant_dynamic-slice_fusion), channel_id=1, source_target_pairs={{0,2},{2,0},{4,6},{6,4},{8,10},{10,8},{12,14},{14,12},{16,18},{18,... | collective-permute-start | bytes 1572872 | tf_op jit(solution)/shard_map/ppermute | solution.py:383
  86.1 14.3 %collective-permute-start.6 = (bf16[128,8,256]{2,1,0:T(8,128)(2,1)S(1)}, bf16[128,8,256]{2,1,0:T(8,128)(2,1)S(1)}, u32[]{:S(2)}, u32[]{:S(2)}) collective-permute-start(bf16[128,8,256]{2,1,0:T(8,128)(2,1)S(1)} %all-to-all-done.1.rs), channel_id=1, source_target_pairs={{0,1},{1,0},{2,3},{3,2},{4,5},{5,4},{6,7},{7,6},{8,9},{9,8},{10,11... | collective-permute-start | bytes 1572872 | tf_op jit(solution)/shard_map/ppermute | solution.py:386
  89.9 17.5 %collective-permute-start.4 = (f32[1024]{0:T(1024)S(1)}, f32[1024]{0:T(1024)S(1)}, u32[]{:S(2)}, u32[]{:S(2)}) collective-permute-start(f32[1024]{0:T(1024)S(1)} %copy-done.4), channel_id=1, source_target_pairs={{0,2},{2,0},{4,6},{6,4},{8,10},{10,8},{12,14},{14,12},{16,18},{18,... | collective-permute-start | bytes 12296 | tf_op jit(solution)/shard_map/ppermute | solution.py:383
  90.2 17.2 %collective-permute-start.1 = (bf16[256,1024]{1,0:T(8,128)(2,1)}, bf16[256,1024]{1,0:T(8,128)(2,1)S(1)}, u32[]{:S(2)}, u32[]{:S(2)}) collective-permute-start(bf16[256,1024]{1,0:T(8,128)(2,1)} %collective-permute-done.wiy), channel_id=1, source_target_pairs={{0,1},{1,0},{2,3},{3,2},{4,5},{5,4},{6,7},{7,6},{8,9},{9,8},{10,11... | collective-permute-start | bytes 1572872 | tf_op jit(solution)/shard_map/ppermute | solution.py:386
  98.5 8.9 %collective-permute-start.3 = (bf16[1024,256]{1,0:T(8,128)(2,1)}, bf16[1024,256]{1,0:T(8,128)(2,1)S(1)}, u32[]{:S(2)}, u32[]{:S(2)}) collective-permute-start(bf16[1024,256]{1,0:T(8,128)(2,1)} %collective-permute-done.2.woy), channel_id=1, source_target_pairs={{0,1},{1,0},{2,3},{3,2},{4,5},{5,4},{6,7},{7,6},{8,9},{9,8},{10,11... | collective-permute-start | bytes 1572872 | tf_op jit(solution)/shard_map/ppermute | solution.py:386
  107.3 15.9 %collective-permute-start.7 = (bf16[256,1536]{1,0:T(8,128)(2,1)S(1)}, bf16[256,1536]{1,0:T(8,128)(2,1)S(1)}, u32[]{:S(2)}, u32[]{:S(2)}) collective-permute-start(bf16[256,1536]{1,0:T(8,128)(2,1)S(1)} %get-tuple-element.48), channel_id=1, source_target_pairs={{0,1},{1,0},{2,3},{3,2},{4,5},{5,4},{6,7},{7,6},{8,9},{9,8},{10,11... | collective-permute-start | bytes 2359304 | tf_op jit(solution)/shard_map/ppermute | solution.py:386
  126.2 63.8 %all-to-all-start.2 = ((bf16[128,8,896]{2,1,0:T(8,128)(2,1)}), bf16[128,8,896]{2,1,0:T(8,128)(2,1)S(1)}, u32[]{:S(2)}, u32[]{:S(2)}) async-start(bf16[128,8,896]{2,1,0:T(8,128)(2,1)} %shard_map.133), calls=%async_computation.2 | async-start | bytes 3670016 | tf_op jit(solution)/shard_map/all_to_all | solution.py:389
  138.4 8.1 %collective-permute-start.9 = (bf16[272,1024]{1,0:T(8,128)(2,1)}, bf16[272,1024]{1,0:T(8,128)(2,1)S(1)}, u32[]{:S(2)}, u32[]{:S(2)}) collective-permute-start(bf16[272,1024]{1,0:T(8,128)(2,1)} %get-tuple-element.64), channel_id=1, source_target_pairs={{0,1},{1,0},{2,3},{3,2},{4,5},{5,4},{6,7},{7,6},{8,9},{9,8},{10,11... | collective-permute-start | bytes 1671176 | tf_op jit(solution)/shard_map/ppermute | solution.py:386
  139.2 7.2 %collective-permute-start.10 = (bf16[1024,256]{1,0:T(8,128)(2,1)}, bf16[1024,256]{1,0:T(8,128)(2,1)S(1)}, u32[]{:S(2)}, u32[]{:S(2)}) collective-permute-start(bf16[1024,256]{1,0:T(8,128)(2,1)} %get-tuple-element.66), channel_id=1, source_target_pairs={{0,1},{1,0},{2,3},{3,2},{4,5},{5,4},{6,7},{7,6},{8,9},{9,8},{10,11... | collective-permute-start | bytes 1572872 | tf_op jit(solution)/shard_map/ppermute | solution.py:386
  144.1 2.4 %copy-start.6 = (f32[272,1024]{1,0:T(8,128)S(1)}, f32[272,1024]{1,0:T(8,128)}, u32[]{:S(2)}) copy-start(f32[272,1024]{1,0:T(8,128)} %get-tuple-element.63.keep_i) | copy-start | bytes 3342340
  144.1 2.4 %copy-start.7 = (f32[1024,256]{1,0:T(8,128)S(1)}, f32[1024,256]{1,0:T(8,128)}, u32[]{:S(2)}) copy-start(f32[1024,256]{1,0:T(8,128)} %get-tuple-element.65.keep_o) | copy-start | bytes 3145732
  146.1 3.6 %collective-permute-start.8 = (bf16[272,1024]{1,0:T(8,128)(2,1)S(1)}, bf16[272,1024]{1,0:T(8,128)(2,1)S(1)}, u32[]{:S(2)}, u32[]{:S(2)}) collective-permute-start(bf16[272,1024]{1,0:T(8,128)(2,1)S(1)} %get-tuple-element.62), channel_id=1, source_target_pairs={{0,1},{1,0},{2,3},{3,2},{4,5},{5,4},{6,7},{7,6},{8,9},{9,8},{10,11... | collective-permute-start | bytes 1671176 | tf_op jit(solution)/shard_map/ppermute | solution.py:386
  146.6 39.6 %collective-permute-start.11 = (bf16[272,1024]{1,0:T(8,128)(2,1)S(1)}, bf16[272,1024]{1,0:T(8,128)(2,1)S(1)}, u32[]{:S(2)}, u32[]{:S(2)}) collective-permute-start(bf16[272,1024]{1,0:T(8,128)(2,1)S(1)} %get-tuple-element.67), channel_id=1, source_target_pairs={{0,2},{2,0},{4,6},{6,4},{8,10},{10,8},{12,14},{14,12},{16,18},{18,... | collective-permute-start | bytes 1671176 | tf_op jit(solution)/shard_map/ppermute | solution.py:383
  147.6 2.1 %collective-permute-start.12 = (bf16[1024,256]{1,0:T(8,128)(2,1)S(1)}, bf16[1024,256]{1,0:T(8,128)(2,1)S(1)}, u32[]{:S(2)}, u32[]{:S(2)}) collective-permute-start(bf16[1024,256]{1,0:T(8,128)(2,1)S(1)} %get-tuple-element.69), channel_id=1, source_target_pairs={{0,1},{1,0},{2,3},{3,2},{4,5},{5,4},{6,7},{7,6},{8,9},{9,8},{10,11... | collective-permute-start | bytes 1572872 | tf_op jit(solution)/shard_map/ppermute | solution.py:386
  148.2 38.1 %collective-permute-start.13 = (bf16[1024,256]{1,0:T(8,128)(2,1)S(1)}, bf16[1024,256]{1,0:T(8,128)(2,1)S(1)}, u32[]{:S(2)}, u32[]{:S(2)}) collective-permute-start(bf16[1024,256]{1,0:T(8,128)(2,1)S(1)} %get-tuple-element.70), channel_id=1, source_target_pairs={{0,2},{2,0},{4,6},{6,4},{8,10},{10,8},{12,14},{14,12},{16,18},{18,... | collective-permute-start | bytes 1572872 | tf_op jit(solution)/shard_map/ppermute | solution.py:383
  186.3 2.2 %copy-start.1 = (bf16[512,512]{1,0:T(8,128)(2,1)S(1)}, bf16[512,512]{1,0:T(8,128)(2,1)}, u32[]{:S(2)}) copy-start(bf16[512,512]{1,0:T(8,128)(2,1)} %wo.3) | copy-start | bytes 1572868
  (11 other events, 12.4 us)

commit v3 on v2

--- a/solution.py
+++ b/solution.py
@@ -55,13 +55,15 @@
     return lax.broadcasted_iota(jnp.int32, shape, 0) < 4
 
 
-def call(body, outs, scratch=(), smem_in=(), n_in=0, smem_out=(), cost=None, specs=None, mib=24):
+def call(body, outs, scratch=(), smem_in=(), n_in=0, smem_out=(), cost=None, specs=None, mib=24, out_hbm=False):
     return pl.pallas_call(
         body,
         out_shape=outs,
         grid=(1,) if specs else (),
         in_specs=[(specs or {}).get(i, SM if i in smem_in else VM) for i in range(n_in)],
-        out_specs=[SM if i in smem_out else VM for i in range(len(outs))],
+        out_specs=[
+            pl.BlockSpec(memory_space=pltpu.HBM) if out_hbm else SM if i in smem_out else VM for i in range(len(outs))
+        ],
         scratch_shapes=list(scratch),
         cost_estimate=cost,
         compiler_params=pltpu.CompilerParams(vmem_limit_bytes=mib * 1024 * 1024),
@@ -173,14 +175,48 @@
     out[:, :, 128:256] = query[...]
 
 
+def slice_kernel(axis, src, out, sem):
+    part = pl.ds(pl.multiple_of(lax.axis_index("narrow") * 256, 256), 256)
+    load = pltpu.make_async_copy(src.at[part, :] if axis == 0 else src.at[:, part], out, sem)
+    load.start()
+    load.wait()
+
+
+def act(pre, gh, cols, hid, gpre):
+    sq = pre * pre
+    t = jnp.tanh(GS * (pre + GC * pre * sq))
+    up = 0.5 * (1.0 + t)
+    hid[:, cols] = (pre * up).astype(BF)
+    slope = up + 0.5 * pre * (1.0 - t * t) * GS * (1.0 + 3.0 * GC * sq)
+    gpre[:, cols] = (gh * slope).astype(BF)
+
+
 def expert_kernel(
-    pos, recv, wi, wiy, win, wo, woy, won, b_ref, bp_ref,
-    send, x_out, c_out, hid_out, gpre_out, keep_i, send_i, keep_o, send_o, x_s, c_s, hid, gpre, o_s, k_s
+    pos, recv, wi_h, wiy_h, win_h, wo_h, woy_h, won_h, b_ref, bp_ref,
+    send_h, x_h, c_h, hid_h, gpre_h, ki_h, si_h, ko_h, so_h,
+    x_s, c_s, hid, gpre, hid_p, gpre_p, o_s, k_s, send, ki, si, ko, so, wi, wiy, win, wo, woy, won, in_sems, out_sems,
 ):
     n = pos[3]
     mine = pl.ds(pl.multiple_of(n * 256, 256), 256)
     other = pl.ds(pl.multiple_of(256 - n * 256, 256), 256)
     low = low_rows((8, W))
+    loads = [
+        pltpu.make_async_copy(a, b, in_sems.at[k])
+        for k, (a, b) in enumerate(
+            ((wi_h, wi), (wo_h, wo), (wiy_h, wiy), (woy_h, woy), (win_h, win), (won_h, won))
+        )
+    ]
+    stores = [
+        pltpu.make_async_copy(a, b, out_sems.at[k])
+        for k, (a, b) in enumerate(
+            (
+                (x_s, x_h), (c_s, c_h), (hid, hid_h), (gpre, gpre_h),
+                (ki, ki_h), (si, si_h), (ko, ko_h), (so, so_h), (send, send_h),
+            )
+        )
+    ]
+    for load in loads:
+        load.start()
 
     @pl.loop(0, 32)
     def _(i):
@@ -194,31 +230,37 @@
         x_s[rows, :] = jnp.concatenate(xs, axis=0).astype(BF)
         c_s[rows, :] = jnp.concatenate(cs, axis=0).astype(BF)
 
-    def act(pre, gh, cols):
-        sq = pre * pre
-        t = jnp.tanh(GS * (pre + GC * pre * sq))
-        up = 0.5 * (1.0 + t)
-        hid[:, cols] = (pre * up).astype(BF)
-        slope = up + 0.5 * pre * (1.0 - t * t) * GS * (1.0 + 3.0 * GC * sq)
-        gpre[:, cols] = (gh * slope).astype(BF)
+    stores[0].start()
+    stores[1].start()
+    loads[0].wait()
+    loads[1].wait()
 
     @pl.loop(0, 4)
     def _(i):
         cols = pl.ds(pl.multiple_of(i * 256, 256), 256)
         pre = mm(x_s[...], wi[:, cols]) + b_ref[:, cols]
         gh = mm_t(c_s[...], wo[cols, :])
-        act(pre, gh, cols)
+        act(pre, gh, cols, hid, gpre)
+
+    stores[2].start()
+    stores[3].start()
+    for load in loads[2:]:
+        load.wait()
 
     @pl.loop(0, 4)
     def _(i):
         cols = pl.ds(pl.multiple_of(i * 256, 256), 256)
         pre = mm(x_s[:, mine], wiy[:, cols]) + mm(x_s[:, other], win[:, cols]) + bp_ref[:, cols]
         gh = mm_t(c_s[:, mine], woy[cols, :]) + mm_t(c_s[:, other], won[cols, :])
-        act(pre, gh, pl.ds(pl.multiple_of(HALF + i * 256, 256), 256))
+        act(pre, gh, cols, hid_p, gpre_p)
+
+    grad_part(n, x_s, c_s, hid_p, gpre_p, ki, si, ko, so)
+    for store in stores[4:8]:
+        store.start()
 
     for yr, kr, part in ((woy, wiy, mine), (won, win, other)):
-        o_s[:, part] = mm(hid[:, :HALF], wo[:, part]) + mm(hid[:, HALF:], yr[...])
-        k_s[:, part] = mm_t(gpre[:, :HALF], wi[part, :]) + mm_t(gpre[:, HALF:], kr[...])
+        o_s[:, part] = mm(hid[...], wo[:, part]) + mm(hid_p[...], yr[...])
+        k_s[:, part] = mm_t(gpre[...], wi[part, :]) + mm_t(gpre_p[...], kr[...])
 
     @pl.loop(0, 64)
     def _(i):
@@ -227,34 +269,31 @@
         send[2 * i, :, :] = jnp.where(low, o, pltpu.roll(k, 4, 0)).astype(BF)
         send[2 * i + 1, :, :] = jnp.where(low, pltpu.roll(o, 4, 0), k).astype(BF)
 
-    x_out[...] = x_s[...]
-    c_out[...] = c_s[...]
-    hid_out[...] = hid[:, :HALF]
-    gpre_out[...] = gpre[:, :HALF]
-    grad_part(n, HALF, x_s, c_s, hid, gpre, keep_i, send_i, keep_o, send_o)
-
-
-def grad_part(n, start, x_s, c_s, hid, gpre, keep_i, send_i, keep_o, send_o):
+    stores[8].start()
+    for store in stores:
+        store.wait()
+
+
+def grad_part(n, x_s, c_s, hid, gpre, keep_i, send_i, keep_o, send_o):
     mine = pl.ds(pl.multiple_of(n * 256, 256), 256)
     other = pl.ds(pl.multiple_of(256 - n * 256, 256), 256)
 
     @pl.loop(0, 2)
     def _(i):
         cols = pl.ds(pl.multiple_of(i * 512, 512), 512)
-        src = pl.ds(pl.multiple_of(start + i * 512, 512), 512)
-        g = gpre[:, src]
+        g = gpre[:, cols]
         keep_i[0:256, cols] = t_mm(x_s[:, mine], g) * SHARE
         send_i[0:256, cols] = (t_mm(x_s[:, other], g) * SHARE).astype(BF)
         bias = jnp.sum(g.astype(F32), axis=0, keepdims=True) * SHARE
         keep_i[256:272, cols] = jnp.broadcast_to(bias, (16, 512))
         send_i[256:272, cols] = jnp.broadcast_to(bias, (16, 512)).astype(BF)
-        h = hid[:, src]
+        h = hid[:, cols]
         keep_o[cols, :] = t_mm(h, c_s[:, mine]) * SHARE
         send_o[cols, :] = (t_mm(h, c_s[:, other]) * SHARE).astype(BF)
 
 
 def weight_kernel(pos, x_s, c_s, hid, gpre, keep_i, send_i, keep_o, send_o):
-    grad_part(pos[3], 0, x_s, c_s, hid, gpre, keep_i, send_i, keep_o, send_o)
+    grad_part(pos[3], x_s, c_s, hid, gpre, keep_i, send_i, keep_o, send_o)
 
 
 def merge_kernel(keep_i, got_i, keep_o, got_o, away_i, away_o):
@@ -388,22 +427,31 @@
     def deal(v):
         return lax.all_to_all(v, "wide", split_axis=0, concat_axis=0, tiled=True)
 
-    def run(body, us, outs, args, scratch=(), smem_in=(), smem_out=(), specs=None, mib=24):
+    def run(body, us, outs, args, scratch=(), smem_in=(), smem_out=(), specs=None, mib=24, out_hbm=False):
         return call(
             body, outs, scratch, smem_in=smem_in, n_in=len(args), smem_out=smem_out, cost=cost(us),
-            specs=specs, mib=mib,
+            specs=specs, mib=mib, out_hbm=out_hbm,
         )(*args)
 
-    wiy = across(lax.dynamic_slice_in_dim(wi, n * 256, 256, 0))
-    woy = across(lax.dynamic_slice_in_dim(wo, n * 256, 256, 1))
+    anywhere = pl.BlockSpec(memory_space=pltpu.HBM)
+
+    def half(v, axis):
+        shape = (256, HALF) if axis == 0 else (HALF, 256)
+        (out,) = run(
+            lambda *refs: slice_kernel(axis, *refs), 1, [sds(shape, BF)], (in_hbm(v),),
+            [pltpu.SemaphoreType.DMA], specs={0: anywhere},
+        )
+        return out
+
+    wiy = across(half(wi, 0))
+    woy = across(half(wo, 1))
     bp = across(bi)
     win, won = beside(wiy), beside(woy)
 
-    anywhere = pl.BlockSpec(memory_space=pltpu.HBM)
     send, slots, qkv, g = run(
         front_kernel, 5,
         [far((CHIPS, 8, 640), BF), sds((NB,), jnp.int32), far((PTS, 3 * W), BF), far((PTS, W), BF)],
-        (ids, in_hbm(x), in_hbm(c), in_hbm(wq), in_hbm(wo_att)),
+        (in_hbm(ids), in_hbm(x), in_hbm(c), in_hbm(wq), in_hbm(wo_att)),
         [
             pltpu.SMEM((NB,), jnp.int32), pltpu.VMEM((W, 128), F32), pltpu.VMEM((W, 3 * W), BF),
             pltpu.VMEM((W, W), BF), pltpu.SemaphoreType.DMA((2,)),
@@ -427,8 +475,16 @@
         [far((CHIPS, 8, W), BF), far((W, W), BF), far((W, W), BF), far((W, HALF), BF), far((W, HALF), BF)]
         + [far(*v) for v in grads],
         (pos, recv, *map(in_hbm, (wi, wiy, win, wo, woy, won)), bi.reshape(1, HALF), bp.reshape(1, HALF)),
-        [pltpu.VMEM((W, W), BF)] * 2 + [pltpu.VMEM((W, 2 * HALF), BF)] * 2 + [pltpu.VMEM((W, W), F32)] * 2, (0,),
-        specs={1: pl.BlockSpec((CHIPS, 8, W), lambda i: (0, 0, 0))}, mib=48,
+        [pltpu.VMEM((W, W), BF)] * 2 + [pltpu.VMEM((W, HALF), BF)] * 4 + [pltpu.VMEM((W, W), F32)] * 2
+        + [pltpu.VMEM((CHIPS, 8, W), BF)] + [pltpu.VMEM(*v) for v in grads]
+        + [
+            pltpu.VMEM(v, BF)
+            for v in ((W, HALF), (256, HALF), (256, HALF), (HALF, W), (HALF, 256), (HALF, 256))
+        ]
+        + [pltpu.SemaphoreType.DMA((6,)), pltpu.SemaphoreType.DMA((9,))],
+        (0,),
+        specs={1: pl.BlockSpec((CHIPS, 8, W), lambda i: (0, 0, 0)), **{k: anywhere for k in range(2, 8)}},
+        out_hbm=True, mib=48,
     )
     got_i, got_o = beside(send_i), beside(send_o)
     rs2 = beside(rs)

time: 193 us -> 191 us (0.990)
  local copies, waits for them, and re-layouts: 11.6 us -> 8.83 us
    dynamic_slice x2 -> x0, local copies, waits for them, and re-layouts: 2.16 us -> none  [the longest x1 1.08 us: layer(): wiy = across(lax.dynamic_slice_in_dim(wi, n * 256, 256, 0))]
    pallas_call x12 -> x14, Pallas kernels: 39.1 us -> 39.8 us  [run(): call(body, outs, scratch, smem_in=smem_in, n_in=len(args), smem_out=smem_...]
    unnamed x36 -> x34, local copies, waits for them, and re-layouts: 9.47 us -> 8.83 us
  transfers between devices with their start and end apart: 17 -> 17, of which waited for: 6 -> 6; matrix products, arithmetic and copies ran while one was open for 1% -> 0% of each run, Pallas kernels for 14% -> 15%
where the time goes in v3:
time: 191 us; the launch traced here: 190 us
  waiting for transfers between devices  91.1 us (48%)
  starting transfers between devices  49.4 us (26%)
  Pallas kernels  39.8 us (21%)
  local copies, waits for them, and re-layouts  8.83 us (5%)
    ppermute x5, waiting for transfers between devices, across(): return lax.ppermute(v, 'wide', pair)  44.6 us
    all_to_all x3, waiting for transfers between devices, deal(): return lax.all_to_all(v, 'wide', split_axis=0, concat_axis=0, tiled=True)  44.4 us
    pallas_call x14, Pallas kernels, run(): call(body, outs, scratch, smem_in=smem_in, n_in=len(args), smem_out=smem_...  39.8 us
    all_to_all x3, starting transfers between devices, deal(): return lax.all_to_all(v, 'wide', split_axis=0, concat_axis=0, tiled=True)  36.8 us
    ppermute x9, starting transfers between devices, beside(): return lax.ppermute(v, 'narrow', swap)  9.15 us
    unnamed x34, local copies, waits for them, and re-layouts  8.83 us
  transfers between devices with their start and end apart: 17, of which 6 were waited for; matrix products, arithmetic and copies ran while one was open for 0% of the time, Pallas kernels for 15%

profile of v3, /device:TPU:1, one launch (start us, length us, event | category | flops | bytes accessed | tf_op | source)
XLA Modules:
  0.0 190.1 jit_solution(9755024281002612024)
XLA Ops:
  0.6 7.0 %shard_map.127 = (bf16[128,8,640]{2,1,0:T(8,128)(2,1)}, s32[64]{0:T(128)S(1)}, bf16[256,1536]{1,0:T(8,128)(2,1)}, bf16[256,512]{1,0:T(8,128)(2,1)}) custom-call(s32[64]{0:T(128)} %ids.1, bf16[256,512]{1,0:T(8,128)(2,1)} %x.1, bf16[256,512]{1,0:T(8,128)(2,1)} %c.1, bf16[512,1536]{1,0:T(8,128)(2,1)} %wq.1, bf16[512,512]{1,0:T(8,128)(2,1)} %wo.1), custom_call_target="tpu_custom_call" | custom-call | flops 5000000000 | bytes 5000000 | tf_op jit(solution)/shard_map/pallas_call | solution.py:431
  7.7 16.5 %all-to-all-start = ((bf16[128,8,640]{2,1,0:T(8,128)(2,1)}), bf16[128,8,640]{2,1,0:T(8,128)(2,1)S(1)}, u32[]{:S(2)}, u32[]{:S(2)}) async-start(bf16[128,8,640]{2,1,0:T(8,128)(2,1)} %get-tuple-element.41), calls=%async_computation | async-start | bytes 2621440 | tf_op jit(solution)/shard_map/all_to_all | solution.py:428
  24.3 1.3 shard_map.131
  26.6 1.2 collective-permute-done.5.near
  27.9 30.4 %all-to-all-done.recv = bf16[128,8,640]{2,1,0:T(8,128)(2,1)S(1)} async-done(((bf16[128,8,640]{2,1,0:T(8,128)(2,1)}), bf16[128,8,640]{2,1,0:T(8,128)(2,1)S(1)}, u32[]{:S(2)}, u32[]{:S(2)}) %all-to-all-start) | async-done | bytes 1310752 | tf_op jit(solution)/shard_map/all_to_all | solution.py:428
  59.3 8.2 %all-to-all-start.1 = ((bf16[128,8,256]{2,1,0:T(8,128)(2,1)}), bf16[128,8,256]{2,1,0:T(8,128)(2,1)S(1)}, u32[]{:S(2)}, u32[]{:S(2)}) async-start(bf16[128,8,256]{2,1,0:T(8,128)(2,1)} %shard_map.133), calls=%async_computation.1 | async-start | bytes 1048576 | tf_op jit(solution)/shard_map/all_to_all | solution.py:428
  67.5 1.1 shard_map.128
  71.3 14.0 %all-to-all-done.1.rs = bf16[128,8,256]{2,1,0:T(8,128)(2,1)S(1)} async-done(((bf16[128,8,256]{2,1,0:T(8,128)(2,1)}), bf16[128,8,256]{2,1,0:T(8,128)(2,1)S(1)}, u32[]{:S(2)}, u32[]{:S(2)}) %all-to-all-start.1) | async-done | bytes 524320 | tf_op jit(solution)/shard_map/all_to_all | solution.py:428
  85.3 3.8 %collective-permute-start.6 = (bf16[128,8,256]{2,1,0:T(8,128)(2,1)S(1)}, bf16[128,8,256]{2,1,0:T(8,128)(2,1)S(1)}, u32[]{:S(2)}, u32[]{:S(2)}) collective-permute-start(bf16[128,8,256]{2,1,0:T(8,128)(2,1)S(1)} %all-to-all-done.1.rs), channel_id=1, source_target_pairs={{0,1},{1,0},{2,3},{3,2},{4,5},{5,4},{6,7},{7,6},{8,9},{9,8},{10,11... | collective-permute-start | bytes 1572872 | tf_op jit(solution)/shard_map/ppermute | solution.py:425
  89.7 8.0 %collective-permute-done.2.woy_h = bf16[1024,256]{1,0:T(8,128)(2,1)} collective-permute-done((bf16[1024,256]{1,0:T(8,128)(2,1)S(1)}, bf16[1024,256]{1,0:T(8,128)(2,1)}, u32[]{:S(2)}, u32[]{:S(2)}) %collective-permute-start.2) | collective-permute-done | bytes 524320 | tf_op jit(solution)/shard_map/ppermute | solution.py:422
  97.7 1.8 collective-permute-start.3
  100.5 1.1 copy-done.12
  101.6 4.9 %shard_map.134 = (bf16[256,512]{1,0:T(8,128)(2,1)S(1)}, bf16[256,1536]{1,0:T(8,128)(2,1)S(1)}, f32[256,1536]{1,0:T(8,128)S(1)}, bf16[256,1536]{1,0:T(8,128)(2,1)S(1)}, f32[8,128]{1,0:T(8,128)S(1)}) custom-call(s32[4]{0:T(128)S(1)} %pad_add_fusion.pos, bf16[128,8,256]{2,1,0:T(8,128)(2,1)S(1)} %all-to-all-done.1.rs, ...), custom_call_target="tpu_custom_call" | custom-call | flops 7000000000 | bytes 7000000 | tf_op jit(solution)/shard_map/pallas_call | solution.py:431
  107.6 13.3 %shard_map.130 = (bf16[128,8,512]{2,1,0:T(8,128)(2,1)}, bf16[512,512]{1,0:T(8,128)(2,1)}, bf16[512,512]{1,0:T(8,128)(2,1)}, bf16[512,1024]{1,0:T(8,128)(2,1)}, b...) custom-call(s32[4]{0:T(128)S(1)} %pad_add_fusion.pos, ...), custom_call_target="tpu_custom_call" | custom-call | flops 12000000000 | bytes 12000000 | tf_op jit(solution)/shard_map/pallas_call | solution.py:431
  121.0 1.2 copy-done.7
  122.2 1.8 shard_map.135
  124.0 12.1 %all-to-all-start.2 = ((bf16[128,8,896]{2,1,0:T(8,128)(2,1)}), bf16[128,8,896]{2,1,0:T(8,128)(2,1)S(1)}, u32[]{:S(2)}, u32[]{:S(2)}) async-start(bf16[128,8,896]{2,1,0:T(8,128)(2,1)} %shard_map.135), calls=%async_computation.2 | async-start | bytes 3670016 | tf_op jit(solution)/shard_map/all_to_all | solution.py:428
  137.4 1.2 copy-done.10
  138.6 1.2 copy-done.11
  141.9 2.1 %shard_map.138 = (f32[272,1024]{1,0:T(8,128)S(1)}, bf16[272,1024]{1,0:T(8,128)(2,1)S(1)}, f32[1024,256]{1,0:T(8,128)S(1)}, bf16[1024,256]{1,0:T(8,128)(2,1)S(1)}) custom-call(s32[4]{0:T(128)S(1)} %pad_add_fusion.pos, bf16[512,512]{1,0:T(8,128)(2,1)S(1)} %copy-done.13, bf16[512,512]{1,0:T(8,128)(2,1)S(1)} %copy-done.14, bf16[512,1024]{1,0:T(8,128)(2,1)S(1)} %copy-done.10, ...), custom_call_target="tpu_custom_call" | custom-call | flops 5000000000 | bytes 5000000 | tf_op jit(solution)/shard_map/pallas_call | solution.py:431
  147.5 36.5 %collective-permute-done.13.far_o = bf16[1024,256]{1,0:T(8,128)(2,1)S(1)} collective-permute-done((bf16[1024,256]{1,0:T(8,128)(2,1)S(1)}, bf16[1024,256]{1,0:T(8,128)(2,1)S(1)}, u32[]{:S(2)}, u32[]{:S(2)}) %collective-permute-start.13) | collective-permute-done | bytes 524320 | tf_op jit(solution)/shard_map/ppermute | solution.py:422
  184.1 2.2 %shard_map.140 = (f32[256,1024]{1,0:T(8,128)}, f32[1,512]{1,0:T(1,128)}, f32[1024,256]{1,0:T(8,128)}) custom-call(s32[4]{0:T(128)S(1)} %pad_add_fusion.pos, f32[272,1024]{1,0:T(8,128)S(1)} %get-tuple-element.61.keep_i, bf16[272,1024]{1,0:T(8,128)(2,1)S(1)} %collective-permute-done.8.got_i, bf16[272,1024]{1,0:T(8,128)(2,1)S(1)} %collective-permute-done.11.far_i, ...), custom_call_target="tpu_custom_call" | custom-call | flops 3000000000 | bytes 3000000 | tf_op jit(solution)/shard_map/pallas_call | solution.py:431
  186.3 1.5 shard_map.136
  187.8 2.3 %shard_map.137 = (bf16[256,512]{1,0:T(8,128)(2,1)}, bf16[256,512]{1,0:T(8,128)(2,1)}, f32[2,2048]{1,0:T(2,128)}) custom-call(s32[64]{0:T(128)S(1)} %get-tuple-element.40.slots, bf16[128,8,896]{2,1,0:T(8,128)(2,1)S(1)} %all-to-all-done.2.ret, f32[256,512]{1,0:T(8,128)} %get-tuple-element.51.base_o, f32[256,512]{1,0:T(8,128)} %get-tuple-element.52.base_k, ...), custom_call_target="tpu_custom_call" | custom-call | flops 3000000000 | bytes 3000000 | tf_op jit(solution)/shard_map/pallas_call | solution.py:431
  (59 shorter events, 14.4 us)
Async XLA Ops:
  7.6 16.6 %copy-start.2 = (bf16[256,512]{1,0:T(8,128)(2,1)S(1)}, bf16[256,512]{1,0:T(8,128)(2,1)}, u32[]{:S(2)}) copy-start(bf16[256,512]{1,0:T(8,128)(2,1)} %x.1) | copy-start | bytes 786436
  7.7 16.6 %copy-start.8 = (bf16[256,512]{1,0:T(8,128)(2,1)S(1)}, bf16[256,512]{1,0:T(8,128)(2,1)}, u32[]{:S(2)}) copy-start(bf16[256,512]{1,0:T(8,128)(2,1)} %get-tuple-element.43.g_ref) | copy-start | bytes 786436
  7.7 50.6 %all-to-all-start = ((bf16[128,8,640]{2,1,0:T(8,128)(2,1)}), bf16[128,8,640]{2,1,0:T(8,128)(2,1)S(1)}, u32[]{:S(2)}, u32[]{:S(2)}) async-start(bf16[128,8,640]{2,1,0:T(8,128)(2,1)} %get-tuple-element.41), calls=%async_computation | async-start | bytes 2621440 | tf_op jit(solution)/shard_map/all_to_all | solution.py:428
  25.5 2.2 %collective-permute-start.5 = (bf16[256,512]{1,0:T(8,128)(2,1)S(1)}, bf16[256,512]{1,0:T(8,128)(2,1)S(1)}, u32[]{:S(2)}, u32[]{:S(2)}) collective-permute-start(bf16[256,512]{1,0:T(8,128)(2,1)S(1)} %get-tuple-element.45), channel_id=1, source_target_pairs={{0,1},{1,0},{2,3},{3,2},{4,5},{5,4},{6,7},{7,6},{8,9},{9,8},{10,11... | collective-permute-start | bytes 786440 | tf_op jit(solution)/shard_map/ppermute | solution.py:425
  59.3 26.0 %all-to-all-start.1 = ((bf16[128,8,256]{2,1,0:T(8,128)(2,1)}), bf16[128,8,256]{2,1,0:T(8,128)(2,1)S(1)}, u32[]{:S(2)}, u32[]{:S(2)}) async-start(bf16[128,8,256]{2,1,0:T(8,128)(2,1)} %shard_map.133), calls=%async_computation.1 | async-start | bytes 1048576 | tf_op jit(solution)/shard_map/all_to_all | solution.py:428
  68.5 20.6 %copy-start.4 = (f32[1024]{0:T(1024)S(1)}, f32[1024]{0:T(1024)}, u32[]{:S(2)}) copy-start(f32[1024]{0:T(1024)} %param.13) | copy-start | bytes 12292
  68.6 31.0 %copy-start.3 = (bf16[256,512]{1,0:T(8,128)(2,1)S(1)}, bf16[256,512]{1,0:T(8,128)(2,1)}, u32[]{:S(2)}) copy-start(bf16[256,512]{1,0:T(8,128)(2,1)} %c.1) | copy-start | bytes 786436
  68.6 20.8 %collective-permute-start = (bf16[256,1024]{1,0:T(8,128)(2,1)S(1)}, bf16[256,1024]{1,0:T(8,128)(2,1)}, u32[]{:S(2)}, u32[]{:S(2)}) collective-permute-start(bf16[256,1024]{1,0:T(8,128)(2,1)S(1)} %shard_map.128), channel_id=1, source_target_pairs={{0,2},{2,0},{4,6},{6,4},{8,10},{10,8},{12,14},{14,12},{16,18},{18,... | collective-permute-start | bytes 1572872 | tf_op jit(solution)/shard_map/ppermute | solution.py:422
  70.3 27.4 %collective-permute-start.2 = (bf16[1024,256]{1,0:T(8,128)(2,1)S(1)}, bf16[1024,256]{1,0:T(8,128)(2,1)}, u32[]{:S(2)}, u32[]{:S(2)}) collective-permute-start(bf16[1024,256]{1,0:T(8,128)(2,1)S(1)} %shard_map.129), channel_id=1, source_target_pairs={{0,2},{2,0},{4,6},{6,4},{8,10},{10,8},{12,14},{14,12},{16,18},{18,... | collective-permute-start | bytes 1572872 | tf_op jit(solution)/shard_map/ppermute | solution.py:422
  85.3 14.3 %collective-permute-start.6 = (bf16[128,8,256]{2,1,0:T(8,128)(2,1)S(1)}, bf16[128,8,256]{2,1,0:T(8,128)(2,1)S(1)}, u32[]{:S(2)}, u32[]{:S(2)}) collective-permute-start(bf16[128,8,256]{2,1,0:T(8,128)(2,1)S(1)} %all-to-all-done.1.rs), channel_id=1, source_target_pairs={{0,1},{1,0},{2,3},{3,2},{4,5},{5,4},{6,7},{7,6},{8,9},{9,8},{10,11... | collective-permute-start | bytes 1572872 | tf_op jit(solution)/shard_map/ppermute | solution.py:425
  89.1 17.5 %collective-permute-start.4 = (f32[1024]{0:T(1024)S(1)}, f32[1024]{0:T(1024)S(1)}, u32[]{:S(2)}, u32[]{:S(2)}) collective-permute-start(f32[1024]{0:T(1024)S(1)} %copy-done.4), channel_id=1, source_target_pairs={{0,2},{2,0},{4,6},{6,4},{8,10},{10,8},{12,14},{14,12},{16,18},{18,... | collective-permute-start | bytes 12296 | tf_op jit(solution)/shard_map/ppermute | solution.py:422
  89.4 17.3 %collective-permute-start.1 = (bf16[256,1024]{1,0:T(8,128)(2,1)}, bf16[256,1024]{1,0:T(8,128)(2,1)S(1)}, u32[]{:S(2)}, u32[]{:S(2)}) collective-permute-start(bf16[256,1024]{1,0:T(8,128)(2,1)} %collective-permute-done.wiy_h), channel_id=1, source_target_pairs={{0,1},{1,0},{2,3},{3,2},{4,5},{5,4},{6,7},{7,6},{8,9},{9,8},{10,11... | collective-permute-start | bytes 1572872 | tf_op jit(solution)/shard_map/ppermute | solution.py:425
  97.7 9.0 %collective-permute-start.3 = (bf16[1024,256]{1,0:T(8,128)(2,1)}, bf16[1024,256]{1,0:T(8,128)(2,1)S(1)}, u32[]{:S(2)}, u32[]{:S(2)}) collective-permute-start(bf16[1024,256]{1,0:T(8,128)(2,1)} %collective-permute-done.2.woy_h), channel_id=1, source_target_pairs={{0,1},{1,0},{2,3},{3,2},{4,5},{5,4},{6,7},{7,6},{8,9},{9,8},{10,11... | collective-permute-start | bytes 1572872 | tf_op jit(solution)/shard_map/ppermute | solution.py:425
  106.5 14.4 %collective-permute-start.7 = (bf16[256,1536]{1,0:T(8,128)(2,1)S(1)}, bf16[256,1536]{1,0:T(8,128)(2,1)S(1)}, u32[]{:S(2)}, u32[]{:S(2)}) collective-permute-start(bf16[256,1536]{1,0:T(8,128)(2,1)S(1)} %get-tuple-element.48), channel_id=1, source_target_pairs={{0,1},{1,0},{2,3},{3,2},{4,5},{5,4},{6,7},{7,6},{8,9},{9,8},{10,11... | collective-permute-start | bytes 2359304 | tf_op jit(solution)/shard_map/ppermute | solution.py:425
  124.0 63.8 %all-to-all-start.2 = ((bf16[128,8,896]{2,1,0:T(8,128)(2,1)}), bf16[128,8,896]{2,1,0:T(8,128)(2,1)S(1)}, u32[]{:S(2)}, u32[]{:S(2)}) async-start(bf16[128,8,896]{2,1,0:T(8,128)(2,1)} %shard_map.135), calls=%async_computation.2 | async-start | bytes 3670016 | tf_op jit(solution)/shard_map/all_to_all | solution.py:428
  136.2 8.1 %collective-permute-start.9 = (bf16[272,1024]{1,0:T(8,128)(2,1)}, bf16[272,1024]{1,0:T(8,128)(2,1)S(1)}, u32[]{:S(2)}, u32[]{:S(2)}) collective-permute-start(bf16[272,1024]{1,0:T(8,128)(2,1)} %get-tuple-element.64), channel_id=1, source_target_pairs={{0,1},{1,0},{2,3},{3,2},{4,5},{5,4},{6,7},{7,6},{8,9},{9,8},{10,11... | collective-permute-start | bytes 1671176 | tf_op jit(solution)/shard_map/ppermute | solution.py:425
  137.1 7.2 %collective-permute-start.10 = (bf16[1024,256]{1,0:T(8,128)(2,1)}, bf16[1024,256]{1,0:T(8,128)(2,1)S(1)}, u32[]{:S(2)}, u32[]{:S(2)}) collective-permute-start(bf16[1024,256]{1,0:T(8,128)(2,1)} %get-tuple-element.66), channel_id=1, source_target_pairs={{0,1},{1,0},{2,3},{3,2},{4,5},{5,4},{6,7},{7,6},{8,9},{9,8},{10,11... | collective-permute-start | bytes 1572872 | tf_op jit(solution)/shard_map/ppermute | solution.py:425
  141.9 2.4 %copy-start.5 = (f32[272,1024]{1,0:T(8,128)S(1)}, f32[272,1024]{1,0:T(8,128)}, u32[]{:S(2)}) copy-start(f32[272,1024]{1,0:T(8,128)} %get-tuple-element.63.keep_i) | copy-start | bytes 3342340
  141.9 2.4 %copy-start.6 = (f32[1024,256]{1,0:T(8,128)S(1)}, f32[1024,256]{1,0:T(8,128)}, u32[]{:S(2)}) copy-start(f32[1024,256]{1,0:T(8,128)} %get-tuple-element.65.keep_o) | copy-start | bytes 3145732
  144.0 3.6 %collective-permute-start.8 = (bf16[272,1024]{1,0:T(8,128)(2,1)S(1)}, bf16[272,1024]{1,0:T(8,128)(2,1)S(1)}, u32[]{:S(2)}, u32[]{:S(2)}) collective-permute-start(bf16[272,1024]{1,0:T(8,128)(2,1)S(1)} %get-tuple-element.62), channel_id=1, source_target_pairs={{0,1},{1,0},{2,3},{3,2},{4,5},{5,4},{6,7},{7,6},{8,9},{9,8},{10,11... | collective-permute-start | bytes 1671176 | tf_op jit(solution)/shard_map/ppermute | solution.py:425
  144.5 39.6 %collective-permute-start.11 = (bf16[272,1024]{1,0:T(8,128)(2,1)S(1)}, bf16[272,1024]{1,0:T(8,128)(2,1)S(1)}, u32[]{:S(2)}, u32[]{:S(2)}) collective-permute-start(bf16[272,1024]{1,0:T(8,128)(2,1)S(1)} %get-tuple-element.67), channel_id=1, source_target_pairs={{0,2},{2,0},{4,6},{6,4},{8,10},{10,8},{12,14},{14,12},{16,18},{18,... | collective-permute-start | bytes 1671176 | tf_op jit(solution)/shard_map/ppermute | solution.py:422
  145.4 2.1 %collective-permute-start.12 = (bf16[1024,256]{1,0:T(8,128)(2,1)S(1)}, bf16[1024,256]{1,0:T(8,128)(2,1)S(1)}, u32[]{:S(2)}, u32[]{:S(2)}) collective-permute-start(bf16[1024,256]{1,0:T(8,128)(2,1)S(1)} %get-tuple-element.69), channel_id=1, source_target_pairs={{0,1},{1,0},{2,3},{3,2},{4,5},{5,4},{6,7},{7,6},{8,9},{9,8},{10,11... | collective-permute-start | bytes 1572872 | tf_op jit(solution)/shard_map/ppermute | solution.py:425
  146.0 38.1 %collective-permute-start.13 = (bf16[1024,256]{1,0:T(8,128)(2,1)S(1)}, bf16[1024,256]{1,0:T(8,128)(2,1)S(1)}, u32[]{:S(2)}, u32[]{:S(2)}) collective-permute-start(bf16[1024,256]{1,0:T(8,128)(2,1)S(1)} %get-tuple-element.70), channel_id=1, source_target_pairs={{0,2},{2,0},{4,6},{6,4},{8,10},{10,8},{12,14},{14,12},{16,18},{18,... | collective-permute-start | bytes 1572872 | tf_op jit(solution)/shard_map/ppermute | solution.py:422
  184.1 2.2 %copy-start.1 = (bf16[512,512]{1,0:T(8,128)(2,1)S(1)}, bf16[512,512]{1,0:T(8,128)(2,1)}, u32[]{:S(2)}) copy-start(bf16[512,512]{1,0:T(8,128)(2,1)} %wo.1) | copy-start | bytes 1572868
  (10 other events, 11.8 us)

commit v4 on v3

--- a/solution.py
+++ b/solution.py
@@ -94,12 +94,12 @@
     for load in loads:
         load.start()
 
-    @pl.loop(0, NB)
-    def _(i):
+    for i in range(NB):
         cnt[i] = 0
 
-    @pl.loop(0, NB)
-    def _(b):
+    @pl.loop(0, NB // 8)
+    def _(step):
+      for b in [8 * step + u for u in range(8)]:
         r = ids[b]
         k = cnt[r]
         cnt[r] = k + 1
@@ -108,8 +108,9 @@
     send[:, :, 0:W] = jnp.zeros((CHIPS, 8, W), BF)
     low = low_rows((8, W))
 
-    @pl.loop(0, 16)
-    def _(i):
+    @pl.loop(0, 4)
+    def _(step):
+      for i in [4 * step + u for u in range(4)]:
         x = x_ref[pl.ds(pl.multiple_of(i * 16, 16), 16), :].astype(F32)
         c = c_ref[pl.ds(pl.multiple_of(i * 16, 16), 16), :].astype(F32)
         for h in range(2):
@@ -136,8 +137,9 @@
         ss[256 + 64 * j : 320 + 64 * j, :] = jnp.where(left, a[:64], a[64:])
     low2 = low_rows((8, 128))
 
-    @pl.loop(0, 64)
-    def _(i):
+    @pl.loop(0, 16)
+    def _(step):
+      for i in [4 * step + u for u in range(4)]:
         v = ss[pl.ds(pl.multiple_of(i * 8, 8), 8), :]
         hi = v.astype(BF).astype(F32)
         lo = v - hi
@@ -218,8 +220,9 @@
     for load in loads:
         load.start()
 
-    @pl.loop(0, 32)
-    def _(i):
+    @pl.loop(0, 8)
+    def _(step):
+      for i in [4 * step + u for u in range(4)]:
         xs, cs = [], []
         for h in range(2):
             a = recv[4 * i + 2 * h].astype(F32)
@@ -235,9 +238,8 @@
     loads[0].wait()
     loads[1].wait()
 
-    @pl.loop(0, 4)
-    def _(i):
-        cols = pl.ds(pl.multiple_of(i * 256, 256), 256)
+    for i in range(4):
+        cols = slice(i * 256, i * 256 + 256)
         pre = mm(x_s[...], wi[:, cols]) + b_ref[:, cols]
         gh = mm_t(c_s[...], wo[cols, :])
         act(pre, gh, cols, hid, gpre)
@@ -247,9 +249,8 @@
     for load in loads[2:]:
         load.wait()
 
-    @pl.loop(0, 4)
-    def _(i):
-        cols = pl.ds(pl.multiple_of(i * 256, 256), 256)
+    for i in range(4):
+        cols = slice(i * 256, i * 256 + 256)
         pre = mm(x_s[:, mine], wiy[:, cols]) + mm(x_s[:, other], win[:, cols]) + bp_ref[:, cols]
         gh = mm_t(c_s[:, mine], woy[cols, :]) + mm_t(c_s[:, other], won[cols, :])
         act(pre, gh, cols, hid_p, gpre_p)
@@ -262,8 +263,9 @@
         o_s[:, part] = mm(hid[...], wo[:, part]) + mm(hid_p[...], yr[...])
         k_s[:, part] = mm_t(gpre[...], wi[part, :]) + mm_t(gpre_p[...], kr[...])
 
-    @pl.loop(0, 64)
-    def _(i):
+    @pl.loop(0, 16)
+    def _(step):
+      for i in [4 * step + u for u in range(4)]:
         rows = pl.ds(pl.multiple_of(i * 8, 8), 8)
         o, k = o_s[rows, :], k_s[rows, :]
         send[2 * i, :, :] = jnp.where(low, o, pltpu.roll(k, 4, 0)).astype(BF)
@@ -496,7 +498,9 @@
     )
     near = beside(away)
     base_o, base_k = run(base_kernel, 1, [far((PTS, W), F32), far((PTS, W), F32)], (x, c, mixed, gq, wq, wo_att))
-    away_i, away_o = run(merge_kernel, 1, [sds((272, HALF), BF), sds((HALF, 256), BF)], (keep_i, got_i, keep_o, got_o))
+    away_i, away_o = run(
+        merge_kernel, 1, [sds((272, HALF), BF), sds((HALF, 256), BF)], (in_hbm(keep_i), got_i, in_hbm(keep_o), got_o)
+    )
     far_i, far_o = across(away_i), across(away_o)
     (joined,) = run(join_kernel, 2, [far((CHIPS, 8, 896), BF)], (ret, keep, near), [pltpu.VMEM((24 * CHIPS, 128), F32)])
     back = deal(joined)

time: 191 us -> 190 us (level)
    unnamed x34 -> x30, local copies, waits for them, and re-layouts: 8.83 us -> 8.81 us
where the time goes in v4:
time: 190 us; the launch traced here: 189 us
  waiting for transfers between devices  90.6 us (48%)
  starting transfers between devices  49.2 us (26%)
  Pallas kernels  39.2 us (21%)
  local copies, waits for them, and re-layouts  8.81 us (5%)
    all_to_all x3, waiting for transfers between devices, deal(): return lax.all_to_all(v, 'wide', split_axis=0, concat_axis=0, tiled=True)  44.4 us
    ppermute x5, waiting for transfers between devices, across(): return lax.ppermute(v, 'wide', pair)  44.1 us
    pallas_call x14, Pallas kernels, run(): call(body, outs, scratch, smem_in=smem_in, n_in=len(args), smem_out=smem_...  39.2 us
    all_to_all x3, starting transfers between devices, deal(): return lax.all_to_all(v, 'wide', split_axis=0, concat_axis=0, tiled=True)  36.8 us
    ppermute x9, starting transfers between devices, beside(): return lax.ppermute(v, 'narrow', swap)  8.92 us
    unnamed x30, local copies, waits for them, and re-layouts  8.81 us
  transfers between devices with their start and end apart: 17, of which 6 were waited for; matrix products, arithmetic and copies ran while one was open for 0% of the time, Pallas kernels for 15%

profile of v4, /device:TPU:1, one launch (start us, length us, event | category | flops | bytes accessed | tf_op | source)
XLA Modules:
  0.0 188.8 jit_solution(2042913873024033231)
XLA Ops:
  0.6 6.5 %shard_map.127 = (bf16[128,8,640]{2,1,0:T(8,128)(2,1)}, s32[64]{0:T(128)S(1)}, bf16[256,1536]{1,0:T(8,128)(2,1)}, bf16[256,512]{1,0:T(8,128)(2,1)}) custom-call(s32[64]{0:T(128)} %ids.1, bf16[256,512]{1,0:T(8,128)(2,1)} %x.1, bf16[256,512]{1,0:T(8,128)(2,1)} %c.1, bf16[512,1536]{1,0:T(8,128)(2,1)} %wq.1, bf16[512,512]{1,0:T(8,128)(2,1)} %wo.1), custom_call_target="tpu_custom_call" | custom-call | flops 5000000000 | bytes 5000000 | tf_op jit(solution)/shard_map/pallas_call | solution.py:433
  7.2 16.5 %all-to-all-start = ((bf16[128,8,640]{2,1,0:T(8,128)(2,1)}), bf16[128,8,640]{2,1,0:T(8,128)(2,1)S(1)}, u32[]{:S(2)}, u32[]{:S(2)}) async-start(bf16[128,8,640]{2,1,0:T(8,128)(2,1)} %get-tuple-element.41), calls=%async_computation | async-start | bytes 2621440 | tf_op jit(solution)/shard_map/all_to_all | solution.py:430
  23.8 1.3 shard_map.131
  26.1 1.2 collective-permute-done.5.near
  27.4 30.4 %all-to-all-done.recv = bf16[128,8,640]{2,1,0:T(8,128)(2,1)S(1)} async-done(((bf16[128,8,640]{2,1,0:T(8,128)(2,1)}), bf16[128,8,640]{2,1,0:T(8,128)(2,1)S(1)}, u32[]{:S(2)}, u32[]{:S(2)}) %all-to-all-start) | async-done | bytes 1310752 | tf_op jit(solution)/shard_map/all_to_all | solution.py:430
  58.8 8.2 %all-to-all-start.1 = ((bf16[128,8,256]{2,1,0:T(8,128)(2,1)}), bf16[128,8,256]{2,1,0:T(8,128)(2,1)S(1)}, u32[]{:S(2)}, u32[]{:S(2)}) async-start(bf16[128,8,256]{2,1,0:T(8,128)(2,1)} %shard_map.133), calls=%async_computation.1 | async-start | bytes 1048576 | tf_op jit(solution)/shard_map/all_to_all | solution.py:430
  70.8 14.0 %all-to-all-done.1.rs = bf16[128,8,256]{2,1,0:T(8,128)(2,1)S(1)} async-done(((bf16[128,8,256]{2,1,0:T(8,128)(2,1)}), bf16[128,8,256]{2,1,0:T(8,128)(2,1)S(1)}, u32[]{:S(2)}, u32[]{:S(2)}) %all-to-all-start.1) | async-done | bytes 524320 | tf_op jit(solution)/shard_map/all_to_all | solution.py:430
  84.8 3.8 %collective-permute-start.6 = (bf16[128,8,256]{2,1,0:T(8,128)(2,1)S(1)}, bf16[128,8,256]{2,1,0:T(8,128)(2,1)S(1)}, u32[]{:S(2)}, u32[]{:S(2)}) collective-permute-start(bf16[128,8,256]{2,1,0:T(8,128)(2,1)S(1)} %all-to-all-done.1.rs), channel_id=1, source_target_pairs={{0,1},{1,0},{2,3},{3,2},{4,5},{5,4},{6,7},{7,6},{8,9},{9,8},{10,11... | collective-permute-start | bytes 1572872 | tf_op jit(solution)/shard_map/ppermute | solution.py:427
  89.2 8.0 %collective-permute-done.2.woy_h = bf16[1024,256]{1,0:T(8,128)(2,1)} collective-permute-done((bf16[1024,256]{1,0:T(8,128)(2,1)S(1)}, bf16[1024,256]{1,0:T(8,128)(2,1)}, u32[]{:S(2)}, u32[]{:S(2)}) %collective-permute-start.2) | collective-permute-done | bytes 524320 | tf_op jit(solution)/shard_map/ppermute | solution.py:424
  97.2 1.8 collective-permute-start.3
  100.0 1.1 copy-done.10
  101.1 4.9 %shard_map.134 = (bf16[256,512]{1,0:T(8,128)(2,1)S(1)}, bf16[256,1536]{1,0:T(8,128)(2,1)S(1)}, f32[256,1536]{1,0:T(8,128)S(1)}, bf16[256,1536]{1,0:T(8,128)(2,1)S(1)}, f32[8,128]{1,0:T(8,128)S(1)}) custom-call(s32[4]{0:T(128)S(1)} %pad_add_fusion.pos, bf16[128,8,256]{2,1,0:T(8,128)(2,1)S(1)} %all-to-all-done.1.rs, ...), custom_call_target="tpu_custom_call" | custom-call | flops 7000000000 | bytes 7000000 | tf_op jit(solution)/shard_map/pallas_call | solution.py:433
  107.1 11.6 %shard_map.130 = (bf16[128,8,512]{2,1,0:T(8,128)(2,1)}, bf16[512,512]{1,0:T(8,128)(2,1)}, bf16[512,512]{1,0:T(8,128)(2,1)}, bf16[512,1024]{1,0:T(8,128)(2,1)}, b...) custom-call(s32[4]{0:T(128)S(1)} %pad_add_fusion.pos, ...), custom_call_target="tpu_custom_call" | custom-call | flops 12000000000 | bytes 12000000 | tf_op jit(solution)/shard_map/pallas_call | solution.py:433
  118.8 1.2 copy-done.5
  120.0 1.8 shard_map.135
  121.9 12.2 %all-to-all-start.2 = ((bf16[128,8,896]{2,1,0:T(8,128)(2,1)}), bf16[128,8,896]{2,1,0:T(8,128)(2,1)S(1)}, u32[]{:S(2)}, u32[]{:S(2)}) async-start(bf16[128,8,896]{2,1,0:T(8,128)(2,1)} %shard_map.135), calls=%async_computation.2 | async-start | bytes 3670016 | tf_op jit(solution)/shard_map/all_to_all | solution.py:430
  135.0 1.2 copy-done.8
  136.2 1.2 copy-done.9
  139.5 2.0 %shard_map.138 = (f32[272,1024]{1,0:T(8,128)S(1)}, bf16[272,1024]{1,0:T(8,128)(2,1)S(1)}, f32[1024,256]{1,0:T(8,128)S(1)}, bf16[1024,256]{1,0:T(8,128)(2,1)S(1)}) custom-call(s32[4]{0:T(128)S(1)} %pad_add_fusion.pos, bf16[512,512]{1,0:T(8,128)(2,1)S(1)} %copy-done.11, bf16[512,512]{1,0:T(8,128)(2,1)S(1)} %copy-done.12, bf16[512,1024]{1,0:T(8,128)(2,1)S(1)} %copy-done.8, ...), custom_call_target="tpu_custom_call" | custom-call | flops 5000000000 | bytes 5000000 | tf_op jit(solution)/shard_map/pallas_call | solution.py:433
  142.1 1.8 shard_map.139
  146.7 36.0 %collective-permute-done.13.far_o = bf16[1024,256]{1,0:T(8,128)(2,1)S(1)} collective-permute-done((bf16[1024,256]{1,0:T(8,128)(2,1)S(1)}, bf16[1024,256]{1,0:T(8,128)(2,1)S(1)}, u32[]{:S(2)}, u32[]{:S(2)}) %collective-permute-start.13) | collective-permute-done | bytes 524320 | tf_op jit(solution)/shard_map/ppermute | solution.py:424
  182.8 2.2 %shard_map.140 = (f32[256,1024]{1,0:T(8,128)}, f32[1,512]{1,0:T(1,128)}, f32[1024,256]{1,0:T(8,128)}) custom-call(s32[4]{0:T(128)S(1)} %pad_add_fusion.pos, f32[272,1024]{1,0:T(8,128)S(1)} %get-tuple-element.61.keep_i, bf16[272,1024]{1,0:T(8,128)(2,1)S(1)} %collective-permute-done.8.got_i, bf16[272,1024]{1,0:T(8,128)(2,1)S(1)} %collective-permute-done.11.far_i, ...), custom_call_target="tpu_custom_call" | custom-call | flops 3000000000 | bytes 3000000 | tf_op jit(solution)/shard_map/pallas_call | solution.py:433
  184.9 1.5 shard_map.136
  186.5 2.3 %shard_map.137 = (bf16[256,512]{1,0:T(8,128)(2,1)}, bf16[256,512]{1,0:T(8,128)(2,1)}, f32[2,2048]{1,0:T(2,128)}) custom-call(s32[64]{0:T(128)S(1)} %get-tuple-element.40.slots, bf16[128,8,896]{2,1,0:T(8,128)(2,1)S(1)} %all-to-all-done.2.ret, f32[256,512]{1,0:T(8,128)} %get-tuple-element.51.base_o, f32[256,512]{1,0:T(8,128)} %get-tuple-element.52.base_k, ...), custom_call_target="tpu_custom_call" | custom-call | flops 3000000000 | bytes 3000000 | tf_op jit(solution)/shard_map/pallas_call | solution.py:433
  (55 shorter events, 15.0 us)
Async XLA Ops:
  7.1 16.6 %copy-start.2 = (bf16[256,512]{1,0:T(8,128)(2,1)S(1)}, bf16[256,512]{1,0:T(8,128)(2,1)}, u32[]{:S(2)}) copy-start(bf16[256,512]{1,0:T(8,128)(2,1)} %x.1) | copy-start | bytes 786436
  7.2 16.6 %copy-start.6 = (bf16[256,512]{1,0:T(8,128)(2,1)S(1)}, bf16[256,512]{1,0:T(8,128)(2,1)}, u32[]{:S(2)}) copy-start(bf16[256,512]{1,0:T(8,128)(2,1)} %get-tuple-element.43.g_ref) | copy-start | bytes 786436
  7.2 50.6 %all-to-all-start = ((bf16[128,8,640]{2,1,0:T(8,128)(2,1)}), bf16[128,8,640]{2,1,0:T(8,128)(2,1)S(1)}, u32[]{:S(2)}, u32[]{:S(2)}) async-start(bf16[128,8,640]{2,1,0:T(8,128)(2,1)} %get-tuple-element.41), calls=%async_computation | async-start | bytes 2621440 | tf_op jit(solution)/shard_map/all_to_all | solution.py:430
  25.0 2.2 %collective-permute-start.5 = (bf16[256,512]{1,0:T(8,128)(2,1)S(1)}, bf16[256,512]{1,0:T(8,128)(2,1)S(1)}, u32[]{:S(2)}, u32[]{:S(2)}) collective-permute-start(bf16[256,512]{1,0:T(8,128)(2,1)S(1)} %get-tuple-element.45), channel_id=1, source_target_pairs={{0,1},{1,0},{2,3},{3,2},{4,5},{5,4},{6,7},{7,6},{8,9},{9,8},{10,11... | collective-permute-start | bytes 786440 | tf_op jit(solution)/shard_map/ppermute | solution.py:427
  58.8 26.0 %all-to-all-start.1 = ((bf16[128,8,256]{2,1,0:T(8,128)(2,1)}), bf16[128,8,256]{2,1,0:T(8,128)(2,1)S(1)}, u32[]{:S(2)}, u32[]{:S(2)}) async-start(bf16[128,8,256]{2,1,0:T(8,128)(2,1)} %shard_map.133), calls=%async_computation.1 | async-start | bytes 1048576 | tf_op jit(solution)/shard_map/all_to_all | solution.py:430
  68.0 20.6 %copy-start.4 = (f32[1024]{0:T(1024)S(1)}, f32[1024]{0:T(1024)}, u32[]{:S(2)}) copy-start(f32[1024]{0:T(1024)} %param.13) | copy-start | bytes 12292
  68.1 31.0 %copy-start.3 = (bf16[256,512]{1,0:T(8,128)(2,1)S(1)}, bf16[256,512]{1,0:T(8,128)(2,1)}, u32[]{:S(2)}) copy-start(bf16[256,512]{1,0:T(8,128)(2,1)} %c.1) | copy-start | bytes 786436
  68.1 20.8 %collective-permute-start = (bf16[256,1024]{1,0:T(8,128)(2,1)S(1)}, bf16[256,1024]{1,0:T(8,128)(2,1)}, u32[]{:S(2)}, u32[]{:S(2)}) collective-permute-start(bf16[256,1024]{1,0:T(8,128)(2,1)S(1)} %shard_map.128), channel_id=1, source_target_pairs={{0,2},{2,0},{4,6},{6,4},{8,10},{10,8},{12,14},{14,12},{16,18},{18,... | collective-permute-start | bytes 1572872 | tf_op jit(solution)/shard_map/ppermute | solution.py:424
  69.8 27.4 %collective-permute-start.2 = (bf16[1024,256]{1,0:T(8,128)(2,1)S(1)}, bf16[1024,256]{1,0:T(8,128)(2,1)}, u32[]{:S(2)}, u32[]{:S(2)}) collective-permute-start(bf16[1024,256]{1,0:T(8,128)(2,1)S(1)} %shard_map.129), channel_id=1, source_target_pairs={{0,2},{2,0},{4,6},{6,4},{8,10},{10,8},{12,14},{14,12},{16,18},{18,... | collective-permute-start | bytes 1572872 | tf_op jit(solution)/shard_map/ppermute | solution.py:424
  84.8 14.3 %collective-permute-start.6 = (bf16[128,8,256]{2,1,0:T(8,128)(2,1)S(1)}, bf16[128,8,256]{2,1,0:T(8,128)(2,1)S(1)}, u32[]{:S(2)}, u32[]{:S(2)}) collective-permute-start(bf16[128,8,256]{2,1,0:T(8,128)(2,1)S(1)} %all-to-all-done.1.rs), channel_id=1, source_target_pairs={{0,1},{1,0},{2,3},{3,2},{4,5},{5,4},{6,7},{7,6},{8,9},{9,8},{10,11... | collective-permute-start | bytes 1572872 | tf_op jit(solution)/shard_map/ppermute | solution.py:427
  88.6 17.5 %collective-permute-start.4 = (f32[1024]{0:T(1024)S(1)}, f32[1024]{0:T(1024)S(1)}, u32[]{:S(2)}, u32[]{:S(2)}) collective-permute-start(f32[1024]{0:T(1024)S(1)} %copy-done.4), channel_id=1, source_target_pairs={{0,2},{2,0},{4,6},{6,4},{8,10},{10,8},{12,14},{14,12},{16,18},{18,... | collective-permute-start | bytes 12296 | tf_op jit(solution)/shard_map/ppermute | solution.py:424
  88.9 17.2 %collective-permute-start.1 = (bf16[256,1024]{1,0:T(8,128)(2,1)}, bf16[256,1024]{1,0:T(8,128)(2,1)S(1)}, u32[]{:S(2)}, u32[]{:S(2)}) collective-permute-start(bf16[256,1024]{1,0:T(8,128)(2,1)} %collective-permute-done.wiy_h), channel_id=1, source_target_pairs={{0,1},{1,0},{2,3},{3,2},{4,5},{5,4},{6,7},{7,6},{8,9},{9,8},{10,11... | collective-permute-start | bytes 1572872 | tf_op jit(solution)/shard_map/ppermute | solution.py:427
  97.2 9.0 %collective-permute-start.3 = (bf16[1024,256]{1,0:T(8,128)(2,1)}, bf16[1024,256]{1,0:T(8,128)(2,1)S(1)}, u32[]{:S(2)}, u32[]{:S(2)}) collective-permute-start(bf16[1024,256]{1,0:T(8,128)(2,1)} %collective-permute-done.2.woy_h), channel_id=1, source_target_pairs={{0,1},{1,0},{2,3},{3,2},{4,5},{5,4},{6,7},{7,6},{8,9},{9,8},{10,11... | collective-permute-start | bytes 1572872 | tf_op jit(solution)/shard_map/ppermute | solution.py:427
  106.0 12.8 %collective-permute-start.7 = (bf16[256,1536]{1,0:T(8,128)(2,1)S(1)}, bf16[256,1536]{1,0:T(8,128)(2,1)S(1)}, u32[]{:S(2)}, u32[]{:S(2)}) collective-permute-start(bf16[256,1536]{1,0:T(8,128)(2,1)S(1)} %get-tuple-element.48), channel_id=1, source_target_pairs={{0,1},{1,0},{2,3},{3,2},{4,5},{5,4},{6,7},{7,6},{8,9},{9,8},{10,11... | collective-permute-start | bytes 2359304 | tf_op jit(solution)/shard_map/ppermute | solution.py:427
  118.8 1.2 copy-start.5
  121.9 64.6 %all-to-all-start.2 = ((bf16[128,8,896]{2,1,0:T(8,128)(2,1)}), bf16[128,8,896]{2,1,0:T(8,128)(2,1)S(1)}, u32[]{:S(2)}, u32[]{:S(2)}) async-start(bf16[128,8,896]{2,1,0:T(8,128)(2,1)} %shard_map.135), calls=%async_computation.2 | async-start | bytes 3670016 | tf_op jit(solution)/shard_map/all_to_all | solution.py:430
  134.0 8.1 %collective-permute-start.9 = (bf16[272,1024]{1,0:T(8,128)(2,1)}, bf16[272,1024]{1,0:T(8,128)(2,1)S(1)}, u32[]{:S(2)}, u32[]{:S(2)}) collective-permute-start(bf16[272,1024]{1,0:T(8,128)(2,1)} %get-tuple-element.64), channel_id=1, source_target_pairs={{0,1},{1,0},{2,3},{3,2},{4,5},{5,4},{6,7},{7,6},{8,9},{9,8},{10,11... | collective-permute-start | bytes 1671176 | tf_op jit(solution)/shard_map/ppermute | solution.py:427
  134.9 7.2 %collective-permute-start.10 = (bf16[1024,256]{1,0:T(8,128)(2,1)}, bf16[1024,256]{1,0:T(8,128)(2,1)S(1)}, u32[]{:S(2)}, u32[]{:S(2)}) collective-permute-start(bf16[1024,256]{1,0:T(8,128)(2,1)} %get-tuple-element.66), channel_id=1, source_target_pairs={{0,1},{1,0},{2,3},{3,2},{4,5},{5,4},{6,7},{7,6},{8,9},{9,8},{10,11... | collective-permute-start | bytes 1572872 | tf_op jit(solution)/shard_map/ppermute | solution.py:427
  141.6 5.1 %collective-permute-start.8 = (bf16[272,1024]{1,0:T(8,128)(2,1)S(1)}, bf16[272,1024]{1,0:T(8,128)(2,1)S(1)}, u32[]{:S(2)}, u32[]{:S(2)}) collective-permute-start(bf16[272,1024]{1,0:T(8,128)(2,1)S(1)} %get-tuple-element.62), channel_id=1, source_target_pairs={{0,1},{1,0},{2,3},{3,2},{4,5},{5,4},{6,7},{7,6},{8,9},{9,8},{10,11... | collective-permute-start | bytes 1671176 | tf_op jit(solution)/shard_map/ppermute | solution.py:427
  143.9 38.9 %collective-permute-start.11 = (bf16[272,1024]{1,0:T(8,128)(2,1)S(1)}, bf16[272,1024]{1,0:T(8,128)(2,1)S(1)}, u32[]{:S(2)}, u32[]{:S(2)}) collective-permute-start(bf16[272,1024]{1,0:T(8,128)(2,1)S(1)} %get-tuple-element.67), channel_id=1, source_target_pairs={{0,2},{2,0},{4,6},{6,4},{8,10},{10,8},{12,14},{14,12},{16,18},{18,... | collective-permute-start | bytes 1671176 | tf_op jit(solution)/shard_map/ppermute | solution.py:424
  144.8 1.9 %collective-permute-start.12 = (bf16[1024,256]{1,0:T(8,128)(2,1)S(1)}, bf16[1024,256]{1,0:T(8,128)(2,1)S(1)}, u32[]{:S(2)}, u32[]{:S(2)}) collective-permute-start(bf16[1024,256]{1,0:T(8,128)(2,1)S(1)} %get-tuple-element.69), channel_id=1, source_target_pairs={{0,1},{1,0},{2,3},{3,2},{4,5},{5,4},{6,7},{7,6},{8,9},{9,8},{10,11... | collective-permute-start | bytes 1572872 | tf_op jit(solution)/shard_map/ppermute | solution.py:427
  145.2 37.6 %collective-permute-start.13 = (bf16[1024,256]{1,0:T(8,128)(2,1)S(1)}, bf16[1024,256]{1,0:T(8,128)(2,1)S(1)}, u32[]{:S(2)}, u32[]{:S(2)}) collective-permute-start(bf16[1024,256]{1,0:T(8,128)(2,1)S(1)} %get-tuple-element.70), channel_id=1, source_target_pairs={{0,2},{2,0},{4,6},{6,4},{8,10},{10,8},{12,14},{14,12},{16,18},{18,... | collective-permute-start | bytes 1572872 | tf_op jit(solution)/shard_map/ppermute | solution.py:424
  182.8 2.2 %copy-start = (bf16[512,1536]{1,0:T(8,128)(2,1)S(1)}, bf16[512,1536]{1,0:T(8,128)(2,1)}, u32[]{:S(2)}) copy-start(bf16[512,1536]{1,0:T(8,128)(2,1)} %wq.1) | copy-start | bytes 4718596
  182.8 2.2 %copy-start.1 = (bf16[512,512]{1,0:T(8,128)(2,1)S(1)}, bf16[512,512]{1,0:T(8,128)(2,1)}, u32[]{:S(2)}) copy-start(bf16[512,512]{1,0:T(8,128)(2,1)} %wo.1) | copy-start | bytes 1572868
  (8 other events, 8.4 us)

commit v5 on v4

--- a/solution.py
+++ b/solution.py
@@ -298,9 +298,8 @@
     grad_part(pos[3], x_s, c_s, hid, gpre, keep_i, send_i, keep_o, send_o)
 
 
-def merge_kernel(keep_i, got_i, keep_o, got_o, away_i, away_o):
-    away_i[...] = (keep_i[...] + got_i[...].astype(F32)).astype(BF)
-    away_o[...] = (keep_o[...] + got_o[...].astype(F32)).astype(BF)
+def merge_kernel(keep, got, away):
+    away[...] = (keep[...] + got[...].astype(F32)).astype(BF)
 
 
 def end_kernel(pos, keep_i, got_i, far_i, keep_o, got_o, far_o, grad_i, bias, grad_o, row):
@@ -498,9 +497,8 @@
     )
     near = beside(away)
     base_o, base_k = run(base_kernel, 1, [far((PTS, W), F32), far((PTS, W), F32)], (x, c, mixed, gq, wq, wo_att))
-    away_i, away_o = run(
-        merge_kernel, 1, [sds((272, HALF), BF), sds((HALF, 256), BF)], (in_hbm(keep_i), got_i, in_hbm(keep_o), got_o)
-    )
+    (away_i,) = run(merge_kernel, 1, [sds((272, HALF), BF)], (in_hbm(keep_i), got_i))
+    (away_o,) = run(merge_kernel, 1, [sds((HALF, 256), BF)], (in_hbm(keep_o), got_o))
     far_i, far_o = across(away_i), across(away_o)
     (joined,) = run(join_kernel, 2, [far((CHIPS, 8, 896), BF)], (ret, keep, near), [pltpu.VMEM((24 * CHIPS, 128), F32)])
     back = deal(joined)

time: 190 us -> 189 us (level)
    pallas_call x14 -> x15, Pallas kernels: 39.2 us -> 40.1 us  [run(): call(body, outs, scratch, smem_in=smem_in, n_in=len(args), smem_out=smem_...]
  transfers between devices with their start and end apart: 17 -> 17, of which waited for: 6 -> 5; matrix products, arithmetic and copies ran while one was open for 0% -> 0% of each run, Pallas kernels for 15% -> 15%
where the time goes in v5:
time: 189 us; the launch traced here: 188 us
  waiting for transfers between devices  89.4 us (47%)
  starting transfers between devices  49 us (26%)
  Pallas kernels  40.1 us (21%)
  local copies, waits for them, and re-layouts  8.82 us (5%)
    all_to_all x3, waiting for transfers between devices, deal(): return lax.all_to_all(v, 'wide', split_axis=0, concat_axis=0, tiled=True)  44.4 us
    ppermute x5, waiting for transfers between devices, across(): return lax.ppermute(v, 'wide', pair)  43.8 us
    pallas_call x15, Pallas kernels, run(): call(body, outs, scratch, smem_in=smem_in, n_in=len(args), smem_out=smem_...  40.1 us
    all_to_all x3, starting transfers between devices, deal(): return lax.all_to_all(v, 'wide', split_axis=0, concat_axis=0, tiled=True)  36.8 us
    unnamed x30, local copies, waits for them, and re-layouts  8.82 us
    ppermute x9, starting transfers between devices, beside(): return lax.ppermute(v, 'narrow', swap)  8.65 us
  transfers between devices with their start and end apart: 17, of which 5 were waited for; matrix products, arithmetic and copies ran while one was open for 0% of the time, Pallas kernels for 15%

profile of v5, /device:TPU:1, one launch (start us, length us, event | category | flops | bytes accessed | tf_op | source)
XLA Modules:
  0.0 188.3 jit_solution(3673997872185953)
XLA Ops:
  0.6 6.5 %shard_map.127 = (bf16[128,8,640]{2,1,0:T(8,128)(2,1)}, s32[64]{0:T(128)S(1)}, bf16[256,1536]{1,0:T(8,128)(2,1)}, bf16[256,512]{1,0:T(8,128)(2,1)}) custom-call(s32[64]{0:T(128)} %ids.1, bf16[256,512]{1,0:T(8,128)(2,1)} %x.1, bf16[256,512]{1,0:T(8,128)(2,1)} %c.1, bf16[512,1536]{1,0:T(8,128)(2,1)} %wq.1, bf16[512,512]{1,0:T(8,128)(2,1)} %wo.1), custom_call_target="tpu_custom_call" | custom-call | flops 5000000000 | bytes 5000000 | tf_op jit(solution)/shard_map/pallas_call | solution.py:432
  7.2 16.5 %all-to-all-start = ((bf16[128,8,640]{2,1,0:T(8,128)(2,1)}), bf16[128,8,640]{2,1,0:T(8,128)(2,1)S(1)}, u32[]{:S(2)}, u32[]{:S(2)}) async-start(bf16[128,8,640]{2,1,0:T(8,128)(2,1)} %get-tuple-element.39), calls=%async_computation | async-start | bytes 2621440 | tf_op jit(solution)/shard_map/all_to_all | solution.py:429
  23.8 1.3 shard_map.131
  26.1 1.2 collective-permute-done.5.near
  27.4 30.4 %all-to-all-done.recv = bf16[128,8,640]{2,1,0:T(8,128)(2,1)S(1)} async-done(((bf16[128,8,640]{2,1,0:T(8,128)(2,1)}), bf16[128,8,640]{2,1,0:T(8,128)(2,1)S(1)}, u32[]{:S(2)}, u32[]{:S(2)}) %all-to-all-start) | async-done | bytes 1310752 | tf_op jit(solution)/shard_map/all_to_all | solution.py:429
  58.8 8.2 %all-to-all-start.1 = ((bf16[128,8,256]{2,1,0:T(8,128)(2,1)}), bf16[128,8,256]{2,1,0:T(8,128)(2,1)S(1)}, u32[]{:S(2)}, u32[]{:S(2)}) async-start(bf16[128,8,256]{2,1,0:T(8,128)(2,1)} %shard_map.133), calls=%async_computation.1 | async-start | bytes 1048576 | tf_op jit(solution)/shard_map/all_to_all | solution.py:429
  70.8 14.0 %all-to-all-done.1.rs = bf16[128,8,256]{2,1,0:T(8,128)(2,1)S(1)} async-done(((bf16[128,8,256]{2,1,0:T(8,128)(2,1)}), bf16[128,8,256]{2,1,0:T(8,128)(2,1)S(1)}, u32[]{:S(2)}, u32[]{:S(2)}) %all-to-all-start.1) | async-done | bytes 524320 | tf_op jit(solution)/shard_map/all_to_all | solution.py:429
  84.8 3.8 %collective-permute-start.6 = (bf16[128,8,256]{2,1,0:T(8,128)(2,1)S(1)}, bf16[128,8,256]{2,1,0:T(8,128)(2,1)S(1)}, u32[]{:S(2)}, u32[]{:S(2)}) collective-permute-start(bf16[128,8,256]{2,1,0:T(8,128)(2,1)S(1)} %all-to-all-done.1.rs), channel_id=1, source_target_pairs={{0,1},{1,0},{2,3},{3,2},{4,5},{5,4},{6,7},{7,6},{8,9},{9,8},{10,11... | collective-permute-start | bytes 1572872 | tf_op jit(solution)/shard_map/ppermute | solution.py:426
  89.2 8.0 %collective-permute-done.2.woy_h = bf16[1024,256]{1,0:T(8,128)(2,1)} collective-permute-done((bf16[1024,256]{1,0:T(8,128)(2,1)S(1)}, bf16[1024,256]{1,0:T(8,128)(2,1)}, u32[]{:S(2)}, u32[]{:S(2)}) %collective-permute-start.2) | collective-permute-done | bytes 524320 | tf_op jit(solution)/shard_map/ppermute | solution.py:423
  97.2 1.8 collective-permute-start.3
  101.2 4.9 %shard_map.134 = (bf16[256,512]{1,0:T(8,128)(2,1)S(1)}, bf16[256,1536]{1,0:T(8,128)(2,1)S(1)}, f32[256,1536]{1,0:T(8,128)S(1)}, bf16[256,1536]{1,0:T(8,128)(2,1)S(1)}, f32[8,128]{1,0:T(8,128)S(1)}) custom-call(s32[4]{0:T(128)S(1)} %pad_add_fusion.pos, bf16[128,8,256]{2,1,0:T(8,128)(2,1)S(1)} %all-to-all-done.1.rs, ...), custom_call_target="tpu_custom_call" | custom-call | flops 7000000000 | bytes 7000000 | tf_op jit(solution)/shard_map/pallas_call | solution.py:432
  107.2 11.6 %shard_map.130 = (bf16[128,8,512]{2,1,0:T(8,128)(2,1)}, bf16[512,512]{1,0:T(8,128)(2,1)}, bf16[512,512]{1,0:T(8,128)(2,1)}, bf16[512,1024]{1,0:T(8,128)(2,1)}, b...) custom-call(s32[4]{0:T(128)S(1)} %pad_add_fusion.pos, ...), custom_call_target="tpu_custom_call" | custom-call | flops 12000000000 | bytes 12000000 | tf_op jit(solution)/shard_map/pallas_call | solution.py:432
  118.8 1.2 copy-done.5
  120.0 1.8 shard_map.135
  121.9 12.1 %all-to-all-start.2 = ((bf16[128,8,896]{2,1,0:T(8,128)(2,1)}), bf16[128,8,896]{2,1,0:T(8,128)(2,1)S(1)}, u32[]{:S(2)}, u32[]{:S(2)}) async-start(bf16[128,8,896]{2,1,0:T(8,128)(2,1)} %shard_map.135), calls=%async_computation.2 | async-start | bytes 3670016 | tf_op jit(solution)/shard_map/all_to_all | solution.py:429
  135.0 1.2 copy-done.8
  136.2 1.2 copy-done.9
  139.5 2.1 %shard_map.138 = (f32[272,1024]{1,0:T(8,128)S(1)}, bf16[272,1024]{1,0:T(8,128)(2,1)S(1)}, f32[1024,256]{1,0:T(8,128)S(1)}, bf16[1024,256]{1,0:T(8,128)(2,1)S(1)}) custom-call(s32[4]{0:T(128)S(1)} %pad_add_fusion.pos, bf16[512,512]{1,0:T(8,128)(2,1)S(1)} %copy-done.11, bf16[512,512]{1,0:T(8,128)(2,1)S(1)} %copy-done.12, bf16[512,1024]{1,0:T(8,128)(2,1)S(1)} %copy-done.8, ...), custom_call_target="tpu_custom_call" | custom-call | flops 5000000000 | bytes 5000000 | tf_op jit(solution)/shard_map/pallas_call | solution.py:432
  142.2 1.4 shard_map.139
  144.5 1.3 shard_map.140
  146.5 35.8 %collective-permute-done.13.far_o = bf16[1024,256]{1,0:T(8,128)(2,1)S(1)} collective-permute-done((bf16[1024,256]{1,0:T(8,128)(2,1)S(1)}, bf16[1024,256]{1,0:T(8,128)(2,1)S(1)}, u32[]{:S(2)}, u32[]{:S(2)}) %collective-permute-start.13) | collective-permute-done | bytes 524320 | tf_op jit(solution)/shard_map/ppermute | solution.py:423
  182.3 2.2 %shard_map.141 = (f32[256,1024]{1,0:T(8,128)}, f32[1,512]{1,0:T(1,128)}, f32[1024,256]{1,0:T(8,128)}) custom-call(s32[4]{0:T(128)S(1)} %pad_add_fusion.pos, f32[272,1024]{1,0:T(8,128)S(1)} %get-tuple-element.59.keep_i, bf16[272,1024]{1,0:T(8,128)(2,1)S(1)} %collective-permute-done.8.got_i, bf16[272,1024]{1,0:T(8,128)(2,1)S(1)} %collective-permute-done.10.far_i, ...), custom_call_target="tpu_custom_call" | custom-call | flops 3000000000 | bytes 3000000 | tf_op jit(solution)/shard_map/pallas_call | solution.py:432
  184.5 1.5 shard_map.136
  186.0 2.3 %shard_map.137 = (bf16[256,512]{1,0:T(8,128)(2,1)}, bf16[256,512]{1,0:T(8,128)(2,1)}, f32[2,2048]{1,0:T(2,128)}) custom-call(s32[64]{0:T(128)S(1)} %get-tuple-element.38.slots, bf16[128,8,896]{2,1,0:T(8,128)(2,1)S(1)} %all-to-all-done.2.ret, f32[256,512]{1,0:T(8,128)} %get-tuple-element.49.base_o, f32[256,512]{1,0:T(8,128)} %get-tuple-element.50.base_k, ...), custom_call_target="tpu_custom_call" | custom-call | flops 3000000000 | bytes 3000000 | tf_op jit(solution)/shard_map/pallas_call | solution.py:432
  (56 shorter events, 15.1 us)
Async XLA Ops:
  7.1 16.6 %copy-start.2 = (bf16[256,512]{1,0:T(8,128)(2,1)S(1)}, bf16[256,512]{1,0:T(8,128)(2,1)}, u32[]{:S(2)}) copy-start(bf16[256,512]{1,0:T(8,128)(2,1)} %x.1) | copy-start | bytes 786436
  7.2 16.6 %copy-start.6 = (bf16[256,512]{1,0:T(8,128)(2,1)S(1)}, bf16[256,512]{1,0:T(8,128)(2,1)}, u32[]{:S(2)}) copy-start(bf16[256,512]{1,0:T(8,128)(2,1)} %get-tuple-element.41.g_ref) | copy-start | bytes 786436
  7.2 50.6 %all-to-all-start = ((bf16[128,8,640]{2,1,0:T(8,128)(2,1)}), bf16[128,8,640]{2,1,0:T(8,128)(2,1)S(1)}, u32[]{:S(2)}, u32[]{:S(2)}) async-start(bf16[128,8,640]{2,1,0:T(8,128)(2,1)} %get-tuple-element.39), calls=%async_computation | async-start | bytes 2621440 | tf_op jit(solution)/shard_map/all_to_all | solution.py:429
  25.0 2.2 %collective-permute-start.5 = (bf16[256,512]{1,0:T(8,128)(2,1)S(1)}, bf16[256,512]{1,0:T(8,128)(2,1)S(1)}, u32[]{:S(2)}, u32[]{:S(2)}) collective-permute-start(bf16[256,512]{1,0:T(8,128)(2,1)S(1)} %get-tuple-element.43), channel_id=1, source_target_pairs={{0,1},{1,0},{2,3},{3,2},{4,5},{5,4},{6,7},{7,6},{8,9},{9,8},{10,11... | collective-permute-start | bytes 786440 | tf_op jit(solution)/shard_map/ppermute | solution.py:426
  58.8 26.0 %all-to-all-start.1 = ((bf16[128,8,256]{2,1,0:T(8,128)(2,1)}), bf16[128,8,256]{2,1,0:T(8,128)(2,1)S(1)}, u32[]{:S(2)}, u32[]{:S(2)}) async-start(bf16[128,8,256]{2,1,0:T(8,128)(2,1)} %shard_map.133), calls=%async_computation.1 | async-start | bytes 1048576 | tf_op jit(solution)/shard_map/all_to_all | solution.py:429
  68.1 20.6 %copy-start.4 = (f32[1024]{0:T(1024)S(1)}, f32[1024]{0:T(1024)}, u32[]{:S(2)}) copy-start(f32[1024]{0:T(1024)} %param.13) | copy-start | bytes 12292
  68.1 31.0 %copy-start.3 = (bf16[256,512]{1,0:T(8,128)(2,1)S(1)}, bf16[256,512]{1,0:T(8,128)(2,1)}, u32[]{:S(2)}) copy-start(bf16[256,512]{1,0:T(8,128)(2,1)} %c.1) | copy-start | bytes 786436
  68.1 20.8 %collective-permute-start = (bf16[256,1024]{1,0:T(8,128)(2,1)S(1)}, bf16[256,1024]{1,0:T(8,128)(2,1)}, u32[]{:S(2)}, u32[]{:S(2)}) collective-permute-start(bf16[256,1024]{1,0:T(8,128)(2,1)S(1)} %shard_map.128), channel_id=1, source_target_pairs={{0,2},{2,0},{4,6},{6,4},{8,10},{10,8},{12,14},{14,12},{16,18},{18,... | collective-permute-start | bytes 1572872 | tf_op jit(solution)/shard_map/ppermute | solution.py:423
  69.8 27.4 %collective-permute-start.2 = (bf16[1024,256]{1,0:T(8,128)(2,1)S(1)}, bf16[1024,256]{1,0:T(8,128)(2,1)}, u32[]{:S(2)}, u32[]{:S(2)}) collective-permute-start(bf16[1024,256]{1,0:T(8,128)(2,1)S(1)} %shard_map.129), channel_id=1, source_target_pairs={{0,2},{2,0},{4,6},{6,4},{8,10},{10,8},{12,14},{14,12},{16,18},{18,... | collective-permute-start | bytes 1572872 | tf_op jit(solution)/shard_map/ppermute | solution.py:423
  84.8 14.3 %collective-permute-start.6 = (bf16[128,8,256]{2,1,0:T(8,128)(2,1)S(1)}, bf16[128,8,256]{2,1,0:T(8,128)(2,1)S(1)}, u32[]{:S(2)}, u32[]{:S(2)}) collective-permute-start(bf16[128,8,256]{2,1,0:T(8,128)(2,1)S(1)} %all-to-all-done.1.rs), channel_id=1, source_target_pairs={{0,1},{1,0},{2,3},{3,2},{4,5},{5,4},{6,7},{7,6},{8,9},{9,8},{10,11... | collective-permute-start | bytes 1572872 | tf_op jit(solution)/shard_map/ppermute | solution.py:426
  88.6 17.5 %collective-permute-start.4 = (f32[1024]{0:T(1024)S(1)}, f32[1024]{0:T(1024)S(1)}, u32[]{:S(2)}, u32[]{:S(2)}) collective-permute-start(f32[1024]{0:T(1024)S(1)} %copy-done.4), channel_id=1, source_target_pairs={{0,2},{2,0},{4,6},{6,4},{8,10},{10,8},{12,14},{14,12},{16,18},{18,... | collective-permute-start | bytes 12296 | tf_op jit(solution)/shard_map/ppermute | solution.py:423
  88.9 17.3 %collective-permute-start.1 = (bf16[256,1024]{1,0:T(8,128)(2,1)}, bf16[256,1024]{1,0:T(8,128)(2,1)S(1)}, u32[]{:S(2)}, u32[]{:S(2)}) collective-permute-start(bf16[256,1024]{1,0:T(8,128)(2,1)} %collective-permute-done.wiy_h), channel_id=1, source_target_pairs={{0,1},{1,0},{2,3},{3,2},{4,5},{5,4},{6,7},{7,6},{8,9},{9,8},{10,11... | collective-permute-start | bytes 1572872 | tf_op jit(solution)/shard_map/ppermute | solution.py:426
  97.2 9.0 %collective-permute-start.3 = (bf16[1024,256]{1,0:T(8,128)(2,1)}, bf16[1024,256]{1,0:T(8,128)(2,1)S(1)}, u32[]{:S(2)}, u32[]{:S(2)}) collective-permute-start(bf16[1024,256]{1,0:T(8,128)(2,1)} %collective-permute-done.2.woy_h), channel_id=1, source_target_pairs={{0,1},{1,0},{2,3},{3,2},{4,5},{5,4},{6,7},{7,6},{8,9},{9,8},{10,11... | collective-permute-start | bytes 1572872 | tf_op jit(solution)/shard_map/ppermute | solution.py:426
  106.1 12.8 %collective-permute-start.7 = (bf16[256,1536]{1,0:T(8,128)(2,1)S(1)}, bf16[256,1536]{1,0:T(8,128)(2,1)S(1)}, u32[]{:S(2)}, u32[]{:S(2)}) collective-permute-start(bf16[256,1536]{1,0:T(8,128)(2,1)S(1)} %get-tuple-element.46), channel_id=1, source_target_pairs={{0,1},{1,0},{2,3},{3,2},{4,5},{5,4},{6,7},{7,6},{8,9},{9,8},{10,11... | collective-permute-start | bytes 2359304 | tf_op jit(solution)/shard_map/ppermute | solution.py:426
  118.8 1.2 copy-start.5
  121.9 64.2 %all-to-all-start.2 = ((bf16[128,8,896]{2,1,0:T(8,128)(2,1)}), bf16[128,8,896]{2,1,0:T(8,128)(2,1)S(1)}, u32[]{:S(2)}, u32[]{:S(2)}) async-start(bf16[128,8,896]{2,1,0:T(8,128)(2,1)} %shard_map.135), calls=%async_computation.2 | async-start | bytes 3670016 | tf_op jit(solution)/shard_map/all_to_all | solution.py:429
  134.0 8.2 %collective-permute-start.9 = (bf16[272,1024]{1,0:T(8,128)(2,1)}, bf16[272,1024]{1,0:T(8,128)(2,1)S(1)}, u32[]{:S(2)}, u32[]{:S(2)}) collective-permute-start(bf16[272,1024]{1,0:T(8,128)(2,1)} %get-tuple-element.62), channel_id=1, source_target_pairs={{0,1},{1,0},{2,3},{3,2},{4,5},{5,4},{6,7},{7,6},{8,9},{9,8},{10,11... | collective-permute-start | bytes 1671176 | tf_op jit(solution)/shard_map/ppermute | solution.py:426
  134.9 9.6 %collective-permute-start.12 = (bf16[1024,256]{1,0:T(8,128)(2,1)}, bf16[1024,256]{1,0:T(8,128)(2,1)S(1)}, u32[]{:S(2)}, u32[]{:S(2)}) collective-permute-start(bf16[1024,256]{1,0:T(8,128)(2,1)} %get-tuple-element.66), channel_id=1, source_target_pairs={{0,1},{1,0},{2,3},{3,2},{4,5},{5,4},{6,7},{7,6},{8,9},{9,8},{10,11... | collective-permute-start | bytes 1572872 | tf_op jit(solution)/shard_map/ppermute | solution.py:426
  141.6 5.0 %collective-permute-start.8 = (bf16[272,1024]{1,0:T(8,128)(2,1)S(1)}, bf16[272,1024]{1,0:T(8,128)(2,1)S(1)}, u32[]{:S(2)}, u32[]{:S(2)}) collective-permute-start(bf16[272,1024]{1,0:T(8,128)(2,1)S(1)} %get-tuple-element.60), channel_id=1, source_target_pairs={{0,1},{1,0},{2,3},{3,2},{4,5},{5,4},{6,7},{7,6},{8,9},{9,8},{10,11... | collective-permute-start | bytes 1671176 | tf_op jit(solution)/shard_map/ppermute | solution.py:426
  142.1 4.4 %collective-permute-start.11 = (bf16[1024,256]{1,0:T(8,128)(2,1)S(1)}, bf16[1024,256]{1,0:T(8,128)(2,1)S(1)}, u32[]{:S(2)}, u32[]{:S(2)}) collective-permute-start(bf16[1024,256]{1,0:T(8,128)(2,1)S(1)} %get-tuple-element.64), channel_id=1, source_target_pairs={{0,1},{1,0},{2,3},{3,2},{4,5},{5,4},{6,7},{7,6},{8,9},{9,8},{10,11... | collective-permute-start | bytes 1572872 | tf_op jit(solution)/shard_map/ppermute | solution.py:426
  143.5 38.8 %collective-permute-start.10 = (bf16[272,1024]{1,0:T(8,128)(2,1)S(1)}, bf16[272,1024]{1,0:T(8,128)(2,1)S(1)}, u32[]{:S(2)}, u32[]{:S(2)}) collective-permute-start(bf16[272,1024]{1,0:T(8,128)(2,1)S(1)} %shard_map.139), channel_id=1, source_target_pairs={{0,2},{2,0},{4,6},{6,4},{8,10},{10,8},{12,14},{14,12},{16,18},{18,... | collective-permute-start | bytes 1671176 | tf_op jit(solution)/shard_map/ppermute | solution.py:423
  145.8 36.5 %collective-permute-start.13 = (bf16[1024,256]{1,0:T(8,128)(2,1)S(1)}, bf16[1024,256]{1,0:T(8,128)(2,1)S(1)}, u32[]{:S(2)}, u32[]{:S(2)}) collective-permute-start(bf16[1024,256]{1,0:T(8,128)(2,1)S(1)} %shard_map.140), channel_id=1, source_target_pairs={{0,2},{2,0},{4,6},{6,4},{8,10},{10,8},{12,14},{14,12},{16,18},{18,... | collective-permute-start | bytes 1572872 | tf_op jit(solution)/shard_map/ppermute | solution.py:423
  182.3 2.2 %copy-start = (bf16[512,1536]{1,0:T(8,128)(2,1)S(1)}, bf16[512,1536]{1,0:T(8,128)(2,1)}, u32[]{:S(2)}) copy-start(bf16[512,1536]{1,0:T(8,128)(2,1)} %wq.1) | copy-start | bytes 4718596
  182.3 2.2 %copy-start.1 = (bf16[512,512]{1,0:T(8,128)(2,1)S(1)}, bf16[512,512]{1,0:T(8,128)(2,1)}, u32[]{:S(2)}) copy-start(bf16[512,512]{1,0:T(8,128)(2,1)} %wo.1) | copy-start | bytes 1572868
  (8 other events, 8.4 us)

commit v6 on v5

--- a/solution.py
+++ b/solution.py
@@ -105,19 +105,16 @@
         cnt[r] = k + 1
         slots[b] = 2 * r + k
 
-    send[:, :, 0:W] = jnp.zeros((CHIPS, 8, W), BF)
-    low = low_rows((8, W))
+    send[:, :, 0 : 2 * W] = jnp.zeros((CHIPS, 4, 2 * W), BF)
 
     @pl.loop(0, 4)
     def _(step):
-      for i in [4 * step + u for u in range(4)]:
-        x = x_ref[pl.ds(pl.multiple_of(i * 16, 16), 16), :].astype(F32)
-        c = c_ref[pl.ds(pl.multiple_of(i * 16, 16), 16), :].astype(F32)
-        for h in range(2):
-            xa, ca = x[8 * h : 8 * h + 8], c[8 * h : 8 * h + 8]
-            xr, cr = pltpu.roll(xa, 4, 0), pltpu.roll(ca, 4, 0)
-            send[slots[4 * i + 2 * h], :, 0:W] = jnp.where(low, xa, cr).astype(BF)
-            send[slots[4 * i + 2 * h + 1], :, 0:W] = jnp.where(low, xr, ca).astype(BF)
+        for i in [4 * step + u for u in range(4)]:
+            x = x_ref[pl.ds(pl.multiple_of(i * 16, 16), 16), :].astype(F32)
+            c = c_ref[pl.ds(pl.multiple_of(i * 16, 16), 16), :].astype(F32)
+            for h in range(4):
+                send[slots[4 * i + h], :, 0:W] = x[4 * h : 4 * h + 4].astype(BF)
+                send[slots[4 * i + h], :, W : 2 * W] = c[4 * h : 4 * h + 4].astype(BF)
 
     for load in loads:
         load.wait()
@@ -135,16 +132,13 @@
         ss[64 * j : 64 * j + 64, :] = jnp.where(left, a[:64], a[64:])
         a = t_mm(qkv[:, s], g[:, s])
         ss[256 + 64 * j : 320 + 64 * j, :] = jnp.where(left, a[:64], a[64:])
-    low2 = low_rows((8, 128))
 
     @pl.loop(0, 16)
     def _(step):
-      for i in [4 * step + u for u in range(4)]:
-        v = ss[pl.ds(pl.multiple_of(i * 8, 8), 8), :]
-        hi = v.astype(BF).astype(F32)
-        lo = v - hi
-        send[2 * i, :, W:] = jnp.where(low2, hi, pltpu.roll(lo, 4, 0)).astype(BF)
-        send[2 * i + 1, :, W:] = jnp.where(low2, pltpu.roll(hi, 4, 0), lo).astype(BF)
+        for i in [4 * step + u for u in range(4)]:
+            v = ss[pl.ds(pl.multiple_of(i * 8, 8), 8), :]
+            send[2 * i, :, 2 * W :] = v[0:4].astype(BF)
+            send[2 * i + 1, :, 2 * W :] = v[4:8].astype(BF)
 
 
 def query_kernel(pos, x_ref, g_ref, keep, send):
@@ -169,8 +163,8 @@
 
 
 def spread_kernel(recv, query, out):
-    v = jnp.sum(recv[...].astype(F32), axis=0)
-    v = (v + pltpu.roll(v, 4, 0)) * (1.0 / TOTAL)
+    v = jnp.sum(recv[...].astype(F32), axis=0) * (1.0 / TOTAL)
+    v = jnp.concatenate([v, v], axis=0)
     hi = v.astype(BF).astype(F32)
     v = jnp.where(low_rows((8, 128)), hi, v - hi).astype(BF)
     out[:, :, 0:128] = jnp.broadcast_to(v[None], (CHIPS, 8, 128))
@@ -222,16 +216,12 @@
 
     @pl.loop(0, 8)
     def _(step):
-      for i in [4 * step + u for u in range(4)]:
-        xs, cs = [], []
-        for h in range(2):
-            a = recv[4 * i + 2 * h].astype(F32)
-            b = recv[4 * i + 2 * h + 1].astype(F32)
-            xs.append(jnp.where(low, a, pltpu.roll(b, 4, 0)))
-            cs.append(jnp.where(low, pltpu.roll(a, 4, 0), b))
-        rows = pl.ds(pl.multiple_of(i * 16, 16), 16)
-        x_s[rows, :] = jnp.concatenate(xs, axis=0).astype(BF)
-        c_s[rows, :] = jnp.concatenate(cs, axis=0).astype(BF)
+        for i in [4 * step + u for u in range(4)]:
+            rows = pl.ds(pl.multiple_of(i * 16, 16), 16)
+            xs = [recv[4 * i + h, :, 0:W].astype(F32) for h in range(4)]
+            cs = [recv[4 * i + h, :, W : 2 * W].astype(F32) for h in range(4)]
+            x_s[rows, :] = jnp.concatenate(xs, axis=0).astype(BF)
+            c_s[rows, :] = jnp.concatenate(cs, axis=0).astype(BF)
 
     stores[0].start()
     stores[1].start()
@@ -451,7 +441,7 @@
 
     send, slots, qkv, g = run(
         front_kernel, 5,
-        [far((CHIPS, 8, 640), BF), sds((NB,), jnp.int32), far((PTS, 3 * W), BF), far((PTS, W), BF)],
+        [far((CHIPS, 4, 1152), BF), sds((NB,), jnp.int32), far((PTS, 3 * W), BF), far((PTS, W), BF)],
         (in_hbm(ids), in_hbm(x), in_hbm(c), in_hbm(wq), in_hbm(wo_att)),
         [
             pltpu.SMEM((NB,), jnp.int32), pltpu.VMEM((W, 128), F32), pltpu.VMEM((W, 3 * W), BF),
@@ -467,7 +457,7 @@
     )
     (spread,) = run(
         spread_kernel, 1, [far((CHIPS, 8, 256), BF)], (recv, dealt_q),
-        specs={0: pl.BlockSpec((CHIPS, 8, 128), lambda i: (0, 0, 4))},
+        specs={0: pl.BlockSpec((CHIPS, 4, 128), lambda i: (0, 0, 8))},
     )
     rs = deal(spread)
     grads = [((272, HALF), F32), ((272, HALF), BF), ((HALF, 256), F32), ((HALF, 256), BF)]
@@ -484,7 +474,7 @@
         ]
         + [pltpu.SemaphoreType.DMA((6,)), pltpu.SemaphoreType.DMA((9,))],
         (0,),
-        specs={1: pl.BlockSpec((CHIPS, 8, W), lambda i: (0, 0, 0)), **{k: anywhere for k in range(2, 8)}},
+        specs={1: pl.BlockSpec((CHIPS, 4, 2 * W), lambda i: (0, 0, 0)), **{k: anywhere for k in range(2, 8)}},
         out_hbm=True, mib=48,
     )
     got_i, got_o = beside(send_i), beside(send_o)

time: 189 us -> 186 us (0.984)
  waiting for transfers between devices: 89.4 us -> 86.7 us
    all_to_all x3, waiting for transfers between devices: 44.4 us -> 41.7 us  [deal(): return lax.all_to_all(v, 'wide', split_axis=0, concat_axis=0, tiled=True)]
where the time goes in v6:
time: 186 us; the launch traced here: 185 us
  waiting for transfers between devices  86.7 us (47%)
  starting transfers between devices  48.8 us (26%)
  Pallas kernels  40 us (22%)
  local copies, waits for them, and re-layouts  8.82 us (5%)
    ppermute x5, waiting for transfers between devices, across(): return lax.ppermute(v, 'wide', pair)  43.8 us
    all_to_all x3, waiting for transfers between devices, deal(): return lax.all_to_all(v, 'wide', split_axis=0, concat_axis=0, tiled=True)  41.7 us
    pallas_call x15, Pallas kernels, run(): call(body, outs, scratch, smem_in=smem_in, n_in=len(args), smem_out=smem_...  40 us
    all_to_all x3, starting transfers between devices, deal(): return lax.all_to_all(v, 'wide', split_axis=0, concat_axis=0, tiled=True)  36.6 us
    unnamed x30, local copies, waits for them, and re-layouts  8.82 us
    ppermute x9, starting transfers between devices, beside(): return lax.ppermute(v, 'narrow', swap)  8.67 us
  transfers between devices with their start and end apart: 17, of which 5 were waited for; matrix products, arithmetic and copies ran while one was open for 0% of the time, Pallas kernels for 15%

profile of v6, /device:TPU:1, one launch (start us, length us, event | category | flops | bytes accessed | tf_op | source)
XLA Modules:
  0.0 185.3 jit_solution(11751259015419680430)
XLA Ops:
  0.6 6.4 %shard_map.127 = (bf16[128,4,1152]{2,1,0:T(4,128)(2,1)}, s32[64]{0:T(128)S(1)}, bf16[256,1536]{1,0:T(8,128)(2,1)}, bf16[256,512]{1,0:T(8,128)(2,1)}) custom-call(s32[64]{0:T(128)} %ids.1, bf16[256,512]{1,0:T(8,128)(2,1)} %x.1, bf16[256,512]{1,0:T(8,128)(2,1)} %c.1, bf16[512,1536]{1,0:T(8,128)(2,1)} %wq.1, bf16[512,512]{1,0:T(8,128)(2,1)} %wo.1), custom_call_target="tpu_custom_call" | custom-call | flops 5000000000 | bytes 5000000 | tf_op jit(solution)/shard_map/pallas_call | solution.py:422
  7.0 16.5 %all-to-all-start = ((bf16[128,4,1152]{2,1,0:T(4,128)(2,1)}), bf16[128,4,1152]{2,1,0:T(4,128)(2,1)S(1)}, u32[]{:S(2)}, u32[]{:S(2)}) async-start(bf16[128,4,1152]{2,1,0:T(4,128)(2,1)} %get-tuple-element.39), calls=%async_computation | async-start | bytes 2359296 | tf_op jit(solution)/shard_map/all_to_all | solution.py:419
  23.6 1.3 shard_map.131
  25.9 1.2 collective-permute-done.5.near
  27.2 27.7 %all-to-all-done.recv = bf16[128,4,1152]{2,1,0:T(4,128)(2,1)S(1)} async-done(((bf16[128,4,1152]{2,1,0:T(4,128)(2,1)}), bf16[128,4,1152]{2,1,0:T(4,128)(2,1)S(1)}, u32[]{:S(2)}, u32[]{:S(2)}) %all-to-all-start) | async-done | bytes 1179680 | tf_op jit(solution)/shard_map/all_to_all | solution.py:419
  56.0 8.0 %all-to-all-start.1 = ((bf16[128,8,256]{2,1,0:T(8,128)(2,1)}), bf16[128,8,256]{2,1,0:T(8,128)(2,1)S(1)}, u32[]{:S(2)}, u32[]{:S(2)}) async-start(bf16[128,8,256]{2,1,0:T(8,128)(2,1)} %shard_map.133), calls=%async_computation.1 | async-start | bytes 1048576 | tf_op jit(solution)/shard_map/all_to_all | solution.py:419
  67.8 14.0 %all-to-all-done.1.rs = bf16[128,8,256]{2,1,0:T(8,128)(2,1)S(1)} async-done(((bf16[128,8,256]{2,1,0:T(8,128)(2,1)}), bf16[128,8,256]{2,1,0:T(8,128)(2,1)S(1)}, u32[]{:S(2)}, u32[]{:S(2)}) %all-to-all-start.1) | async-done | bytes 524320 | tf_op jit(solution)/shard_map/all_to_all | solution.py:419
  81.8 3.8 %collective-permute-start.6 = (bf16[128,8,256]{2,1,0:T(8,128)(2,1)S(1)}, bf16[128,8,256]{2,1,0:T(8,128)(2,1)S(1)}, u32[]{:S(2)}, u32[]{:S(2)}) collective-permute-start(bf16[128,8,256]{2,1,0:T(8,128)(2,1)S(1)} %all-to-all-done.1.rs), channel_id=1, source_target_pairs={{0,1},{1,0},{2,3},{3,2},{4,5},{5,4},{6,7},{7,6},{8,9},{9,8},{10,11... | collective-permute-start | bytes 1572872 | tf_op jit(solution)/shard_map/ppermute | solution.py:416
  86.2 8.0 %collective-permute-done.2.woy_h = bf16[1024,256]{1,0:T(8,128)(2,1)} collective-permute-done((bf16[1024,256]{1,0:T(8,128)(2,1)S(1)}, bf16[1024,256]{1,0:T(8,128)(2,1)}, u32[]{:S(2)}, u32[]{:S(2)}) %collective-permute-start.2) | collective-permute-done | bytes 524320 | tf_op jit(solution)/shard_map/ppermute | solution.py:413
  94.2 1.8 collective-permute-start.3
  98.2 4.9 %shard_map.134 = (bf16[256,512]{1,0:T(8,128)(2,1)S(1)}, bf16[256,1536]{1,0:T(8,128)(2,1)S(1)}, f32[256,1536]{1,0:T(8,128)S(1)}, bf16[256,1536]{1,0:T(8,128)(2,1)S(1)}, f32[8,128]{1,0:T(8,128)S(1)}) custom-call(s32[4]{0:T(128)S(1)} %pad_add_fusion.pos, bf16[128,8,256]{2,1,0:T(8,128)(2,1)S(1)} %all-to-all-done.1.rs, ...), custom_call_target="tpu_custom_call" | custom-call | flops 7000000000 | bytes 7000000 | tf_op jit(solution)/shard_map/pallas_call | solution.py:422
  104.2 11.6 %shard_map.130 = (bf16[128,8,512]{2,1,0:T(8,128)(2,1)}, bf16[512,512]{1,0:T(8,128)(2,1)}, bf16[512,512]{1,0:T(8,128)(2,1)}, bf16[512,1024]{1,0:T(8,128)(2,1)}, b...) custom-call(s32[4]{0:T(128)S(1)} %pad_add_fusion.pos, ...), custom_call_target="tpu_custom_call" | custom-call | flops 12000000000 | bytes 12000000 | tf_op jit(solution)/shard_map/pallas_call | solution.py:422
  115.8 1.2 copy-done.5
  117.0 1.8 shard_map.135
  118.9 12.1 %all-to-all-start.2 = ((bf16[128,8,896]{2,1,0:T(8,128)(2,1)}), bf16[128,8,896]{2,1,0:T(8,128)(2,1)S(1)}, u32[]{:S(2)}, u32[]{:S(2)}) async-start(bf16[128,8,896]{2,1,0:T(8,128)(2,1)} %shard_map.135), calls=%async_computation.2 | async-start | bytes 3670016 | tf_op jit(solution)/shard_map/all_to_all | solution.py:419
  132.0 1.2 copy-done.8
  133.2 1.2 copy-done.9
  136.5 2.0 %shard_map.138 = (f32[272,1024]{1,0:T(8,128)S(1)}, bf16[272,1024]{1,0:T(8,128)(2,1)S(1)}, f32[1024,256]{1,0:T(8,128)S(1)}, bf16[1024,256]{1,0:T(8,128)(2,1)S(1)}) custom-call(s32[4]{0:T(128)S(1)} %pad_add_fusion.pos, bf16[512,512]{1,0:T(8,128)(2,1)S(1)} %copy-done.11, bf16[512,512]{1,0:T(8,128)(2,1)S(1)} %copy-done.12, bf16[512,1024]{1,0:T(8,128)(2,1)S(1)} %copy-done.8, ...), custom_call_target="tpu_custom_call" | custom-call | flops 5000000000 | bytes 5000000 | tf_op jit(solution)/shard_map/pallas_call | solution.py:422
  139.2 1.4 shard_map.139
  141.5 1.3 shard_map.140
  143.5 35.8 %collective-permute-done.13.far_o = bf16[1024,256]{1,0:T(8,128)(2,1)S(1)} collective-permute-done((bf16[1024,256]{1,0:T(8,128)(2,1)S(1)}, bf16[1024,256]{1,0:T(8,128)(2,1)S(1)}, u32[]{:S(2)}, u32[]{:S(2)}) %collective-permute-start.13) | collective-permute-done | bytes 524320 | tf_op jit(solution)/shard_map/ppermute | solution.py:413
  179.3 2.2 %shard_map.141 = (f32[256,1024]{1,0:T(8,128)}, f32[1,512]{1,0:T(1,128)}, f32[1024,256]{1,0:T(8,128)}) custom-call(s32[4]{0:T(128)S(1)} %pad_add_fusion.pos, f32[272,1024]{1,0:T(8,128)S(1)} %get-tuple-element.59.keep_i, bf16[272,1024]{1,0:T(8,128)(2,1)S(1)} %collective-permute-done.8.got_i, bf16[272,1024]{1,0:T(8,128)(2,1)S(1)} %collective-permute-done.10.far_i, ...), custom_call_target="tpu_custom_call" | custom-call | flops 3000000000 | bytes 3000000 | tf_op jit(solution)/shard_map/pallas_call | solution.py:422
  181.5 1.5 shard_map.136
  183.0 2.3 %shard_map.137 = (bf16[256,512]{1,0:T(8,128)(2,1)}, bf16[256,512]{1,0:T(8,128)(2,1)}, f32[2,2048]{1,0:T(2,128)}) custom-call(s32[64]{0:T(128)S(1)} %get-tuple-element.38.slots, bf16[128,8,896]{2,1,0:T(8,128)(2,1)S(1)} %all-to-all-done.2.ret, f32[256,512]{1,0:T(8,128)} %get-tuple-element.49.base_o, f32[256,512]{1,0:T(8,128)} %get-tuple-element.50.base_k, ...), custom_call_target="tpu_custom_call" | custom-call | flops 3000000000 | bytes 3000000 | tf_op jit(solution)/shard_map/pallas_call | solution.py:422
  (56 shorter events, 15.1 us)
Async XLA Ops:
  7.0 16.6 %copy-start.2 = (bf16[256,512]{1,0:T(8,128)(2,1)S(1)}, bf16[256,512]{1,0:T(8,128)(2,1)}, u32[]{:S(2)}) copy-start(bf16[256,512]{1,0:T(8,128)(2,1)} %x.1) | copy-start | bytes 786436
  7.0 16.6 %copy-start.6 = (bf16[256,512]{1,0:T(8,128)(2,1)S(1)}, bf16[256,512]{1,0:T(8,128)(2,1)}, u32[]{:S(2)}) copy-start(bf16[256,512]{1,0:T(8,128)(2,1)} %get-tuple-element.41.g_ref) | copy-start | bytes 786436
  7.0 47.9 %all-to-all-start = ((bf16[128,4,1152]{2,1,0:T(4,128)(2,1)}), bf16[128,4,1152]{2,1,0:T(4,128)(2,1)S(1)}, u32[]{:S(2)}, u32[]{:S(2)}) async-start(bf16[128,4,1152]{2,1,0:T(4,128)(2,1)} %get-tuple-element.39), calls=%async_computation | async-start | bytes 2359296 | tf_op jit(solution)/shard_map/all_to_all | solution.py:419
  24.9 2.2 %collective-permute-start.5 = (bf16[256,512]{1,0:T(8,128)(2,1)S(1)}, bf16[256,512]{1,0:T(8,128)(2,1)S(1)}, u32[]{:S(2)}, u32[]{:S(2)}) collective-permute-start(bf16[256,512]{1,0:T(8,128)(2,1)S(1)} %get-tuple-element.43), channel_id=1, source_target_pairs={{0,1},{1,0},{2,3},{3,2},{4,5},{5,4},{6,7},{7,6},{8,9},{9,8},{10,11... | collective-permute-start | bytes 786440 | tf_op jit(solution)/shard_map/ppermute | solution.py:416
  56.0 25.8 %all-to-all-start.1 = ((bf16[128,8,256]{2,1,0:T(8,128)(2,1)}), bf16[128,8,256]{2,1,0:T(8,128)(2,1)S(1)}, u32[]{:S(2)}, u32[]{:S(2)}) async-start(bf16[128,8,256]{2,1,0:T(8,128)(2,1)} %shard_map.133), calls=%async_computation.1 | async-start | bytes 1048576 | tf_op jit(solution)/shard_map/all_to_all | solution.py:419
  65.1 20.6 %copy-start.4 = (f32[1024]{0:T(1024)S(1)}, f32[1024]{0:T(1024)}, u32[]{:S(2)}) copy-start(f32[1024]{0:T(1024)} %param.13) | copy-start | bytes 12292
  65.1 31.0 %copy-start.3 = (bf16[256,512]{1,0:T(8,128)(2,1)S(1)}, bf16[256,512]{1,0:T(8,128)(2,1)}, u32[]{:S(2)}) copy-start(bf16[256,512]{1,0:T(8,128)(2,1)} %c.1) | copy-start | bytes 786436
  65.1 20.8 %collective-permute-start = (bf16[256,1024]{1,0:T(8,128)(2,1)S(1)}, bf16[256,1024]{1,0:T(8,128)(2,1)}, u32[]{:S(2)}, u32[]{:S(2)}) collective-permute-start(bf16[256,1024]{1,0:T(8,128)(2,1)S(1)} %shard_map.128), channel_id=1, source_target_pairs={{0,2},{2,0},{4,6},{6,4},{8,10},{10,8},{12,14},{14,12},{16,18},{18,... | collective-permute-start | bytes 1572872 | tf_op jit(solution)/shard_map/ppermute | solution.py:413
  66.8 27.4 %collective-permute-start.2 = (bf16[1024,256]{1,0:T(8,128)(2,1)S(1)}, bf16[1024,256]{1,0:T(8,128)(2,1)}, u32[]{:S(2)}, u32[]{:S(2)}) collective-permute-start(bf16[1024,256]{1,0:T(8,128)(2,1)S(1)} %shard_map.129), channel_id=1, source_target_pairs={{0,2},{2,0},{4,6},{6,4},{8,10},{10,8},{12,14},{14,12},{16,18},{18,... | collective-permute-start | bytes 1572872 | tf_op jit(solution)/shard_map/ppermute | solution.py:413
  81.8 14.3 %collective-permute-start.6 = (bf16[128,8,256]{2,1,0:T(8,128)(2,1)S(1)}, bf16[128,8,256]{2,1,0:T(8,128)(2,1)S(1)}, u32[]{:S(2)}, u32[]{:S(2)}) collective-permute-start(bf16[128,8,256]{2,1,0:T(8,128)(2,1)S(1)} %all-to-all-done.1.rs), channel_id=1, source_target_pairs={{0,1},{1,0},{2,3},{3,2},{4,5},{5,4},{6,7},{7,6},{8,9},{9,8},{10,11... | collective-permute-start | bytes 1572872 | tf_op jit(solution)/shard_map/ppermute | solution.py:416
  85.6 17.5 %collective-permute-start.4 = (f32[1024]{0:T(1024)S(1)}, f32[1024]{0:T(1024)S(1)}, u32[]{:S(2)}, u32[]{:S(2)}) collective-permute-start(f32[1024]{0:T(1024)S(1)} %copy-done.4), channel_id=1, source_target_pairs={{0,2},{2,0},{4,6},{6,4},{8,10},{10,8},{12,14},{14,12},{16,18},{18,... | collective-permute-start | bytes 12296 | tf_op jit(solution)/shard_map/ppermute | solution.py:413
  85.9 17.3 %collective-permute-start.1 = (bf16[256,1024]{1,0:T(8,128)(2,1)}, bf16[256,1024]{1,0:T(8,128)(2,1)S(1)}, u32[]{:S(2)}, u32[]{:S(2)}) collective-permute-start(bf16[256,1024]{1,0:T(8,128)(2,1)} %collective-permute-done.wiy_h), channel_id=1, source_target_pairs={{0,1},{1,0},{2,3},{3,2},{4,5},{5,4},{6,7},{7,6},{8,9},{9,8},{10,11... | collective-permute-start | bytes 1572872 | tf_op jit(solution)/shard_map/ppermute | solution.py:416
  94.2 9.0 %collective-permute-start.3 = (bf16[1024,256]{1,0:T(8,128)(2,1)}, bf16[1024,256]{1,0:T(8,128)(2,1)S(1)}, u32[]{:S(2)}, u32[]{:S(2)}) collective-permute-start(bf16[1024,256]{1,0:T(8,128)(2,1)} %collective-permute-done.2.woy_h), channel_id=1, source_target_pairs={{0,1},{1,0},{2,3},{3,2},{4,5},{5,4},{6,7},{7,6},{8,9},{9,8},{10,11... | collective-permute-start | bytes 1572872 | tf_op jit(solution)/shard_map/ppermute | solution.py:416
  103.1 12.7 %collective-permute-start.7 = (bf16[256,1536]{1,0:T(8,128)(2,1)S(1)}, bf16[256,1536]{1,0:T(8,128)(2,1)S(1)}, u32[]{:S(2)}, u32[]{:S(2)}) collective-permute-start(bf16[256,1536]{1,0:T(8,128)(2,1)S(1)} %get-tuple-element.46), channel_id=1, source_target_pairs={{0,1},{1,0},{2,3},{3,2},{4,5},{5,4},{6,7},{7,6},{8,9},{9,8},{10,11... | collective-permute-start | bytes 2359304 | tf_op jit(solution)/shard_map/ppermute | solution.py:416
  115.8 1.2 copy-start.5
  118.9 64.2 %all-to-all-start.2 = ((bf16[128,8,896]{2,1,0:T(8,128)(2,1)}), bf16[128,8,896]{2,1,0:T(8,128)(2,1)S(1)}, u32[]{:S(2)}, u32[]{:S(2)}) async-start(bf16[128,8,896]{2,1,0:T(8,128)(2,1)} %shard_map.135), calls=%async_computation.2 | async-start | bytes 3670016 | tf_op jit(solution)/shard_map/all_to_all | solution.py:419
  131.0 8.2 %collective-permute-start.9 = (bf16[272,1024]{1,0:T(8,128)(2,1)}, bf16[272,1024]{1,0:T(8,128)(2,1)S(1)}, u32[]{:S(2)}, u32[]{:S(2)}) collective-permute-start(bf16[272,1024]{1,0:T(8,128)(2,1)} %get-tuple-element.62), channel_id=1, source_target_pairs={{0,1},{1,0},{2,3},{3,2},{4,5},{5,4},{6,7},{7,6},{8,9},{9,8},{10,11... | collective-permute-start | bytes 1671176 | tf_op jit(solution)/shard_map/ppermute | solution.py:416
  131.9 9.6 %collective-permute-start.12 = (bf16[1024,256]{1,0:T(8,128)(2,1)}, bf16[1024,256]{1,0:T(8,128)(2,1)S(1)}, u32[]{:S(2)}, u32[]{:S(2)}) collective-permute-start(bf16[1024,256]{1,0:T(8,128)(2,1)} %get-tuple-element.66), channel_id=1, source_target_pairs={{0,1},{1,0},{2,3},{3,2},{4,5},{5,4},{6,7},{7,6},{8,9},{9,8},{10,11... | collective-permute-start | bytes 1572872 | tf_op jit(solution)/shard_map/ppermute | solution.py:416
  138.6 5.0 %collective-permute-start.8 = (bf16[272,1024]{1,0:T(8,128)(2,1)S(1)}, bf16[272,1024]{1,0:T(8,128)(2,1)S(1)}, u32[]{:S(2)}, u32[]{:S(2)}) collective-permute-start(bf16[272,1024]{1,0:T(8,128)(2,1)S(1)} %get-tuple-element.60), channel_id=1, source_target_pairs={{0,1},{1,0},{2,3},{3,2},{4,5},{5,4},{6,7},{7,6},{8,9},{9,8},{10,11... | collective-permute-start | bytes 1671176 | tf_op jit(solution)/shard_map/ppermute | solution.py:416
  139.1 4.4 %collective-permute-start.11 = (bf16[1024,256]{1,0:T(8,128)(2,1)S(1)}, bf16[1024,256]{1,0:T(8,128)(2,1)S(1)}, u32[]{:S(2)}, u32[]{:S(2)}) collective-permute-start(bf16[1024,256]{1,0:T(8,128)(2,1)S(1)} %get-tuple-element.64), channel_id=1, source_target_pairs={{0,1},{1,0},{2,3},{3,2},{4,5},{5,4},{6,7},{7,6},{8,9},{9,8},{10,11... | collective-permute-start | bytes 1572872 | tf_op jit(solution)/shard_map/ppermute | solution.py:416
  140.5 38.8 %collective-permute-start.10 = (bf16[272,1024]{1,0:T(8,128)(2,1)S(1)}, bf16[272,1024]{1,0:T(8,128)(2,1)S(1)}, u32[]{:S(2)}, u32[]{:S(2)}) collective-permute-start(bf16[272,1024]{1,0:T(8,128)(2,1)S(1)} %shard_map.139), channel_id=1, source_target_pairs={{0,2},{2,0},{4,6},{6,4},{8,10},{10,8},{12,14},{14,12},{16,18},{18,... | collective-permute-start | bytes 1671176 | tf_op jit(solution)/shard_map/ppermute | solution.py:413
  142.8 36.5 %collective-permute-start.13 = (bf16[1024,256]{1,0:T(8,128)(2,1)S(1)}, bf16[1024,256]{1,0:T(8,128)(2,1)S(1)}, u32[]{:S(2)}, u32[]{:S(2)}) collective-permute-start(bf16[1024,256]{1,0:T(8,128)(2,1)S(1)} %shard_map.140), channel_id=1, source_target_pairs={{0,2},{2,0},{4,6},{6,4},{8,10},{10,8},{12,14},{14,12},{16,18},{18,... | collective-permute-start | bytes 1572872 | tf_op jit(solution)/shard_map/ppermute | solution.py:413
  179.3 2.2 %copy-start = (bf16[512,1536]{1,0:T(8,128)(2,1)S(1)}, bf16[512,1536]{1,0:T(8,128)(2,1)}, u32[]{:S(2)}) copy-start(bf16[512,1536]{1,0:T(8,128)(2,1)} %wq.1) | copy-start | bytes 4718596
  179.3 2.2 %copy-start.1 = (bf16[512,512]{1,0:T(8,128)(2,1)S(1)}, bf16[512,512]{1,0:T(8,128)(2,1)}, u32[]{:S(2)}) copy-start(bf16[512,512]{1,0:T(8,128)(2,1)} %wo.1) | copy-start | bytes 1572868
  (8 other events, 8.4 us)
